TPU v7x, 32 devices: a whole 2x2x4 slice. The times are simulated.
32 devices in a mesh: cluster: 4 (over y, core), sub: 8 (over z, x).
Axes of the slice: x: 2, y: 2, z: 4, core: 2. Of those that a mesh axis runs over, the one named last changes fastest.
Arguments:
- load: float32 [57344, 256], P(('cluster', 'sub'))
- schur: float32 [57344, 1792], P(('cluster', 'sub')), as said below
- modes: float32 [57344, 128], P(('cluster', 'sub')), may hold values from -0.125 to 0.125
- coarse_inverse: float32 [4096, 1024], P(('cluster', 'sub')), as said below
- interface_rows: int32 [32], P(('cluster', 'sub')), may hold values from 896 to 1792, as said below
- mode_count: int32 [32], P(('cluster', 'sub')), may hold values from 64 to 128, as said below
- left_rows: int32 [32, 384], P(('cluster', 'sub')), may hold values from 0 to 1792, as said below
- right_rows: int32 [32, 384], P(('cluster', 'sub')), may hold values from 0 to 1792, as said below
Outputs:
- solution: float32 [57344, 256], P(('cluster', 'sub'))
- residual: float32 [57344, 256], P(('cluster', 'sub'))
Inputs may be any that keep to these rules, and one draw needn't show every extreme that they name: `interface_rows`: every subdomain has at least half of 1792 live rows, and some subdomain has exactly 1792. `mode_count`: every subdomain has at least half of 128 live modes, and some subdomain has exactly 128. Slot j of right_rows[g] and slot j of left_rows[g + 1] name the same interface unknown; the used slots of a row come first, all other slots hold 1792. Two neighbours share at least half of 384 rows and some pair shares exactly 384. The used entries of left_rows[g] and right_rows[g] are distinct live rows of g. left_rows[0] and right_rows[31] are unused. `right_rows`: see left_rows. `schur`: each block S_g is symmetric positive definite with a positive diagonal. `coarse_inverse`: each cluster's coarse inverse is symmetric positive definite.
All inputs are finite; a program needn't handle non-finite values.
Results may differ from a plain program's by a relative error of at most 0.0001.
Values sent between devices are 32-bit elements; how exact they have to be, the bound alone decides.
No kernel may reach another device: no remote copies, remote signals or barrier semaphores. Data moves between devices by JAX's collectives and lax.ppermute only.
A program may use at most 128 MiB of HBM per device.

v0:
```python
import jax
import jax.numpy as jnp
from jax import lax
from jax.sharding import PartitionSpec as P

ITERS = 3


def passed_along(value, axis, by):
    devices = lax.axis_size(axis)
    pairs = [(i, i + by) for i in range(devices) if 0 <= i + by < devices]
    return lax.ppermute(value, axis, pairs)


def take_rows(field, indices):
    return jnp.take(field, indices, axis=0, mode="fill", fill_value=0.0)


def assemble(field, left_index, right_index):
    to_left = take_rows(field, left_index)
    to_right = take_rows(field, right_index)
    from_left = passed_along(to_right, ("cluster", "sub"), 1)
    from_right = passed_along(to_left, ("cluster", "sub"), -1)
    merged = field.at[left_index].add(from_left, mode="drop")
    return merged.at[right_index].add(from_right, mode="drop")


def local(load, schur, modes, coarse_inverse, interface_rows, mode_count, left_rows, right_rows):
    highest = lax.Precision.HIGHEST
    order = schur.shape[0]
    mode_total = modes.shape[1]
    left_index = left_rows[0]
    right_index = right_rows[0]
    positions = jnp.arange(order, dtype=jnp.int32)
    live = (positions < interface_rows[0]).astype(jnp.float32)
    ones_shared = jnp.ones((left_index.shape[0],), jnp.float32)
    counted = jnp.zeros((order,), jnp.float32).at[left_index].add(ones_shared, mode="drop")
    counted = counted.at[right_index].add(ones_shared, mode="drop")
    share = (live / (1.0 + counted))[:, None]
    live_column = live[:, None]
    mode_live = (jnp.arange(mode_total, dtype=jnp.int32) < mode_count[0]).astype(jnp.float32)[
        :, None
    ]
    schur_diag = jnp.diagonal(schur)[:, None]
    rhs = assemble(live_column * load, left_index, right_index)
    solution = jnp.zeros_like(rhs)
    residual = rhs
    for iteration in range(ITERS):
        modal = jnp.einsum(
            "im,ik->mk",
            modes,
            share * residual,
            precision=highest,
            preferred_element_type=jnp.float32,
        )
        modal = modal * mode_live
        correction = jnp.dot(
            coarse_inverse,
            lax.all_gather(modal, "sub", axis=0, tiled=True),
            precision=highest,
            preferred_element_type=jnp.float32,
        )
        correction = correction * mode_live
        prolonged = jnp.dot(
            modes, correction, precision=highest, preferred_element_type=jnp.float32
        )
        direction = assemble(share * (prolonged + residual / schur_diag), left_index, right_index)
        product = jnp.dot(schur, direction, precision=highest, preferred_element_type=jnp.float32)
        image = assemble(live_column * product, left_index, right_index)
        numerator, denominator = lax.psum(
            (jnp.sum(share * residual * image, axis=0), jnp.sum(share * image * image, axis=0)),
            ("cluster", "sub"),
        )
        alpha = (numerator / (denominator + 1e-06))[None, :]
        solution = solution + alpha * direction
        residual = residual - alpha * image
    return (solution, residual)


def solution(mesh):
    return jax.shard_map(
        local,
        mesh=mesh,
        in_specs=(
            P(("cluster", "sub"), None),
            P(("cluster", "sub"), None),
            P(("cluster", "sub"), None),
            P(("cluster", "sub"), None),
            P(("cluster", "sub")),
            P(("cluster", "sub")),
            P(("cluster", "sub"), None),
            P(("cluster", "sub"), None),
        ),
        out_specs=(P(("cluster", "sub"), None), P(("cluster", "sub"), None)),
        check_vma=False,
    )
```

profile of v0, /device:TPU:0, one launch (start us, length us, event | category | flops | bytes accessed | tf_op | source)
XLA Modules:
  0.0 678.6 jit_solution(7623673633662888873)
XLA Ops:
  13.1 4.9 collective-permute-start
  35.1 5.1 scatter_fusion.1
  40.2 5.1 scatter_fusion.2
  49.8 28.0 %gather_fusion = f32[1792]{0:T(1024)S(1)} fusion(f32[1792,1792]{1,0:T(8,128)} %param.11, s32[1792]{0:T(1024)S(1)} %or_reduce_fusion), kind=kCustom, calls=%fused_computation.14 | custom fusion | bytes 28672 | tf_op jit(solution)/shard_map/jit(diagonal)/cond/branch_0_fun/gather | solution.py:44
  77.7 13.4 %all-gather.4.cloned.1.call-done = f32[1024,256]{0,1:T(8,128)} async-done(((f32[128,256]{0,1:T(8,128)}), f32[1024,256]{0,1:T(8,128)}) %all-gather.4.cloned.1.call-update) | async-done | bytes 1048592 | tf_op jit(solution)/shard_map/all_gather | solution.py:59
  112.0 12.7 %collective-permute-done.2 = f32[384,256]{1,0:T(8,128)} collective-permute-done((f32[384,256]{1,0:T(8,128)S(1)}, f32[384,256]{1,0:T(8,128)}, u32[]{:S(2)}, u32[]{:S(2)}) %collective-permute-start.2) | collective-permute-done | bytes 393248 | tf_op jit(solution)/shard_map/ppermute | solution.py:12
  132.8 27.0 %fusion = f32[1792,256]{0,1:T(8,128)} fusion(f32[1792,256]{1,0:T(8,128)S(1)} %scatter_fusion.4, f32[1792,1792]{1,0:T(8,128)} %param.11, f32[1792]{0:T(1024)S(1)} %fusion.33), kind=kOutput, calls=%fused_computation.40 | convolution fusion | flops 9865461760 | bytes 16522240 | tf_op jit(solution)/shard_map/dot_general | solution.py:68
  171.2 5.2 collective-permute-start.4
  179.6 12.0 %collective-permute-done.4 = f32[384,256]{1,0:T(8,128)} collective-permute-done((f32[384,256]{1,0:T(8,128)S(1)}, f32[384,256]{1,0:T(8,128)}, u32[]{:S(2)}, u32[]{:S(2)}) %collective-permute-start.4) | collective-permute-done | bytes 393248 | tf_op jit(solution)/shard_map/ppermute | solution.py:12
  191.6 5.6 scatter_fusion.5
  197.2 5.6 scatter_fusion.6
  208.0 38.9 %all-reduce.2 = (f32[256]{0:T(256)S(1)}, f32[256]{0:T(256)S(1)}) all-reduce(f32[256]{0:T(256)S(1)} %get-tuple-element.12, f32[256]{0:T(256)S(1)} %get-tuple-element.11), channel_id=1, replica_groups=mesh['cluster'=4,'sub'=8] {'cluster','sub'}, use_global_device_ids=true, to_apply=%region_9.11 | all-reduce | flops 512 | bytes 4096 | tf_op jit(solution)/shard_map/psum | solution.py:70
  252.8 39.9 %all-gather.6.cloned.1.call-done = f32[1024,256]{0,1:T(8,128)} async-done(((f32[128,256]{0,1:T(8,128)}), f32[1024,256]{0,1:T(8,128)}) %all-gather.6.cloned.1.call-update) | async-done | bytes 1048592 | tf_op jit(solution)/shard_map/all_gather | solution.py:59
  317.4 12.9 %collective-permute-done.6 = f32[384,256]{1,0:T(8,128)} collective-permute-done((f32[384,256]{1,0:T(8,128)S(1)}, f32[384,256]{1,0:T(8,128)}, u32[]{:S(2)}, u32[]{:S(2)}) %collective-permute-start.6) | collective-permute-done | bytes 393248 | tf_op jit(solution)/shard_map/ppermute | solution.py:12
  330.2 5.6 scatter_fusion.7
  335.9 5.6 scatter_fusion.8
  341.5 27.9 %fusion.1 = f32[1792,256]{0,1:T(8,128)} fusion(f32[1792,256]{1,0:T(8,128)} %scatter_fusion.8, f32[1792,1792]{1,0:T(8,128)} %param.11, f32[1792]{0:T(1024)S(1)} %fusion.33), kind=kOutput, calls=%fused_computation.41 | convolution fusion | flops 9865461760 | bytes 16522240 | tf_op jit(solution)/shard_map/dot_general | solution.py:68
  380.8 5.2 collective-permute-start.8
  389.2 12.0 %collective-permute-done.8 = f32[384,256]{1,0:T(8,128)} collective-permute-done((f32[384,256]{1,0:T(8,128)S(1)}, f32[384,256]{1,0:T(8,128)}, u32[]{:S(2)}, u32[]{:S(2)}) %collective-permute-start.8) | collective-permute-done | bytes 393248 | tf_op jit(solution)/shard_map/ppermute | solution.py:12
  401.2 5.6 scatter_fusion.9
  406.8 5.6 scatter_fusion.10
  417.6 38.9 %all-reduce.1 = (f32[256]{0:T(256)S(1)}, f32[256]{0:T(256)S(1)}) all-reduce(f32[256]{0:T(256)S(1)} %get-tuple-element.10, f32[256]{0:T(256)S(1)} %get-tuple-element.9), channel_id=1, replica_groups=mesh['cluster'=4,'sub'=8] {'cluster','sub'}, use_global_device_ids=true, to_apply=%region_17.19 | all-reduce | flops 512 | bytes 4096 | tf_op jit(solution)/shard_map/psum | solution.py:70
  462.3 40.0 %all-gather.8.cloned.1.call-done = f32[1024,256]{0,1:T(8,128)} async-done(((f32[128,256]{0,1:T(8,128)}), f32[1024,256]{0,1:T(8,128)}) %all-gather.8.cloned.1.call-update) | async-done | bytes 1048592 | tf_op jit(solution)/shard_map/all_gather | solution.py:59
  524.6 14.0 %collective-permute-done.10 = f32[384,256]{1,0:T(8,128)S(1)} collective-permute-done((f32[384,256]{1,0:T(8,128)S(1)}, f32[384,256]{1,0:T(8,128)S(1)}, u32[]{:S(2)}, u32[]{:S(2)}) %collective-permute-start.10) | collective-permute-done | bytes 393248 | tf_op jit(solution)/shard_map/ppermute | solution.py:12
  538.6 5.3 scatter_fusion.11
  544.0 5.3 scatter_fusion.12
  549.3 27.9 %fusion.2 = f32[1792,256]{0,1:T(8,128)} fusion(f32[1792,256]{1,0:T(8,128)} %scatter_fusion.12, f32[1792,1792]{1,0:T(8,128)} %param.11, f32[1792]{0:T(1024)S(1)} %fusion.33), kind=kOutput, calls=%fused_computation.42 | convolution fusion | flops 9865461760 | bytes 16522240 | tf_op jit(solution)/shard_map/dot_general | solution.py:68
  600.9 7.1 %collective-permute-done.12 = f32[384,256]{1,0:T(8,128)S(1)} collective-permute-done((f32[384,256]{1,0:T(8,128)}, f32[384,256]{1,0:T(8,128)S(1)}, u32[]{:S(2)}, u32[]{:S(2)}) %collective-permute-start.12) | collective-permute-done | bytes 393248 | tf_op jit(solution)/shard_map/ppermute | solution.py:12
  608.0 5.1 scatter_fusion.13
  613.1 5.1 scatter_fusion.14
  623.1 38.7 %all-reduce = (f32[256]{0:T(256)S(1)}, f32[256]{0:T(256)S(1)}) all-reduce(f32[256]{0:T(256)S(1)} %get-tuple-element.8, f32[256]{0:T(256)S(1)} %get-tuple-element.7), channel_id=1, replica_groups=mesh['cluster'=4,'sub'=8] {'cluster','sub'}, use_global_device_ids=true, to_apply=%region_25.27 | all-reduce | flops 512 | bytes 4096 | tf_op jit(solution)/shard_map/psum | solution.py:70
  661.7 5.6 multiply_subtract_fusion
  (169 shorter events, 185.8 us)
Async XLA Ops:
  7.2 40.0 %copy-start = (f32[1792,128]{1,0:T(8,128)S(1)}, f32[1792,128]{1,0:T(8,128)}, u32[]{:S(2)}) copy-start(f32[1792,128]{1,0:T(8,128)} %param.12) | copy-start | bytes 2752516
  7.2 84.0 %all-gather.4.cloned.1.call-start = ((), (), s32[]{:S(2)}) async-start(), calls=%async_computation | async-start | bytes 1179648 | tf_op jit(solution)/shard_map/all_gather | solution.py:59
  8.0 4.2 copy-start.21
  10.5 7.6 %copy-start.2 = (f32[1792,256]{1,0:T(8,128)}, f32[1792,256]{1,0:T(8,128)S(1)}, u32[]{:S(2)}) copy-start(f32[1792,256]{1,0:T(8,128)S(1)} %broadcast_multiply_fusion) | copy-start | bytes 5505028
  10.5 7.5 %copy-start.31 = (s32[1,384]{1,0:T(1,128)S(1)}, s32[1,384]{1,0:T(1,128)}, u32[]{:S(2)}) copy-start(s32[1,384]{1,0:T(1,128)} %param.16) | copy-start | bytes 4612
  13.1 22.0 %collective-permute-start = (f32[384,256]{1,0:T(8,128)}, f32[384,256]{1,0:T(8,128)S(1)}, u32[]{:S(2)}, u32[]{:S(2)}) collective-permute-start(f32[384,256]{1,0:T(8,128)} %broadcast_select_fusion.13), channel_id=1, source_target_pairs={{0,1},{1,2},{2,3},{3,4},{4,5},{5,6},{6,7},{7,8},{8,9},{9,10},{10,1... | collective-permute-start | bytes 1179656 | tf_op jit(solution)/shard_map/ppermute | solution.py:12
  19.9 20.3 %collective-permute-start.1 = (f32[384,256]{1,0:T(8,128)S(1)}, f32[384,256]{1,0:T(8,128)S(1)}, u32[]{:S(2)}, u32[]{:S(2)}) collective-permute-start(f32[384,256]{1,0:T(8,128)S(1)} %broadcast_select_fusion.12), channel_id=1, source_target_pairs={{1,0},{2,1},{3,2},{4,3},{5,4},{6,5},{7,6},{8,7},{9,8},{10,9},{11,1... | collective-permute-start | bytes 1179656 | tf_op jit(solution)/shard_map/ppermute | solution.py:12
  21.9 13.2 %copy-start.12 = (s32[384]{0:T(512)}, s32[384]{0:T(512)S(1)}, u32[]{:S(2)}) copy-start(s32[384]{0:T(512)S(1)} %fusion.37) | copy-start | bytes 4612
  27.2 13.0 %copy-start.9 = (s32[384]{0:T(512)}, s32[384]{0:T(512)S(1)}, u32[]{:S(2)}) copy-start(s32[384]{0:T(512)S(1)} %fusion.38) | copy-start | bytes 4612
  49.5 243.2 %all-gather.6.cloned.1.call-start = ((), (), s32[]{:S(2)}) async-start(), calls=%async_computation.1 | async-start | bytes 1179648 | tf_op jit(solution)/shard_map/all_gather | solution.py:59
  49.7 41.4 %copy-start.8 = (f32[128,1024]{1,0:T(8,128)S(1)}, f32[128,1024]{1,0:T(8,128)}, u32[]{:S(2)}) copy-start(f32[128,1024]{1,0:T(8,128)} %param.13) | copy-start | bytes 1572868
  101.7 7.0 %copy-start.25 = (pred[384]{0:T(512)(128)(4,1)S(1)}, pred[384]{0:T(512)(128)(4,1)}, u32[]{:S(2)}) copy-start(pred[384]{0:T(512)(128)(4,1)} %copy-done.24) | copy-start | bytes 1156
  101.7 23.0 %copy-start.13 = (s32[384]{0:T(512)S(1)}, s32[384]{0:T(512)}, u32[]{:S(2)}) copy-start(s32[384]{0:T(512)} %copy-done.12) | copy-start | bytes 4612
  105.1 19.7 %collective-permute-start.2 = (f32[384,256]{1,0:T(8,128)S(1)}, f32[384,256]{1,0:T(8,128)}, u32[]{:S(2)}, u32[]{:S(2)}) collective-permute-start(f32[384,256]{1,0:T(8,128)S(1)} %broadcast_select_fusion.11), channel_id=1, source_target_pairs={{0,1},{1,2},{2,3},{3,4},{4,5},{5,6},{6,7},{7,8},{8,9},{9,10},{10,1... | collective-permute-start | bytes 1179656 | tf_op jit(solution)/shard_map/ppermute | solution.py:12
  110.6 17.9 %copy-start.10 = (s32[384]{0:T(512)S(1)}, s32[384]{0:T(512)}, u32[]{:S(2)}) copy-start(s32[384]{0:T(512)} %copy-done.9) | copy-start | bytes 4612
  110.6 17.9 %collective-permute-start.3 = (f32[384,256]{1,0:T(8,128)}, f32[384,256]{1,0:T(8,128)}, u32[]{:S(2)}, u32[]{:S(2)}) collective-permute-start(f32[384,256]{1,0:T(8,128)} %broadcast_select_fusion.10), channel_id=1, source_target_pairs={{1,0},{2,1},{3,2},{4,3},{5,4},{6,5},{7,6},{8,7},{9,8},{10,9},{11,1... | collective-permute-start | bytes 1179656 | tf_op jit(solution)/shard_map/ppermute | solution.py:12
  171.2 20.4 %collective-permute-start.4 = (f32[384,256]{1,0:T(8,128)S(1)}, f32[384,256]{1,0:T(8,128)}, u32[]{:S(2)}, u32[]{:S(2)}) collective-permute-start(f32[384,256]{1,0:T(8,128)S(1)} %broadcast_select_fusion.9), channel_id=1, source_target_pairs={{0,1},{1,2},{2,3},{3,4},{4,5},{5,6},{6,7},{7,8},{8,9},{9,10},{10,1... | collective-permute-start | bytes 1179656 | tf_op jit(solution)/shard_map/ppermute | solution.py:12
  178.3 18.9 %collective-permute-start.5 = (f32[384,256]{1,0:T(8,128)}, f32[384,256]{1,0:T(8,128)}, u32[]{:S(2)}, u32[]{:S(2)}) collective-permute-start(f32[384,256]{1,0:T(8,128)} %broadcast_select_fusion.8), channel_id=1, source_target_pairs={{1,0},{2,1},{3,2},{4,3},{5,4},{6,5},{7,6},{8,7},{9,8},{10,9},{11,1... | collective-permute-start | bytes 1179656 | tf_op jit(solution)/shard_map/ppermute | solution.py:12
  252.7 249.6 %all-gather.8.cloned.1.call-start = ((), (), s32[]{:S(2)}) async-start(), calls=%async_computation.2 | async-start | bytes 1179648 | tf_op jit(solution)/shard_map/all_gather | solution.py:59
  310.5 19.7 %collective-permute-start.6 = (f32[384,256]{1,0:T(8,128)S(1)}, f32[384,256]{1,0:T(8,128)}, u32[]{:S(2)}, u32[]{:S(2)}) collective-permute-start(f32[384,256]{1,0:T(8,128)S(1)} %broadcast_select_fusion.7), channel_id=1, source_target_pairs={{0,1},{1,2},{2,3},{3,4},{4,5},{5,6},{6,7},{7,8},{8,9},{9,10},{10,1... | collective-permute-start | bytes 1179656 | tf_op jit(solution)/shard_map/ppermute | solution.py:12
  316.1 19.8 %collective-permute-start.7 = (f32[384,256]{1,0:T(8,128)}, f32[384,256]{1,0:T(8,128)}, u32[]{:S(2)}, u32[]{:S(2)}) collective-permute-start(f32[384,256]{1,0:T(8,128)} %broadcast_select_fusion.6), channel_id=1, source_target_pairs={{1,0},{2,1},{3,2},{4,3},{5,4},{6,5},{7,6},{8,7},{9,8},{10,9},{11,1... | collective-permute-start | bytes 1179656 | tf_op jit(solution)/shard_map/ppermute | solution.py:12
  380.8 20.4 %collective-permute-start.8 = (f32[384,256]{1,0:T(8,128)S(1)}, f32[384,256]{1,0:T(8,128)}, u32[]{:S(2)}, u32[]{:S(2)}) collective-permute-start(f32[384,256]{1,0:T(8,128)S(1)} %broadcast_select_fusion.5), channel_id=1, source_target_pairs={{0,1},{1,2},{2,3},{3,4},{4,5},{5,6},{6,7},{7,8},{8,9},{9,10},{10,1... | collective-permute-start | bytes 1179656 | tf_op jit(solution)/shard_map/ppermute | solution.py:12
  387.9 18.9 %collective-permute-start.9 = (f32[384,256]{1,0:T(8,128)}, f32[384,256]{1,0:T(8,128)}, u32[]{:S(2)}, u32[]{:S(2)}) collective-permute-start(f32[384,256]{1,0:T(8,128)} %broadcast_select_fusion.4), channel_id=1, source_target_pairs={{1,0},{2,1},{3,2},{4,3},{5,4},{6,5},{7,6},{8,7},{9,8},{10,9},{11,1... | collective-permute-start | bytes 1179656 | tf_op jit(solution)/shard_map/ppermute | solution.py:12
  518.9 19.7 %collective-permute-start.10 = (f32[384,256]{1,0:T(8,128)S(1)}, f32[384,256]{1,0:T(8,128)S(1)}, u32[]{:S(2)}, u32[]{:S(2)}) collective-permute-start(f32[384,256]{1,0:T(8,128)S(1)} %broadcast_select_fusion.3), channel_id=1, source_target_pairs={{0,1},{1,2},{2,3},{3,4},{4,5},{5,6},{6,7},{7,8},{8,9},{9,10},{10,1... | collective-permute-start | bytes 1179656 | tf_op jit(solution)/shard_map/ppermute | solution.py:12
  523.4 20.6 %collective-permute-start.11 = (f32[384,256]{1,0:T(8,128)}, f32[384,256]{1,0:T(8,128)S(1)}, u32[]{:S(2)}, u32[]{:S(2)}) collective-permute-start(f32[384,256]{1,0:T(8,128)} %broadcast_select_fusion.2), channel_id=1, source_target_pairs={{1,0},{2,1},{3,2},{4,3},{5,4},{6,5},{7,6},{8,7},{9,8},{10,9},{11,1... | collective-permute-start | bytes 1179656 | tf_op jit(solution)/shard_map/ppermute | solution.py:12
  580.0 3.3 copy-start.17
  587.4 20.6 %collective-permute-start.12 = (f32[384,256]{1,0:T(8,128)}, f32[384,256]{1,0:T(8,128)S(1)}, u32[]{:S(2)}, u32[]{:S(2)}) collective-permute-start(f32[384,256]{1,0:T(8,128)} %broadcast_select_fusion.1), channel_id=1, source_target_pairs={{0,1},{1,2},{2,3},{3,4},{4,5},{5,6},{6,7},{7,8},{8,9},{9,10},{10,1... | collective-permute-start | bytes 1179656 | tf_op jit(solution)/shard_map/ppermute | solution.py:12
  593.3 19.8 %collective-permute-start.13 = (f32[384,256]{1,0:T(8,128)}, f32[384,256]{1,0:T(8,128)S(1)}, u32[]{:S(2)}, u32[]{:S(2)}) collective-permute-start(f32[384,256]{1,0:T(8,128)} %broadcast_select_fusion), channel_id=1, source_target_pairs={{1,0},{2,1},{3,2},{4,3},{5,4},{6,5},{7,6},{8,7},{9,8},{10,9},{11,1... | collective-permute-start | bytes 1179656 | tf_op jit(solution)/shard_map/ppermute | solution.py:12
  599.2 8.8 %copy-start.14 = (s32[384]{0:T(512)S(1)}, s32[384]{0:T(512)}, u32[]{:S(2)}) copy-start(s32[384]{0:T(512)} %copy-done.12) | copy-start | bytes 4612
  600.9 12.2 %copy-start.11 = (s32[384]{0:T(512)S(1)}, s32[384]{0:T(512)}, u32[]{:S(2)}) copy-start(s32[384]{0:T(512)} %copy-done.9) | copy-start | bytes 4612
  621.1 40.6 %copy-start.28 = (f32[256]{0:T(256)S(1)}, f32[256]{0:T(256)}, u32[]{:S(2)}) copy-start(f32[256]{0:T(256)} %copy-done.27) | copy-start | bytes 3076
  621.1 40.6 %copy-start.30 = (f32[256]{0:T(256)S(1)}, f32[256]{0:T(256)}, u32[]{:S(2)}) copy-start(f32[256]{0:T(256)} %copy-done.29) | copy-start | bytes 3076
  (17 other events, 37.5 us)
Sparse Core Ops, SparseCore 0:
  49.6 41.5 all-gather.3
  252.8 39.8 all-gather.5
  462.5 39.8 all-gather.7
where the time goes:
time: 690 us; the launch traced here: 679 us
  waiting for transfers between devices  168 us (24%)
  other arithmetic  119 us (17%)
  blocking collectives  116 us (17%)
  local copies, waits for them, and re-layouts  110 us (16%)
  matrix products  110 us (16%)
  starting transfers between devices  39.4 us (6%)
  between operations  15.9 us (2%)
    psum x3, blocking collectives, local(): lax.psum((jnp.sum(share * residual * image, axis=0), jnp.sum(share * imag...  116 us
    all_gather x3, waiting for transfers between devices, local(): lax.all_gather(modal, 'sub', axis=0, tiled=True)  93.3 us
    dot_general x3, matrix products, local(): jnp.dot(schur, direction, precision=highest, preferred_element_type=jnp.f...  82.9 us
    ppermute x14, waiting for transfers between devices, passed_along(): return lax.ppermute(value, axis, pairs)  74.6 us
    gather x14, local copies, waits for them, and re-layouts, take_rows(): return jnp.take(field, indices, axis=0, mode='fill', fill_value=0.0)  43 us
    ppermute x14, starting transfers between devices, passed_along(): return lax.ppermute(value, axis, pairs)  39.2 us
    scatter-add x7, other arithmetic, assemble(): return merged.at[right_index].add(from_right, mode='drop')  36.5 us
    scatter-add x7, other arithmetic, assemble(): merged = field.at[left_index].add(from_left, mode='drop')  36.1 us
  transfers between devices with their start and end apart: 17, of which 10 were waited for; matrix products, arithmetic and copies ran while one was open for 14% of the time, Pallas kernels for 0%

commit v1 on v0

v1 whole, which is shorter than its diff:
```python
import functools

import jax
import jax.numpy as jnp
from jax import lax
from jax.experimental import pallas as pl
from jax.experimental.pallas import tpu as pltpu
from jax.sharding import PartitionSpec as P

BOTH = ("cluster", "sub")
F32 = jnp.float32
BF16 = jnp.bfloat16
ITERS = 3
INTERPRET = False


def split2(x):
    hi = x.astype(BF16)
    return hi, (x - hi.astype(F32)).astype(BF16)


def split3(x):
    hi = x.astype(BF16)
    rest = x - hi.astype(F32)
    mid = rest.astype(BF16)
    return hi, mid, (rest - mid.astype(F32)).astype(BF16)


def mm(a, b):
    return jnp.dot(a, b, preferred_element_type=F32)


def mm_nt(a, b):
    return lax.dot_general(a, b, (((1,), (1,)), ((), ())), preferred_element_type=F32)


def mm3(a, b):
    return mm(a[0], b[0]) + (mm(a[0], b[1]) + mm(a[1], b[0]))


def pick(onehot, parts):
    return sum(mm(onehot, part) for part in parts)


def accumulate(ref, value):
    first = pl.program_id(0) == 0

    @pl.when(first)
    def _():
        ref[...] = value

    @pl.when(jnp.logical_not(first))
    def _():
        ref[...] += value


def block_of(order):
    return 256 if order % 256 == 0 else order


def call(body, name, grid, ins, outs, flops, scratch=()):
    specs = [s for _, s in ins]
    arrays = [a for a, _ in ins]
    moved = sum(a.size * a.dtype.itemsize for a in arrays)
    moved += sum(functools.reduce(lambda p, q: p * q, s, 1) * jnp.dtype(d).itemsize for s, d, _ in outs)
    return pl.pallas_call(
        body,
        name=name,
        grid=grid,
        in_specs=specs,
        out_specs=[s for _, _, s in outs],
        out_shape=[jax.ShapeDtypeStruct(s, d) for s, d, _ in outs],
        scratch_shapes=list(scratch),
        cost_estimate=pl.CostEstimate(flops=int(flops), bytes_accessed=int(moved), transcendentals=0),
        compiler_params=pltpu.CompilerParams(vmem_limit_bytes=48 * 1024 * 1024),
        interpret=INTERPRET,
    )(*arrays)


def whole(a):
    shape = a.shape
    return (a, pl.BlockSpec(shape, lambda *_: (0,) * len(shape)))


def rows_of(a, b):
    return (a, pl.BlockSpec((b, a.shape[1]), lambda k: (k, 0)))


def cols_of(a, b):
    return (a, pl.BlockSpec((a.shape[0], b), lambda k: (0, k)))


def out_rows(shape, dtype, b):
    return (shape, dtype, pl.BlockSpec((b, shape[1]), lambda k: (k, 0)))


def out_cols(shape, dtype, b):
    return (shape, dtype, pl.BlockSpec((shape[0], b), lambda k: (0, k)))


def out_whole(shape, dtype):
    return (shape, dtype, pl.BlockSpec(shape, lambda *_: (0,) * len(shape)))


def scalar(a):
    return (a, pl.BlockSpec(memory_space=pltpu.SMEM))


def gather_load(index_col, load, b):
    two, (order, k) = index_col.shape[0], load.shape
    half = two // 2

    def body(idx_ref, load_ref, g_ref, left_ref, right_ref):
        lane = lax.broadcasted_iota(jnp.int32, (two, b), 1) + pl.program_id(0) * b
        onehot = jnp.where(idx_ref[...] == lane, 1.0, 0.0).astype(BF16)
        g_ref[...] = onehot
        rows = pick(onehot, split3(load_ref[...]))
        accumulate(left_ref, rows[:half])
        accumulate(right_ref, rows[half:])

    return call(
        body, "gather_load", (order // b,),
        [whole(index_col), rows_of(load, b)],
        [out_cols((two, order), BF16, b), out_whole((half, k), F32), out_whole((half, k), F32)],
        6 * two * order * k,
    )


def prepare(live_rows, live_modes, index_row, onehot, schur, modes, modes_t, b):
    two, order = onehot.shape
    half = two // 2
    nm = modes.shape[1]
    pieces = half // nm
    tall = half + 8 * pieces
    steps = order // b

    def body(rows_ref, count_ref, idx_ref, g_ref, s_ref, modes_ref, modes_t_ref,
             hi_ref, lo_ref, gt_ref, phi_ref, pth_ref, ptl_ref, vec_ref,
             left_ref, right_ref, pts_ref, sd_ref):
        k = pl.program_id(0)
        start = k * b
        hi, lo = split2(s_ref[...])
        hi_ref[...] = hi
        lo_ref[...] = lo
        row_id = lax.broadcasted_iota(jnp.int32, (b, two), 0) + start
        gt = jnp.where(idx_ref[...] == row_id, 1.0, 0.0)
        gt_ref[...] = gt.astype(BF16)
        g = g_ref[...]
        live_c = jnp.where(lax.broadcasted_iota(jnp.int32, (b, 1), 0) + start < rows_ref[0], 1.0, 0.0)
        live_r = jnp.where(lax.broadcasted_iota(jnp.int32, (1, b), 1) + start < rows_ref[0], 1.0, 0.0)
        share_c = live_c / (1.0 + jnp.sum(gt, axis=1, keepdims=True))
        share_r = live_r / (1.0 + jnp.sum(g.astype(F32), axis=0, keepdims=True))
        square = s_ref[:, pl.ds(pl.multiple_of(start, b), b)]
        eye = lax.broadcasted_iota(jnp.int32, (b, b), 0) == lax.broadcasted_iota(jnp.int32, (b, b), 1)
        square = jnp.where(eye, square, 0.0)
        sd_c = share_c / jnp.sum(square, axis=1, keepdims=True)
        sd_r = share_r / jnp.sum(square, axis=0, keepdims=True)
        lane = lax.broadcasted_iota(jnp.int32, (b, 128), 1)
        vec_ref[...] = jnp.where(lane == 0, share_c, jnp.where(lane == 1, live_c, sd_c))
        mask_r = jnp.where(lax.broadcasted_iota(jnp.int32, (1, nm), 1) < count_ref[0], 1.0, 0.0)
        mask_c = jnp.where(lax.broadcasted_iota(jnp.int32, (nm, 1), 0) < count_ref[0], 1.0, 0.0)
        phi = share_c * (modes_ref[...] * mask_r)
        phi_ref[...] = phi
        phi_t = share_r * (modes_t_ref[...] * mask_c)
        pth, ptl = split2(phi_t)
        pth_ref[...] = pth
        ptl_ref[...] = ptl
        shared = pick(g, split3(phi))
        accumulate(pts_ref, mm_nt(pth, g) + mm_nt(ptl, g))
        parts = [jnp.broadcast_to(p.astype(F32), (16, b)).astype(BF16) for p in split3(sd_r)]
        found = mm_nt(jnp.concatenate(parts, axis=0), g)
        accumulate(sd_ref, found[0:8] + found[16:24] + found[32:40])

        @pl.when(k == 0)
        def _():
            left_ref[:half] = shared[:half]
            right_ref[:half] = shared[half:]

        @pl.when(k > 0)
        def _():
            left_ref[:half] += shared[:half]
            right_ref[:half] += shared[half:]

        @pl.when(k == steps - 1)
        def _():
            for t in range(pieces):
                left_ref[half + 8 * t:half + 8 * t + 8] = sd_ref[:, t * nm:(t + 1) * nm]
                right_ref[half + 8 * t:half + 8 * t + 8] = sd_ref[:, half + t * nm:half + (t + 1) * nm]

    return call(
        body, "prepare", (steps,),
        [scalar(live_rows), scalar(live_modes), whole(index_row), cols_of(onehot, b),
         rows_of(schur, b), rows_of(modes, b), cols_of(modes_t, b)],
        [out_rows((order, order), BF16, b), out_rows((order, order), BF16, b),
         out_rows((order, two), BF16, b), out_rows((order, nm), F32, b),
         out_cols((nm, order), BF16, b), out_cols((nm, order), BF16, b),
         out_rows((order, 128), F32, b), out_whole((tall, nm), F32), out_whole((tall, nm), F32),
         out_whole((nm, two), F32)],
        2 * two * order * nm * 5,
        scratch=[pltpu.VMEM((8, two), F32)],
    )


def extend(onehot_t, phi, vec, from_prev, from_next, b):
    order, two = onehot_t.shape
    half = two // 2
    nm = phi.shape[1]
    pieces = half // nm

    def rows_at(ref):
        return jnp.concatenate([ref[half + 8 * t:half + 8 * t + 8] for t in range(pieces)], axis=1)

    def body(gt_ref, phi_ref, vec_ref, prev_ref, next_ref, hi_ref, lo_ref, w_ref):
        gt = gt_ref[...]
        total = vec_ref[:, 2:3]
        own = split2(phi_ref[...])
        hi_ref[:, :nm], lo_ref[:, :nm] = own
        for i, ref in enumerate((prev_ref, next_ref)):
            sel = gt[:, i * half:(i + 1) * half]
            hi, lo = split2(pick(sel, split2(ref[:half])))
            hi_ref[:, (i + 1) * nm:(i + 2) * nm] = hi
            lo_ref[:, (i + 1) * nm:(i + 2) * nm] = lo
            for part in split3(rows_at(ref)):
                wide = jnp.concatenate([part.astype(F32), part.astype(F32)], axis=0).astype(BF16)
                total = total + mm_nt(sel, wide)[:, 0:1]
        w_ref[...] = jnp.broadcast_to(total, (b, 128))

    return call(
        body, "extend", (order // b,),
        [rows_of(onehot_t, b), rows_of(phi, b), rows_of(vec, b), whole(from_prev), whole(from_next)],
        [out_rows((order, 3 * nm), BF16, b), out_rows((order, 3 * nm), BF16, b),
         out_rows((order, 128), F32, b)],
        2 * order * half * nm * 4,
    )


def restrict_start(phi_t, field, b):
    nm, order = phi_t[0].shape
    k = field.shape[1]

    def body(h_ref, l_ref, f_ref, o_ref):
        accumulate(o_ref, mm3((h_ref[...], l_ref[...]), split2(f_ref[...])))

    return call(
        body, "restrict_start", (order // b,),
        [cols_of(phi_t[0], b), cols_of(phi_t[1], b), rows_of(field, b)],
        [out_whole((nm, k), F32)], 6 * nm * order * k,
    )[0]


def restrict_finish(phi_ts, from_prev, from_next, own, scale=None, before=None):
    nm, two = phi_ts.shape
    half = two // 2
    k = own.shape[1]
    chained = scale is not None

    def body(p_ref, a_ref, c_ref, m_ref, *rest):
        left = mm3(split2(p_ref[:, :half]), split2(a_ref[...]))
        right = mm3(split2(p_ref[:, half:]), split2(c_ref[...]))
        total = m_ref[...] + (left + right)
        if chained:
            total = rest[1][...] - rest[0][0:1] * total
        rest[-1][...] = total

    ins = [whole(phi_ts), whole(from_prev), whole(from_next), whole(own)]
    if chained:
        ins += [whole(scale), whole(before)]
    return call(body, "restrict_finish", (1,), ins, [out_whole((nm, k), F32)], 6 * nm * two * k)[0]


def coarse(inverse, blocks):
    nm, co = inverse.shape
    k = blocks[0].shape[1]
    n = len(blocks)
    size = blocks[0].shape[0]

    def body(i_ref, *rest):
        o_ref = rest[n]
        xh, xl = rest[n + 1], rest[n + 2]
        for i in range(n):
            hi, lo = split2(rest[i][...])
            xh[i * size:(i + 1) * size] = hi
            xl[i * size:(i + 1) * size] = lo
        o_ref[...] = mm3(split2(i_ref[...]), (xh[...], xl[...]))

    return call(
        body, "coarse", (1,),
        [whole(inverse)] + [whole(x) for x in blocks],
        [out_whole((nm, k), F32)], 6 * nm * co * k,
        scratch=[pltpu.VMEM((co, k), BF16), pltpu.VMEM((co, k), BF16)],
    )[0]


def assemble_first(onehot_t, vec, w, load, from_prev, from_next, b):
    order, two = onehot_t.shape
    half = two // 2
    k = load.shape[1]

    def body(gt_ref, vec_ref, w_ref, f_ref, a_ref, c_ref, r_ref, xh_ref, xl_ref):
        gt = gt_ref[...]
        r = vec_ref[:, 1:2] * f_ref[...]
        r = r + pick(gt[:, :half], split3(a_ref[...]))
        r = r + pick(gt[:, half:], split3(c_ref[...]))
        r_ref[...] = r
        xh_ref[...], xl_ref[...] = split2(w_ref[:, 0:1] * r)

    return call(
        body, "assemble_first", (order // b,),
        [rows_of(onehot_t, b), rows_of(vec, b), rows_of(w, b), rows_of(load, b),
         whole(from_prev), whole(from_next)],
        [out_rows((order, k), F32, b), out_rows((order, k), BF16, b), out_rows((order, k), BF16, b)],
        6 * order * two * k,
    )


def assemble_image(onehot_t, vec, w, q, from_prev, from_next, resid, b, scale=None, image=None, last=False):
    order, two = onehot_t.shape
    half = two // 2
    k = q.shape[1]
    chained = scale is not None
    n_in = 9 if chained else 7

    def body(*refs):
        gt_ref, vec_ref, w_ref, q_ref, a_ref, c_ref, r_ref = refs[:7]
        outs = list(refs[n_in:])
        gt = gt_ref[...]
        new = q_ref[...]
        new = new + pick(gt[:, :half], split2(a_ref[...]))
        new = new + pick(gt[:, half:], split2(c_ref[...]))
        r = r_ref[...]
        if chained:
            s = refs[7][0:1]
            old = refs[8][...]
            new = old - s * new
            if not last:
                r = r - s * old
                outs.pop(0)[...] = r
        outs.pop(0)[...] = new
        weighted = vec_ref[:, 0:1] * new
        num = jnp.sum(weighted * r, axis=0, keepdims=True)
        den = jnp.sum(weighted * new, axis=0, keepdims=True)
        row = lax.broadcasted_iota(jnp.int32, (8, k), 0)
        accumulate(outs.pop(0), jnp.where(row == 0, num, jnp.where(row == 1, den, 0.0)))
        if not last:
            outs[0][...], outs[1][...] = split2(w_ref[:, 0:1] * new)

    ins = [rows_of(onehot_t, b), rows_of(vec, b), rows_of(w, b), rows_of(q, b),
           whole(from_prev), whole(from_next), rows_of(resid, b)]
    outs = []
    if chained:
        ins += [whole(scale), rows_of(image, b)]
        if not last:
            outs += [out_rows((order, k), F32, b)]
    outs += [out_rows((order, k), F32, b), out_whole((8, k), F32)]
    if not last:
        outs += [out_rows((order, k), BF16, b), out_rows((order, k), BF16, b)]
    return call(body, "assemble_image", (order // b,), ins, outs, 4 * order * two * k)


def schur_first(s, onehot, x, px, b):
    order = s[0].shape[0]
    two = onehot.shape[0]
    k = x[0].shape[1]
    n = px[0].shape[1]

    def body(sh_ref, sl_ref, g_ref, xh_ref, xl_ref, ph_ref, pl_ref, y_ref, ys_ref, qh_ref, ql_ref, qs_ref):
        sh, sl, g = sh_ref[...], sl_ref[...], g_ref[...]
        y = mm3((sh, sl), (xh_ref[...], xl_ref[...]))
        y_ref[...] = y
        accumulate(ys_ref, pick(g, split2(y)))
        parts = split2(mm3((sh, sl), (ph_ref[...], pl_ref[...])))
        qh_ref[...], ql_ref[...] = parts
        accumulate(qs_ref, pick(g, parts))

    return call(
        body, "schur_first", (order // b,),
        [rows_of(s[0], b), rows_of(s[1], b), cols_of(onehot, b), whole(x[0]), whole(x[1]),
         whole(px[0]), whole(px[1])],
        [out_rows((order, k), F32, b), out_whole((two, k), F32),
         out_rows((order, n), BF16, b), out_rows((order, n), BF16, b), out_whole((two, n), F32)],
        6 * order * order * (k + n) + 4 * two * order * (k + n),
    )


def schur_apply(s, onehot, x, b):
    order = s[0].shape[0]
    two = onehot.shape[0]
    k = x[0].shape[1]

    def body(sh_ref, sl_ref, g_ref, xh_ref, xl_ref, y_ref, ys_ref):
        y = mm3((sh_ref[...], sl_ref[...]), (xh_ref[...], xl_ref[...]))
        y_ref[...] = y
        accumulate(ys_ref, pick(g_ref[...], split2(y)))

    return call(
        body, "schur_apply", (order // b,),
        [rows_of(s[0], b), rows_of(s[1], b), cols_of(onehot, b), whole(x[0]), whole(x[1])],
        [out_rows((order, k), F32, b), out_whole((two, k), F32)],
        6 * order * order * k + 4 * two * order * k,
    )


def shared_image(q_shared, y_shared, stack):
    two, n = q_shared.shape
    half = two // 2
    nm, k = stack[0].shape

    def body(q_ref, y_ref, a_ref, b_ref, c_ref, left_ref, right_ref):
        total = y_ref[...]
        for i, ref in enumerate((a_ref, b_ref, c_ref)):
            total = total + mm3(split2(q_ref[:, i * nm:(i + 1) * nm]), split2(ref[...]))
        left_ref[...] = total[:half]
        right_ref[...] = total[half:]

    return call(
        body, "shared_image", (1,),
        [whole(q_shared), whole(y_shared)] + [whole(x) for x in stack],
        [out_whole((half, k), F32), out_whole((half, k), F32)], 6 * two * n * k,
    )


def local_image(q, y, vec, phi_t, stack, b, restrict):
    order, n = q[0].shape
    nm, k = stack[0].shape

    def body(qh_ref, ql_ref, y_ref, vec_ref, th_ref, tl_ref, a_ref, b_ref, c_ref, o_ref, *m_ref):
        total = y_ref[...]
        for i, ref in enumerate((a_ref, b_ref, c_ref)):
            part = slice(i * nm, (i + 1) * nm)
            total = total + mm3((qh_ref[:, part], ql_ref[:, part]), split2(ref[...]))
        total = vec_ref[:, 1:2] * total
        o_ref[...] = total
        if restrict:
            accumulate(m_ref[0], mm3((th_ref[...], tl_ref[...]), split2(total)))

    outs = [out_rows((order, k), F32, b)]
    if restrict:
        outs += [out_whole((nm, k), F32)]
    return call(
        body, "local_image", (order // b,),
        [rows_of(q[0], b), rows_of(q[1], b), rows_of(y, b), rows_of(vec, b),
         cols_of(phi_t[0], b), cols_of(phi_t[1], b)] + [whole(x) for x in stack],
        outs, 6 * order * n * k + 6 * nm * order * k,
    )


def directions(px, w, scales, resids, image, stacks, b):
    order, n = px[0].shape
    nm, k = stacks[0][0].shape
    (a0, a1), (r0, r1) = scales, resids
    c0, e0, e1 = stacks

    def body(h_ref, l_ref, w_ref, a0_ref, a1_ref, r0_ref, r1_ref, i1_ref, *rest):
        sol_ref, res_ref, dir_ref = rest[9:]
        s0, s1 = a0_ref[0:1], a1_ref[0:1]
        wc = w_ref[:, 0:1]
        x0, x1 = r0_ref[...], r1_ref[...]
        x2 = x1 - s1 * i1_ref[...]
        sol = wc * (s0 * x0 + s1 * x1)
        last = wc * x2
        for i in range(3):
            part = slice(i * nm, (i + 1) * nm)
            p = (h_ref[:, part], l_ref[:, part])
            c = rest[i][...]
            d = c - s0 * rest[3 + i][...]
            f = d - s1 * rest[6 + i][...]
            sol = sol + mm3(p, split2(s0 * c + s1 * d))
            last = last + mm3(p, split2(f))
        sol_ref[...] = sol
        res_ref[...] = x2
        dir_ref[...] = last

    return call(
        body, "directions", (order // b,),
        [rows_of(px[0], b), rows_of(px[1], b), rows_of(w, b), whole(a0), whole(a1),
         rows_of(r0, b), rows_of(r1, b), rows_of(image, b)] + [whole(x) for x in (*c0, *e0, *e1)],
        [out_rows((order, k), F32, b)] * 3, 12 * order * n * k,
    )


def passed_along(value, by):
    n = lax.axis_size(BOTH)
    return lax.ppermute(value, BOTH, [(i, i + by) for i in range(n) if 0 <= i + by < n])


def exchanged(to_prev, to_next):
    return passed_along(to_next, 1), passed_along(to_prev, -1)


def power_of_two(n):
    return n & (n - 1) == 0


def summed(value):
    for axis in BOTH:
        n = lax.axis_size(axis)
        if not power_of_two(n):
            value = lax.psum(value, axis)
            continue
        step = 1
        while step < n:
            value = value + lax.ppermute(value, axis, [(i, i ^ step) for i in range(n)])
            step *= 2
    return value


def direct(n):
    return power_of_two(n) and n <= 8


def cluster_blocks(modal):
    n = lax.axis_size("sub")
    if not direct(n):
        return [lax.all_gather(modal, "sub", axis=0, tiled=True)]
    return [modal] + [lax.ppermute(modal, "sub", [(i, i ^ d) for i in range(n)]) for d in range(1, n)]


def ordered_inverse(inverse):
    n = lax.axis_size("sub")
    if not direct(n):
        return inverse
    me = lax.axis_index("sub")
    size = inverse.shape[1] // n
    return jnp.concatenate(
        [lax.dynamic_slice_in_dim(inverse, (me ^ d) * size, size, 1) for d in range(n)], axis=1
    )


def local(load, schur, modes, coarse_inverse, interface_rows, mode_count, left_rows, right_rows):
    b = block_of(schur.shape[0])
    index_row = jnp.concatenate([left_rows, right_rows], axis=1)
    index_col = index_row.reshape(-1, 1)
    inverse = ordered_inverse(coarse_inverse)

    onehot, left, right = gather_load(index_col, load, b)
    from_prev, from_next = exchanged(left, right)
    s_hi, s_lo, onehot_t, phi, pt_hi, pt_lo, vec, phi_left, phi_right, phi_ts = prepare(
        interface_rows, mode_count, index_row, onehot, schur, modes, modes.T, b
    )
    s, phi_t = (s_hi, s_lo), (pt_hi, pt_lo)
    phi_prev, phi_next = exchanged(phi_left, phi_right)
    own = restrict_start(phi_t, load, b)
    modal = restrict_finish(phi_ts, from_prev, from_next, own)
    blocks = cluster_blocks(modal)
    px_hi, px_lo, w = extend(onehot_t, phi, vec, phi_prev, phi_next, b)
    px = (px_hi, px_lo)
    resid, x_hi, x_lo = assemble_first(onehot_t, vec, w, load, from_prev, from_next, b)
    y, y_shared, q_hi, q_lo, q_shared = schur_first(s, onehot, (x_hi, x_lo), px, b)
    q = (q_hi, q_lo)

    scales, resids, stacks = [], [resid], []
    image = scale = None
    for iteration in range(ITERS):
        last = iteration == ITERS - 1
        center = coarse(inverse, blocks)
        before, after = exchanged(center, center)
        stack = (center, before, after)
        stacks.append(stack)
        left, right = shared_image(q_shared, y_shared, stack)
        from_prev, from_next = exchanged(left, right)
        found = local_image(q, y, vec, phi_t, stack, b, not last)
        field = found[0]
        if iteration > 0:
            scale = sums[0:1] / (sums[1:2] + 1e-06)
            scale = jnp.broadcast_to(scale, (8, scale.shape[1]))
            scales.append(scale)
        if not last:
            previous = modal
            modal = restrict_finish(phi_ts, from_prev, from_next, found[1], scale,
                                    None if scale is None else image_modal)
            image_modal = modal
            blocks = cluster_blocks(modal)
            made = assemble_image(onehot_t, vec, w, field, from_prev, from_next, resid, b, scale, image)
            if iteration > 0:
                resid, made = made[0], made[1:]
                resids.append(resid)
            image, sums, x_hi, x_lo = made
            sums = summed(sums)
            y, y_shared = schur_apply(s, onehot, (x_hi, x_lo), b)
        else:
            sol, resid, final = directions(px, w, scales, resids, image, stacks, b)
            image, sums = assemble_image(onehot_t, vec, w, field, from_prev, from_next, resid, b,
                                         scale, image, last=True)
            sums = summed(sums)
    scale = sums[0:1] / (sums[1:2] + 1e-06)
    return sol + scale * final, resid - scale * image


def solution(mesh):
    rows = P(BOTH, None)
    return jax.shard_map(
        local,
        mesh=mesh,
        in_specs=(rows, rows, rows, rows, P(BOTH), P(BOTH), rows, rows),
        out_specs=(rows, rows),
        check_vma=False,
    )
```

time: 690 us -> 358 us (0.52); the launches traced: 679 us -> 355 us
  Pallas kernels: 0 us -> 167 us
  other arithmetic: 119 us -> 2.39 us
  blocking collectives: 116 us -> 0 us
  matrix products: 110 us -> 0 us
  waiting for transfers between devices: 168 us -> 70.5 us
  local copies, waits for them, and re-layouts: 110 us -> 17.6 us
  starting transfers between devices: 39.4 us -> 95.7 us
  between operations: 15.9 us -> 2.52 us
    pallas_call x0 -> x24, Pallas kernels: none -> 167 us  [call(): pl.pallas_call(body, name=name, grid=grid, in_specs=specs, out_specs=[s f...]
    psum x3 -> x0, blocking collectives: 116 us -> none  [local(): lax.psum((jnp.sum(share * residual * image, axis=0), jnp.sum(share * imag...]
    dot_general x12 -> x0, matrix products: 110 us -> none  [the longest x3 82.9 us: local(): jnp.dot(schur, direction, precision=highest, preferred_element_type=jnp.f...]
    all_gather x3 -> x0, waiting for transfers between devices: 93.3 us -> none  [local(): lax.all_gather(modal, 'sub', axis=0, tiled=True)]
    scatter-add x16 -> x0, other arithmetic: 80 us -> none  [the longest x7 36.5 us: assemble(): return merged.at[right_index].add(from_right, mode='drop')]
    gather x15 -> x0, local copies, waits for them, and re-layouts: 71 us -> none  [the longest x14 43 us: take_rows(): return jnp.take(field, indices, axis=0, mode='fill', fill_value=0.0)]
    ppermute x14 -> x52, starting transfers between devices: 39.2 us -> 95.7 us  [the longest x16 46.1 us: passed_along(): lax.ppermute(value, BOTH, [(i, i + by) for i in range(n) if 0 <= i + by <...]
    select_n x18 -> x0, other arithmetic: 18.8 us -> none  [the longest x16 17.4 us: take_rows(): return jnp.take(field, indices, axis=0, mode='fill', fill_value=0.0)]
  transfers between devices with their start and end apart: 17 -> 52, of which waited for: 10 -> 21; matrix products, arithmetic and copies ran while one was open for 14% -> 1% of each run, Pallas kernels for 0% -> 42%
where the time goes in v1:
time: 358 us; the launch traced here: 355 us
  Pallas kernels  167 us (47%)
  starting transfers between devices  95.7 us (27%)
  waiting for transfers between devices  70.5 us (20%)
  local copies, waits for them, and re-layouts  17.6 us (5%)
    pallas_call x24, Pallas kernels, call(): pl.pallas_call(body, name=name, grid=grid, in_specs=specs, out_specs=[s f...  167 us
    ppermute x16, starting transfers between devices, passed_along(): lax.ppermute(value, BOTH, [(i, i + by) for i in range(n) if 0 <= i + by <...  46.1 us
    ppermute x15, waiting for transfers between devices, summed(): value = value + lax.ppermute(value, axis, [(i, i ^ step) for i in range(n)])  44.2 us
    ppermute x21, starting transfers between devices, cluster_blocks(): lax.ppermute(modal, 'sub', [(i, i ^ d) for i in range(n)])  39.2 us
    unnamed x45, local copies, waits for them, and re-layouts  16.7 us
    ppermute x16, waiting for transfers between devices, passed_along(): lax.ppermute(value, BOTH, [(i, i + by) for i in range(n) if 0 <= i + by <...  14.9 us
    ppermute x21, waiting for transfers between devices, cluster_blocks(): lax.ppermute(modal, 'sub', [(i, i ^ d) for i in range(n)])  11.4 us
    ppermute x15, starting transfers between devices, summed(): value = value + lax.ppermute(value, axis, [(i, i ^ step) for i in range(n)])  10.4 us
  transfers between devices with their start and end apart: 52, of which 21 were waited for; matrix products, arithmetic and copies ran while one was open for 1% of the time, Pallas kernels for 42%

profile of v1, /device:TPU:0, one launch (start us, length us, event | category | flops | bytes accessed | tf_op | source)
XLA Modules:
  0.0 355.3 jit_solution(16616056170404183927)
XLA Ops:
  3.7 5.3 %gather_load.1 = (bf16[768,1792]{1,0:T(8,128)(2,1)S(1)}, f32[384,256]{1,0:T(8,128)}, f32[384,256]{1,0:T(8,128)}) custom-call(s32[768,1]{1,0:T(8,128)S(1)} %copy.11.idx_ref, f32[1792,256]{1,0:T(8,128)S(1)} %copy-done.5), custom_call_target="tpu_custom_call" | custom-call | flops 2113929216 | bytes 5377024 | tf_op jit(solution)/shard_map/gather_load/pallas_call | solution.py:66
  10.5 4.9 %collective-permute-start.2 = (f32[384,256]{1,0:T(8,128)}, f32[384,256]{1,0:T(8,128)S(1)}, u32[]{:S(2)}, u32[]{:S(2)}) collective-permute-start(f32[384,256]{1,0:T(8,128)} %get-tuple-element.65), channel_id=1, source_target_pairs={{0,1},{1,2},{2,3},{3,4},{4,5},{5,6},{6,7},{7,8},{8,9},{9,10},{10,1... | collective-permute-start | bytes 1179656 | tf_op jit(solution)/shard_map/ppermute | solution.py:483
  20.4 18.0 %prepare.1 = (bf16[1792,1792]{1,0:T(8,128)(2,1)}, bf16[1792,1792]{1,0:T(8,128)(2,1)}, bf16[1792,768]{1,0:T(8,128)(2,1)}, f32[1792,128]{1,0:T(8,128)S(1)}, bf16[1...) custom-call(s32[1]{0:T(128)S(6)} %copy.21.rows_ref, ...), custom_call_target="tpu_custom_call" | custom-call | flops 1761607680 | bytes 36596744 | tf_op jit(solution)/shard_map/prepare/pallas_call | solution.py:66
  39.4 4.5 %collective-permute-start = (f32[408,128]{1,0:T(8,128)}, f32[408,128]{1,0:T(8,128)S(1)}, u32[]{:S(2)}, u32[]{:S(2)}) collective-permute-start(f32[408,128]{1,0:T(8,128)} %get-tuple-element.58), channel_id=1, source_target_pairs={{0,1},{1,2},{2,3},{3,4},{4,5},{5,6},{6,7},{7,8},{8,9},{9,10},{10,1... | collective-permute-start | bytes 626696 | tf_op jit(solution)/shard_map/ppermute | solution.py:483
  53.4 6.1 %collective-permute-start.10 = (f32[128,256]{1,0:T(8,128)S(1)}, f32[128,256]{1,0:T(8,128)S(1)}, u32[]{:S(2)}, u32[]{:S(2)}) collective-permute-start(f32[128,256]{1,0:T(8,128)S(1)} %restrict_finish.3.rest_0_), channel_id=1, source_target_pairs={{0,7},{1,6},{2,5},{3,4},{4,3},{5,2},{6,1},{7,0},{8,15},{9,14},{10,... | collective-permute-start | bytes 393224 | tf_op jit(solution)/shard_map/ppermute | solution.py:515
  60.1 7.3 %extend.1 = (bf16[1792,384]{1,0:T(8,128)(2,1)S(1)}, bf16[1792,384]{1,0:T(8,128)(2,1)S(1)}, f32[1792,128]{1,0:T(8,128)S(1)}) custom-call(bf16[1792,768]{1,0:T(8,128)(2,1)} %get-tuple-element.55.gt_ref.refs_0_, f32[1792,128]{1,0:T(8,128)S(1)} %copy-done.13, f32[1792,128]{1,0:T(8,128)S(1)} %get-tuple-element.57.vec_ref.refs_1_, ...), custom_call_target="tpu_custom_call" | custom-call | flops 704643072 | bytes 8675328 | tf_op jit(solution)/shard_map/extend/pallas_call | solution.py:66
  77.0 8.0 %assemble_first.1 = (f32[1792,256]{1,0:T(8,128)}, bf16[1792,256]{1,0:T(8,128)(2,1)S(1)}, bf16[1792,256]{1,0:T(8,128)(2,1)S(1)}) custom-call(bf16[1792,768]{1,0:T(8,128)(2,1)} %get-tuple-element.55.gt_ref.refs_0_, f32[1792,128]{1,0:T(8,128)S(1)} %get-tuple-element.57.vec_ref.refs_1_, f32[1792,128]{1,0:T(8,128)S(1)} %get-tuple-element.62.w_ref.refs_2_, ...), custom_call_target="tpu_custom_call" | custom-call | flops 2113929216 | bytes 10878976 | tf_op jit(solution)/shard_map/assemble_first/pallas_call | solution.py:66
  89.8 4.6 %collective-permute-start.11 = (f32[128,256]{1,0:T(8,128)S(1)}, f32[128,256]{1,0:T(8,128)S(1)}, u32[]{:S(2)}, u32[]{:S(2)}) collective-permute-start(f32[128,256]{1,0:T(8,128)S(1)} %coarse.3.a_ref.rest_0_), channel_id=1, source_target_pairs={{0,1},{1,2},{2,3},{3,4},{4,5},{5,6},{6,7},{7,8},{8,9},{9,10},{10,1... | collective-permute-start | bytes 393224 | tf_op jit(solution)/shard_map/ppermute | solution.py:483
  94.4 37.6 %schur_first.1 = (f32[1792,256]{1,0:T(8,128)}, f32[768,256]{1,0:T(8,128)S(1)}, bf16[1792,384]{1,0:T(8,128)(2,1)S(1)}, bf16[1792,384]{1,0:T(8,128)(2,1)}, f32[768,384]{1,0:T(8,128)S(1)}) custom-call(bf16[1792,1792]{1,0:T(8,128)(2,1)} %get-tuple-element.63.sh_ref, bf16[1792,1792]{1,0:T(8,128)(2,1)} %get-tuple-element.64.sl_ref, bf16[768,1792]{1,0:T(8,128)(2,1)} %copy-done.3, ...), custom_call_target="tpu_custom_call" | custom-call | flops 15854469120 | bytes 26738688 | tf_op jit(solution)/shard_map/schur_first/pallas_call | solution.py:66
  137.6 7.8 %local_image.3 = (f32[1792,256]{1,0:T(8,128)}, f32[128,256]{1,0:T(8,128)S(1)}) custom-call(bf16[1792,384]{1,0:T(8,128)(2,1)S(1)} %get-tuple-element.69.qh_ref, bf16[1792,384]{1,0:T(8,128)(2,1)S(1)} %copy-done, f32[1792,256]{1,0:T(8,128)} %get-tuple-element.71.y_ref, f32[1792,128]{1,0:T(8,128)S(1)} %get-tuple-element.57.vec_ref.refs_1_, ...), custom_call_target="tpu_custom_call" | custom-call | flops 1409286144 | bytes 8781824 | tf_op jit(solution)/shard_map/local_image/pallas_call | solution.py:66
  145.5 7.7 %collective-permute-done.13.refs_4_.a_ref = f32[384,256]{1,0:T(8,128)S(1)} collective-permute-done((f32[384,256]{1,0:T(8,128)S(1)}, f32[384,256]{1,0:T(8,128)S(1)}, u32[]{:S(2)}, u32[]{:S(2)}) %collective-permute-start.13) | collective-permute-done | bytes 393248 | tf_op jit(solution)/shard_map/ppermute | solution.py:483
  153.2 4.1 %collective-permute-done.14.refs_5_.c_ref = f32[384,256]{1,0:T(8,128)S(1)} collective-permute-done((f32[384,256]{1,0:T(8,128)S(1)}, f32[384,256]{1,0:T(8,128)S(1)}, u32[]{:S(2)}, u32[]{:S(2)}) %collective-permute-start.14) | collective-permute-done | bytes 393248 | tf_op jit(solution)/shard_map/ppermute | solution.py:483
  160.5 4.8 %collective-permute-start.23 = (f32[128,256]{1,0:T(8,128)S(1)}, f32[128,256]{1,0:T(8,128)S(1)}, u32[]{:S(2)}, u32[]{:S(2)}) collective-permute-start(f32[128,256]{1,0:T(8,128)S(1)} %restrict_finish.4.rest_0_.rest_1_), channel_id=1, source_target_pairs={{0,4},{1,5},{2,6},{3,7},{4,0},{5,1},{6,2},{7,3},{8,12},{9,13},{10,... | collective-permute-start | bytes 393224 | tf_op jit(solution)/shard_map/ppermute | solution.py:515
  166.8 6.2 %collective-permute-start.21 = (f32[128,256]{1,0:T(8,128)S(1)}, f32[128,256]{1,0:T(8,128)S(1)}, u32[]{:S(2)}, u32[]{:S(2)}) collective-permute-start(f32[128,256]{1,0:T(8,128)S(1)} %restrict_finish.4.rest_0_.rest_1_), channel_id=1, source_target_pairs={{0,2},{1,3},{2,0},{3,1},{4,6},{5,7},{6,4},{7,5},{8,10},{9,11},{10,... | collective-permute-start | bytes 393224 | tf_op jit(solution)/shard_map/ppermute | solution.py:515
  173.5 7.6 %assemble_image.3 = (f32[1792,256]{1,0:T(8,128)}, f32[8,256]{1,0:T(8,128)S(1)}, bf16[1792,256]{1,0:T(8,128)(2,1)S(1)}, bf16[1792,256]{1,0:T(8,128)(2,1)S(1)}) custom-call(bf16[1792,768]{1,0:T(8,128)(2,1)} %get-tuple-element.55.gt_ref.refs_0_, f32[1792,128]{1,0:T(8,128)S(1)} %get-tuple-element.57.vec_ref.refs_1_, ...), custom_call_target="tpu_custom_call" | custom-call | flops 1409286144 | bytes 12722176 | tf_op jit(solution)/shard_map/assemble_image/pallas_call | solution.py:66
  182.9 4.6 %collective-permute-start.27 = (f32[128,256]{1,0:T(8,128)S(1)}, f32[128,256]{1,0:T(8,128)S(1)}, u32[]{:S(2)}, u32[]{:S(2)}) collective-permute-start(f32[128,256]{1,0:T(8,128)S(1)} %coarse.4.a_ref.rest_3_), channel_id=1, source_target_pairs={{0,1},{1,2},{2,3},{3,4},{4,5},{5,6},{6,7},{7,8},{8,9},{9,10},{10,1... | collective-permute-start | bytes 393224 | tf_op jit(solution)/shard_map/ppermute | solution.py:483
  187.5 13.5 %schur_apply.2 = (f32[1792,256]{1,0:T(8,128)S(1)}, f32[768,256]{1,0:T(8,128)S(1)}) custom-call(bf16[1792,1792]{1,0:T(8,128)(2,1)} %get-tuple-element.63.sh_ref, bf16[1792,1792]{1,0:T(8,128)(2,1)} %get-tuple-element.64.sl_ref, bf16[768,1792]{1,0:T(8,128)(2,1)} %copy-done.3, bf16[1792,256]{1,0:T(8,128)(2,1)S(1)} %get-tuple-element.82.xh_ref, ...), custom_call_target="tpu_custom_call" | custom-call | flops 6341787648 | bytes 20054016 | tf_op jit(solution)/shard_map/schur_apply/pallas_call | solution.py:66
  203.3 5.5 %collective-permute-start.29 = (f32[384,256]{1,0:T(8,128)S(1)}, f32[384,256]{1,0:T(8,128)S(1)}, u32[]{:S(2)}, u32[]{:S(2)}) collective-permute-start(f32[384,256]{1,0:T(8,128)S(1)} %get-tuple-element.88), channel_id=1, source_target_pairs={{0,1},{1,2},{2,3},{3,4},{4,5},{5,6},{6,7},{7,8},{8,9},{9,10},{10,1... | collective-permute-start | bytes 1179656 | tf_op jit(solution)/shard_map/ppermute | solution.py:483
  210.2 6.0 %collective-permute-start.16 = (f32[8,256]{1,0:T(8,128)S(1)}, f32[8,256]{1,0:T(8,128)S(1)}, u32[]{:S(2)}, u32[]{:S(2)}) collective-permute-start(f32[8,256]{1,0:T(8,128)S(1)} %add.89), channel_id=1, source_target_pairs={{0,16},{8,24},{16,0},{24,8},{1,17},{9,25},{17,1},{25,9},{2,18},{10... | collective-permute-start | bytes 24584 | tf_op jit(solution)/shard_map/ppermute | solution.py:502
  217.8 12.5 %collective-permute-done.17 = f32[8,256]{1,0:T(8,128)S(1)} collective-permute-done((f32[8,256]{1,0:T(8,128)S(1)}, f32[8,256]{1,0:T(8,128)S(1)}, u32[]{:S(2)}, u32[]{:S(2)}) %collective-permute-start.17) | collective-permute-done | bytes 8224 | tf_op jit(solution)/shard_map/ppermute | solution.py:502
  234.2 4.3 %collective-permute-done.19 = f32[8,256]{1,0:T(8,128)S(1)} collective-permute-done((f32[8,256]{1,0:T(8,128)S(1)}, f32[8,256]{1,0:T(8,128)S(1)}, u32[]{:S(2)}, u32[]{:S(2)}) %collective-permute-start.19) | collective-permute-done | bytes 8224 | tf_op jit(solution)/shard_map/ppermute | solution.py:502
  238.5 7.8 %local_image.4 = (f32[1792,256]{1,0:T(8,128)}, f32[128,256]{1,0:T(8,128)S(1)}) custom-call(bf16[1792,384]{1,0:T(8,128)(2,1)S(1)} %get-tuple-element.69.qh_ref, bf16[1792,384]{1,0:T(8,128)(2,1)S(1)} %copy-done, f32[1792,256]{1,0:T(8,128)} %copy-done.7, f32[1792,128]{1,0:T(8,128)S(1)} %get-tuple-element.57.vec_ref.refs_1_, ...), custom_call_target="tpu_custom_call" | custom-call | flops 1409286144 | bytes 8781824 | tf_op jit(solution)/shard_map/local_image/pallas_call | solution.py:66
  249.6 8.3 %assemble_image.4 = (f32[1792,256]{1,0:T(8,128)}, f32[1792,256]{1,0:T(8,128)}, f32[8,256]{1,0:T(8,128)S(1)}, bf16[1792,256]{1,0:T(8,128)(2,1)S(1)}, bf16[1792,256]{1,0:T(8,128)(2,1)S(1)}) custom-call(bf16[1792,768]{1,0:T(8,128)(2,1)} %get-tuple-element.55.gt_ref.refs_0_, f32[1792,128]{1,0:T(8,128)S(1)} %get-tuple-element.57.vec_ref.refs_1_, ...), custom_call_target="tpu_custom_call" | custom-call | flops 1409286144 | bytes 16400384 | tf_op jit(solution)/shard_map/assemble_image/pallas_call | solution.py:66
  274.8 4.4 %collective-permute-done.40.rest_5_ = f32[128,256]{1,0:T(8,128)S(1)} collective-permute-done((f32[128,256]{1,0:T(8,128)S(1)}, f32[128,256]{1,0:T(8,128)S(1)}, u32[]{:S(2)}, u32[]{:S(2)}) %collective-permute-start.40) | collective-permute-done | bytes 131104 | tf_op jit(solution)/shard_map/ppermute | solution.py:515
  283.4 4.6 %collective-permute-start.43 = (f32[128,256]{1,0:T(8,128)S(1)}, f32[128,256]{1,0:T(8,128)S(1)}, u32[]{:S(2)}, u32[]{:S(2)}) collective-permute-start(f32[128,256]{1,0:T(8,128)S(1)} %coarse.5.rest_6_.a_ref), channel_id=1, source_target_pairs={{0,1},{1,2},{2,3},{3,4},{4,5},{5,6},{6,7},{7,8},{8,9},{9,10},{10,1... | collective-permute-start | bytes 393224 | tf_op jit(solution)/shard_map/ppermute | solution.py:483
  287.9 13.5 %schur_apply.3 = (f32[1792,256]{1,0:T(8,128)S(1)}, f32[768,256]{1,0:T(8,128)S(1)}) custom-call(bf16[1792,1792]{1,0:T(8,128)(2,1)} %get-tuple-element.63.sh_ref, bf16[1792,1792]{1,0:T(8,128)(2,1)} %get-tuple-element.64.sl_ref, bf16[768,1792]{1,0:T(8,128)(2,1)} %copy-done.3, bf16[1792,256]{1,0:T(8,128)(2,1)S(1)} %get-tuple-element.96.xh_ref, ...), custom_call_target="tpu_custom_call" | custom-call | flops 6341787648 | bytes 20054016 | tf_op jit(solution)/shard_map/schur_apply/pallas_call | solution.py:66
  303.8 3.8 %collective-permute-start.45 = (f32[384,256]{1,0:T(8,128)S(1)}, f32[384,256]{1,0:T(8,128)S(1)}, u32[]{:S(2)}, u32[]{:S(2)}) collective-permute-start(f32[384,256]{1,0:T(8,128)S(1)} %get-tuple-element.100), channel_id=1, source_target_pairs={{0,1},{1,2},{2,3},{3,4},{4,5},{5,6},{6,7},{7,8},{8,9},{9,10},{10,1... | collective-permute-start | bytes 1179656 | tf_op jit(solution)/shard_map/ppermute | solution.py:483
  308.9 6.9 %local_image.5.refs_3_ = f32[1792,256]{1,0:T(8,128)} custom-call(bf16[1792,384]{1,0:T(8,128)(2,1)S(1)} %get-tuple-element.69.qh_ref, bf16[1792,384]{1,0:T(8,128)(2,1)S(1)} %copy-done, f32[1792,256]{1,0:T(8,128)} %copy-done.4, f32[1792,128]{1,0:T(8,128)S(1)} %get-tuple-element.57.vec_ref.refs_1_, bf16[128,1792]{1,0:T(8,128)(2,1)S(1)} %get-tuple-element.72.h_ref.th_ref, ...), custom_call_target="tpu_custom_call" | custom-call | flops 1409286144 | bytes 8650752 | tf_op jit(solution)/shard_map/local_image/pallas_call | solution.py:66
  315.8 9.0 %directions.1 = (f32[1792,256]{1,0:T(8,128)}, f32[1792,256]{1,0:T(8,128)}, f32[1792,256]{1,0:T(8,128)}) custom-call(bf16[1792,384]{1,0:T(8,128)(2,1)S(1)} %copy-done.9, bf16[1792,384]{1,0:T(8,128)(2,1)S(1)} %copy-done.11, f32[1792,128]{1,0:T(8,128)S(1)} %get-tuple-element.62.w_ref.refs_2_, f32[8,256]{1,0:T(8,128)S(1)} %broadcast_in_dim.15.refs_7_.rest_0_.a0_ref, ...), custom_call_target="tpu_custom_call" | custom-call | flops 2113929216 | bytes 15876096 | tf_op jit(solution)/shard_map/directions/pallas_call | solution.py:66
  327.9 7.6 %assemble_image.5 = (f32[1792,256]{1,0:T(8,128)S(1)}, f32[8,256]{1,0:T(8,128)S(1)}) custom-call(bf16[1792,768]{1,0:T(8,128)(2,1)} %get-tuple-element.55.gt_ref.refs_0_, f32[1792,128]{1,0:T(8,128)S(1)} %get-tuple-element.57.vec_ref.refs_1_, f32[1792,128]{1,0:T(8,128)S(1)} %get-tuple-element.62.w_ref.refs_2_, f32[1792,256]{1,0:T(8,128)} %local_image.5.refs_3_, ...), custom_call_target="tpu_custom_call" | custom-call | flops 1409286144 | bytes 12730368 | tf_op jit(solution)/shard_map/assemble_image/pallas_call | solution.py:66
  341.0 3.6 %collective-permute-done.49 = f32[8,256]{1,0:T(8,128)S(1)} collective-permute-done((f32[8,256]{1,0:T(8,128)S(1)}, f32[8,256]{1,0:T(8,128)S(1)}, u32[]{:S(2)}, u32[]{:S(2)}) %collective-permute-start.49) | collective-permute-done | bytes 8224 | tf_op jit(solution)/shard_map/ppermute | solution.py:502
  348.4 4.5 %collective-permute-done.51 = f32[8,256]{1,0:T(8,128)S(1)} collective-permute-done((f32[8,256]{1,0:T(8,128)S(1)}, f32[8,256]{1,0:T(8,128)S(1)}, u32[]{:S(2)}, u32[]{:S(2)}) %collective-permute-start.51) | collective-permute-done | bytes 8224 | tf_op jit(solution)/shard_map/ppermute | solution.py:502
  (165 shorter events, 97.6 us)
Async XLA Ops:
  10.5 41.5 %collective-permute-start.2 = (f32[384,256]{1,0:T(8,128)}, f32[384,256]{1,0:T(8,128)S(1)}, u32[]{:S(2)}, u32[]{:S(2)}) collective-permute-start(f32[384,256]{1,0:T(8,128)} %get-tuple-element.65), channel_id=1, source_target_pairs={{0,1},{1,2},{2,3},{3,4},{4,5},{5,6},{6,7},{7,8},{8,9},{9,10},{10,1... | collective-permute-start | bytes 1179656 | tf_op jit(solution)/shard_map/ppermute | solution.py:483
  15.4 36.7 %collective-permute-start.3 = (f32[384,256]{1,0:T(8,128)}, f32[384,256]{1,0:T(8,128)}, u32[]{:S(2)}, u32[]{:S(2)}) collective-permute-start(f32[384,256]{1,0:T(8,128)} %get-tuple-element.66), channel_id=1, source_target_pairs={{1,0},{2,1},{3,2},{4,3},{5,4},{6,5},{7,6},{8,7},{9,8},{10,9},{11,1... | collective-permute-start | bytes 1179656 | tf_op jit(solution)/shard_map/ppermute | solution.py:483
  39.4 20.7 %collective-permute-start = (f32[408,128]{1,0:T(8,128)}, f32[408,128]{1,0:T(8,128)S(1)}, u32[]{:S(2)}, u32[]{:S(2)}) collective-permute-start(f32[408,128]{1,0:T(8,128)} %get-tuple-element.58), channel_id=1, source_target_pairs={{0,1},{1,2},{2,3},{3,4},{4,5},{5,6},{6,7},{7,8},{8,9},{9,10},{10,1... | collective-permute-start | bytes 626696 | tf_op jit(solution)/shard_map/ppermute | solution.py:483
  43.9 16.2 %collective-permute-start.1 = (f32[408,128]{1,0:T(8,128)}, f32[408,128]{1,0:T(8,128)}, u32[]{:S(2)}, u32[]{:S(2)}) collective-permute-start(f32[408,128]{1,0:T(8,128)} %get-tuple-element.59), channel_id=1, source_target_pairs={{1,0},{2,1},{3,2},{4,3},{5,4},{6,5},{7,6},{8,7},{9,8},{10,9},{11,1... | collective-permute-start | bytes 626696 | tf_op jit(solution)/shard_map/ppermute | solution.py:483
  53.4 21.5 %collective-permute-start.10 = (f32[128,256]{1,0:T(8,128)S(1)}, f32[128,256]{1,0:T(8,128)S(1)}, u32[]{:S(2)}, u32[]{:S(2)}) collective-permute-start(f32[128,256]{1,0:T(8,128)S(1)} %restrict_finish.3.rest_0_), channel_id=1, source_target_pairs={{0,7},{1,6},{2,5},{3,4},{4,3},{5,2},{6,1},{7,0},{8,15},{9,14},{10,... | collective-permute-start | bytes 393224 | tf_op jit(solution)/shard_map/ppermute | solution.py:515
  59.6 16.0 %collective-permute-start.9 = (f32[128,256]{1,0:T(8,128)S(1)}, f32[128,256]{1,0:T(8,128)S(1)}, u32[]{:S(2)}, u32[]{:S(2)}) collective-permute-start(f32[128,256]{1,0:T(8,128)S(1)} %restrict_finish.3.rest_0_), channel_id=1, source_target_pairs={{0,6},{1,7},{2,4},{3,5},{4,2},{5,3},{6,0},{7,1},{8,14},{9,15},{10,... | collective-permute-start | bytes 393224 | tf_op jit(solution)/shard_map/ppermute | solution.py:515
  69.8 15.2 %collective-permute-start.8 = (f32[128,256]{1,0:T(8,128)S(1)}, f32[128,256]{1,0:T(8,128)S(1)}, u32[]{:S(2)}, u32[]{:S(2)}) collective-permute-start(f32[128,256]{1,0:T(8,128)S(1)} %restrict_finish.3.rest_0_), channel_id=1, source_target_pairs={{0,5},{1,4},{2,7},{3,6},{4,1},{5,0},{6,3},{7,2},{8,13},{9,12},{10,... | collective-permute-start | bytes 393224 | tf_op jit(solution)/shard_map/ppermute | solution.py:515
  71.6 14.2 %collective-permute-start.7 = (f32[128,256]{1,0:T(8,128)S(1)}, f32[128,256]{1,0:T(8,128)S(1)}, u32[]{:S(2)}, u32[]{:S(2)}) collective-permute-start(f32[128,256]{1,0:T(8,128)S(1)} %restrict_finish.3.rest_0_), channel_id=1, source_target_pairs={{0,4},{1,5},{2,6},{3,7},{4,0},{5,1},{6,2},{7,3},{8,12},{9,13},{10,... | collective-permute-start | bytes 393224 | tf_op jit(solution)/shard_map/ppermute | solution.py:515
  75.0 13.1 %collective-permute-start.5 = (f32[128,256]{1,0:T(8,128)S(1)}, f32[128,256]{1,0:T(8,128)S(1)}, u32[]{:S(2)}, u32[]{:S(2)}) collective-permute-start(f32[128,256]{1,0:T(8,128)S(1)} %restrict_finish.3.rest_0_), channel_id=1, source_target_pairs={{0,2},{1,3},{2,0},{3,1},{4,6},{5,7},{6,4},{7,5},{8,10},{9,11},{10,... | collective-permute-start | bytes 393224 | tf_op jit(solution)/shard_map/ppermute | solution.py:515
  75.6 12.5 %collective-permute-start.4 = (f32[128,256]{1,0:T(8,128)S(1)}, f32[128,256]{1,0:T(8,128)S(1)}, u32[]{:S(2)}, u32[]{:S(2)}) collective-permute-start(f32[128,256]{1,0:T(8,128)S(1)} %restrict_finish.3.rest_0_), channel_id=1, source_target_pairs={{0,1},{1,0},{2,3},{3,2},{4,5},{5,4},{6,7},{7,6},{8,9},{9,8},{10,11... | collective-permute-start | bytes 393224 | tf_op jit(solution)/shard_map/ppermute | solution.py:515
  88.5 43.4 %collective-permute-start.12 = (f32[128,256]{1,0:T(8,128)S(1)}, f32[128,256]{1,0:T(8,128)S(1)}, u32[]{:S(2)}, u32[]{:S(2)}) collective-permute-start(f32[128,256]{1,0:T(8,128)S(1)} %coarse.3.a_ref.rest_0_), channel_id=1, source_target_pairs={{1,0},{2,1},{3,2},{4,3},{5,4},{6,5},{7,6},{8,7},{9,8},{10,9},{11,1... | collective-permute-start | bytes 393224 | tf_op jit(solution)/shard_map/ppermute | solution.py:483
  89.8 42.1 %collective-permute-start.11 = (f32[128,256]{1,0:T(8,128)S(1)}, f32[128,256]{1,0:T(8,128)S(1)}, u32[]{:S(2)}, u32[]{:S(2)}) collective-permute-start(f32[128,256]{1,0:T(8,128)S(1)} %coarse.3.a_ref.rest_0_), channel_id=1, source_target_pairs={{0,1},{1,2},{2,3},{3,4},{4,5},{5,6},{6,7},{7,8},{8,9},{9,10},{10,1... | collective-permute-start | bytes 393224 | tf_op jit(solution)/shard_map/ppermute | solution.py:483
  133.0 20.2 %collective-permute-start.13 = (f32[384,256]{1,0:T(8,128)S(1)}, f32[384,256]{1,0:T(8,128)S(1)}, u32[]{:S(2)}, u32[]{:S(2)}) collective-permute-start(f32[384,256]{1,0:T(8,128)S(1)} %get-tuple-element.78), channel_id=1, source_target_pairs={{0,1},{1,2},{2,3},{3,4},{4,5},{5,6},{6,7},{7,8},{8,9},{9,10},{10,1... | collective-permute-start | bytes 1179656 | tf_op jit(solution)/shard_map/ppermute | solution.py:483
  136.2 21.1 %collective-permute-start.14 = (f32[384,256]{1,0:T(8,128)S(1)}, f32[384,256]{1,0:T(8,128)S(1)}, u32[]{:S(2)}, u32[]{:S(2)}) collective-permute-start(f32[384,256]{1,0:T(8,128)S(1)} %get-tuple-element.79), channel_id=1, source_target_pairs={{1,0},{2,1},{3,2},{4,3},{5,4},{6,5},{7,6},{8,7},{9,8},{10,9},{11,1... | collective-permute-start | bytes 1179656 | tf_op jit(solution)/shard_map/ppermute | solution.py:483
  157.8 15.3 %collective-permute-start.25 = (f32[128,256]{1,0:T(8,128)S(1)}, f32[128,256]{1,0:T(8,128)S(1)}, u32[]{:S(2)}, u32[]{:S(2)}) collective-permute-start(f32[128,256]{1,0:T(8,128)S(1)} %restrict_finish.4.rest_0_.rest_1_), channel_id=1, source_target_pairs={{0,6},{1,7},{2,4},{3,5},{4,2},{5,3},{6,0},{7,1},{8,14},{9,15},{10,... | collective-permute-start | bytes 393224 | tf_op jit(solution)/shard_map/ppermute | solution.py:515
  160.5 20.6 %collective-permute-start.24 = (f32[128,256]{1,0:T(8,128)S(1)}, f32[128,256]{1,0:T(8,128)S(1)}, u32[]{:S(2)}, u32[]{:S(2)}) collective-permute-start(f32[128,256]{1,0:T(8,128)S(1)} %restrict_finish.4.rest_0_.rest_1_), channel_id=1, source_target_pairs={{0,5},{1,4},{2,7},{3,6},{4,1},{5,0},{6,3},{7,2},{8,13},{9,12},{10,... | collective-permute-start | bytes 393224 | tf_op jit(solution)/shard_map/ppermute | solution.py:515
  160.5 20.6 %collective-permute-start.23 = (f32[128,256]{1,0:T(8,128)S(1)}, f32[128,256]{1,0:T(8,128)S(1)}, u32[]{:S(2)}, u32[]{:S(2)}) collective-permute-start(f32[128,256]{1,0:T(8,128)S(1)} %restrict_finish.4.rest_0_.rest_1_), channel_id=1, source_target_pairs={{0,4},{1,5},{2,6},{3,7},{4,0},{5,1},{6,2},{7,3},{8,12},{9,13},{10,... | collective-permute-start | bytes 393224 | tf_op jit(solution)/shard_map/ppermute | solution.py:515
  165.4 15.8 %collective-permute-start.22 = (f32[128,256]{1,0:T(8,128)S(1)}, f32[128,256]{1,0:T(8,128)S(1)}, u32[]{:S(2)}, u32[]{:S(2)}) collective-permute-start(f32[128,256]{1,0:T(8,128)S(1)} %restrict_finish.4.rest_0_.rest_1_), channel_id=1, source_target_pairs={{0,3},{1,2},{2,1},{3,0},{4,7},{5,6},{6,5},{7,4},{8,11},{9,10},{10,... | collective-permute-start | bytes 393224 | tf_op jit(solution)/shard_map/ppermute | solution.py:515
  166.8 14.4 %collective-permute-start.21 = (f32[128,256]{1,0:T(8,128)S(1)}, f32[128,256]{1,0:T(8,128)S(1)}, u32[]{:S(2)}, u32[]{:S(2)}) collective-permute-start(f32[128,256]{1,0:T(8,128)S(1)} %restrict_finish.4.rest_0_.rest_1_), channel_id=1, source_target_pairs={{0,2},{1,3},{2,0},{3,1},{4,6},{5,7},{6,4},{7,5},{8,10},{9,11},{10,... | collective-permute-start | bytes 393224 | tf_op jit(solution)/shard_map/ppermute | solution.py:515
  181.2 29.0 %collective-permute-start.15 = (f32[8,256]{1,0:T(8,128)S(1)}, f32[8,256]{1,0:T(8,128)S(1)}, u32[]{:S(2)}, u32[]{:S(2)}) collective-permute-start(f32[8,256]{1,0:T(8,128)S(1)} %get-tuple-element.81), channel_id=1, source_target_pairs={{0,8},{8,0},{16,24},{24,16},{1,9},{9,1},{17,25},{25,17},{2,10},{10... | collective-permute-start | bytes 24584 | tf_op jit(solution)/shard_map/ppermute | solution.py:502
  181.6 20.6 %collective-permute-start.28 = (f32[128,256]{1,0:T(8,128)S(1)}, f32[128,256]{1,0:T(8,128)S(1)}, u32[]{:S(2)}, u32[]{:S(2)}) collective-permute-start(f32[128,256]{1,0:T(8,128)S(1)} %coarse.4.a_ref.rest_3_), channel_id=1, source_target_pairs={{1,0},{2,1},{3,2},{4,3},{5,4},{6,5},{7,6},{8,7},{9,8},{10,9},{11,1... | collective-permute-start | bytes 393224 | tf_op jit(solution)/shard_map/ppermute | solution.py:483
  182.9 19.3 %collective-permute-start.27 = (f32[128,256]{1,0:T(8,128)S(1)}, f32[128,256]{1,0:T(8,128)S(1)}, u32[]{:S(2)}, u32[]{:S(2)}) collective-permute-start(f32[128,256]{1,0:T(8,128)S(1)} %coarse.4.a_ref.rest_3_), channel_id=1, source_target_pairs={{0,1},{1,2},{2,3},{3,4},{4,5},{5,6},{6,7},{7,8},{8,9},{9,10},{10,1... | collective-permute-start | bytes 393224 | tf_op jit(solution)/shard_map/ppermute | solution.py:483
  203.3 43.0 %collective-permute-start.29 = (f32[384,256]{1,0:T(8,128)S(1)}, f32[384,256]{1,0:T(8,128)S(1)}, u32[]{:S(2)}, u32[]{:S(2)}) collective-permute-start(f32[384,256]{1,0:T(8,128)S(1)} %get-tuple-element.88), channel_id=1, source_target_pairs={{0,1},{1,2},{2,3},{3,4},{4,5},{5,6},{6,7},{7,8},{8,9},{9,10},{10,1... | collective-permute-start | bytes 1179656 | tf_op jit(solution)/shard_map/ppermute | solution.py:483
  208.9 37.5 %collective-permute-start.30 = (f32[384,256]{1,0:T(8,128)S(1)}, f32[384,256]{1,0:T(8,128)S(1)}, u32[]{:S(2)}, u32[]{:S(2)}) collective-permute-start(f32[384,256]{1,0:T(8,128)S(1)} %get-tuple-element.89), channel_id=1, source_target_pairs={{1,0},{2,1},{3,2},{4,3},{5,4},{6,5},{7,6},{8,7},{9,8},{10,9},{11,1... | collective-permute-start | bytes 1179656 | tf_op jit(solution)/shard_map/ppermute | solution.py:483
  217.8 12.5 %collective-permute-start.17 = (f32[8,256]{1,0:T(8,128)S(1)}, f32[8,256]{1,0:T(8,128)S(1)}, u32[]{:S(2)}, u32[]{:S(2)}) collective-permute-start(f32[8,256]{1,0:T(8,128)S(1)} %add.90), channel_id=1, source_target_pairs={{0,1},{1,0},{2,3},{3,2},{4,5},{5,4},{6,7},{7,6},{8,9},{9,8},{10,11... | collective-permute-start | bytes 24584 | tf_op jit(solution)/shard_map/ppermute | solution.py:502
  246.8 26.0 %collective-permute-start.42 = (f32[128,256]{1,0:T(8,128)S(1)}, f32[128,256]{1,0:T(8,128)S(1)}, u32[]{:S(2)}, u32[]{:S(2)}) collective-permute-start(f32[128,256]{1,0:T(8,128)S(1)} %restrict_finish.5.rest_0_), channel_id=1, source_target_pairs={{0,7},{1,6},{2,5},{3,4},{4,3},{5,2},{6,1},{7,0},{8,15},{9,14},{10,... | collective-permute-start | bytes 393224 | tf_op jit(solution)/shard_map/ppermute | solution.py:515
  247.2 26.8 %collective-permute-start.41 = (f32[128,256]{1,0:T(8,128)S(1)}, f32[128,256]{1,0:T(8,128)S(1)}, u32[]{:S(2)}, u32[]{:S(2)}) collective-permute-start(f32[128,256]{1,0:T(8,128)S(1)} %restrict_finish.5.rest_0_), channel_id=1, source_target_pairs={{0,6},{1,7},{2,4},{3,5},{4,2},{5,3},{6,0},{7,1},{8,14},{9,15},{10,... | collective-permute-start | bytes 393224 | tf_op jit(solution)/shard_map/ppermute | solution.py:515
  279.3 23.4 %collective-permute-start.35 = (f32[8,256]{1,0:T(8,128)S(1)}, f32[8,256]{1,0:T(8,128)S(1)}, u32[]{:S(2)}, u32[]{:S(2)}) collective-permute-start(f32[8,256]{1,0:T(8,128)S(1)} %add.98), channel_id=1, source_target_pairs={{0,4},{1,5},{2,6},{3,7},{4,0},{5,1},{6,2},{7,3},{8,12},{9,13},{10,... | collective-permute-start | bytes 24584 | tf_op jit(solution)/shard_map/ppermute | solution.py:502
  282.1 20.6 %collective-permute-start.44 = (f32[128,256]{1,0:T(8,128)S(1)}, f32[128,256]{1,0:T(8,128)S(1)}, u32[]{:S(2)}, u32[]{:S(2)}) collective-permute-start(f32[128,256]{1,0:T(8,128)S(1)} %coarse.5.rest_6_.a_ref), channel_id=1, source_target_pairs={{1,0},{2,1},{3,2},{4,3},{5,4},{6,5},{7,6},{8,7},{9,8},{10,9},{11,1... | collective-permute-start | bytes 393224 | tf_op jit(solution)/shard_map/ppermute | solution.py:483
  283.4 19.3 %collective-permute-start.43 = (f32[128,256]{1,0:T(8,128)S(1)}, f32[128,256]{1,0:T(8,128)S(1)}, u32[]{:S(2)}, u32[]{:S(2)}) collective-permute-start(f32[128,256]{1,0:T(8,128)S(1)} %coarse.5.rest_6_.a_ref), channel_id=1, source_target_pairs={{0,1},{1,2},{2,3},{3,4},{4,5},{5,6},{6,7},{7,8},{8,9},{9,10},{10,1... | collective-permute-start | bytes 393224 | tf_op jit(solution)/shard_map/ppermute | solution.py:483
  303.8 21.1 %collective-permute-start.45 = (f32[384,256]{1,0:T(8,128)S(1)}, f32[384,256]{1,0:T(8,128)S(1)}, u32[]{:S(2)}, u32[]{:S(2)}) collective-permute-start(f32[384,256]{1,0:T(8,128)S(1)} %get-tuple-element.100), channel_id=1, source_target_pairs={{0,1},{1,2},{2,3},{3,4},{4,5},{5,6},{6,7},{7,8},{8,9},{9,10},{10,1... | collective-permute-start | bytes 1179656 | tf_op jit(solution)/shard_map/ppermute | solution.py:483
  307.6 20.3 %collective-permute-start.46 = (f32[384,256]{1,0:T(8,128)S(1)}, f32[384,256]{1,0:T(8,128)S(1)}, u32[]{:S(2)}, u32[]{:S(2)}) collective-permute-start(f32[384,256]{1,0:T(8,128)S(1)} %get-tuple-element.101), channel_id=1, source_target_pairs={{1,0},{2,1},{3,2},{4,3},{5,4},{6,5},{7,6},{8,7},{9,8},{10,9},{11,1... | collective-permute-start | bytes 1179656 | tf_op jit(solution)/shard_map/ppermute | solution.py:483
  (38 other events, 258.5 us)

commit v2 on v0

v2 whole, which is shorter than its diff:
```python
import jax
import jax.numpy as jnp
from jax import lax
from jax.experimental import pallas as pl
from jax.experimental.pallas import tpu as pltpu
from jax.sharding import PartitionSpec as P

BOTH = ("cluster", "sub")
F32 = jnp.float32
BF16 = jnp.bfloat16
ITERS = 3
INTERPRET = False
SUMS = 8


def split2(x):
    hi = x.astype(BF16)
    return hi, (x - hi.astype(F32)).astype(BF16)


def split3(x):
    hi = x.astype(BF16)
    rest = x - hi.astype(F32)
    mid = rest.astype(BF16)
    return hi, mid, (rest - mid.astype(F32)).astype(BF16)


def mm(a, b):
    return jnp.dot(a, b, preferred_element_type=F32)


def mm3(a, b):
    return mm(jnp.concatenate([a[0], a[0]], 1), jnp.concatenate([b[0], b[1]], 0)) + mm(a[1], b[0])


def pick(onehot, parts):
    return mm(jnp.concatenate([onehot] * len(parts), 1), jnp.concatenate(parts, 0))


def shape(*dims, dtype=F32):
    return jax.ShapeDtypeStruct(dims, dtype)


def call(body, name, ins, outs, flops, scalars=(), scratch=(), mb=8):
    moved = sum(a.size * a.dtype.itemsize for a in (*ins, *outs))
    found = pl.pallas_call(
        body,
        name=name,
        in_specs=[pl.BlockSpec(memory_space=pltpu.SMEM)] * len(scalars)
        + [pl.BlockSpec(memory_space=pltpu.VMEM)] * len(ins),
        out_specs=[pl.BlockSpec(memory_space=pltpu.VMEM)] * len(outs),
        out_shape=list(outs),
        scratch_shapes=list(scratch),
        cost_estimate=pl.CostEstimate(flops=int(flops), bytes_accessed=int(moved), transcendentals=0),
        compiler_params=pltpu.CompilerParams(vmem_limit_bytes=mb * 1024 * 1024),
        interpret=INTERPRET,
    )(*scalars, *ins)
    return found


def over_blocks(order, step, carry=0, unroll=False):
    b = block_of(order)
    if unroll:
        for k in range(0, order, b):
            carry = step(pl.ds(k, b), k, carry)
        return carry

    def one(k, carry):
        at = pl.multiple_of(k * b, b)
        return step(pl.ds(at, b), at, carry)

    return lax.fori_loop(0, order // b, one, carry)


def block_of(order):
    return 256 if order % 256 == 0 else order


def gather_rows(source, index, outs, half, order):
    group = 8 if half % 8 == 0 else 1
    for side, out in enumerate(outs):

        def step(j, _, side=side, out=out):
            for u in range(group):
                slot = j * group + u
                row = jnp.minimum(index(side, slot), order - 1)
                out[pl.ds(slot, 1), :] = source[pl.ds(row, 1), :]
            return 0

        lax.fori_loop(0, half // group, step, 0)


def sides(me_ref, left_ref, right_ref):
    even = lax.rem(me_ref[0], 2) == 0

    def index(side, slot):
        a, c = (right_ref, left_ref) if side == 0 else (left_ref, right_ref)
        return jnp.where(even, a[0, slot], c[0, slot])

    return index


def row_sides(me_ref, left_ref, right_ref):
    even = lax.rem(me_ref[0], 2) == 0
    left, right = left_ref[...], right_ref[...]
    return jnp.where(even, right, left), jnp.where(even, left, right)


def used_slots(out, count):
    slot = lax.broadcasted_iota(jnp.int32, out.shape, 0)
    out[...] = jnp.where(slot < count, out[...], 0.0)


def used_count(row, order):
    return jnp.sum(jnp.where(row < order, 1, 0))


def gather_load(me, left, right, load):
    half = left.shape[1]
    order, k = load.shape

    def body(me_ref, ls_ref, rs_ref, lv_ref, rv_ref, load_ref, x_ref, d_ref):
        gather_rows(load_ref, sides(me_ref, ls_ref, rs_ref), (x_ref, d_ref), half, order)
        rows = row_sides(me_ref, lv_ref, rv_ref)
        used_slots(x_ref, used_count(rows[0], order))
        used_slots(d_ref, used_count(rows[1], order))

    return call(body, "gather_load", [left, right, load], [shape(half, k)] * 2, 0, [me, left, right])


def halves(me, inverse):
    nm, co = inverse.shape

    def body(me_ref, c_ref, same_ref, other_ref):
        par = lax.rem(me_ref[0], 2)
        for j in range(co // nm // 2):
            to = slice(j * nm, (j + 1) * nm)
            same_ref[:, to] = c_ref[:, pl.ds(pl.multiple_of((2 * j + par) * nm, nm), nm)]
            other_ref[:, to] = c_ref[:, pl.ds(pl.multiple_of((2 * j + 1 - par) * nm, nm), nm)]

    return call(body, "halves", [inverse], [shape(nm, co // 2)] * 2, 0, [me])


def prepare(me, live_rows, live_modes, left, right, schur, modes):
    order, nm = modes.shape
    half = left.shape[1]
    two = 2 * half
    pieces = half // nm
    tall = half + 8 * pieces
    b = block_of(order)

    def body(me_ref, rows_ref, count_ref, l_ref, r_ref, s_ref, modes_ref,
             gt_ref, ph_ref, pl_ref, pth_ref, ptl_ref, vec_ref, x_ref, d_ref, tsh_ref, tsl_ref):
        index = jnp.concatenate(row_sides(me_ref, l_ref, r_ref), axis=1)
        mask = jnp.where(lax.broadcasted_iota(jnp.int32, (1, nm), 1) < count_ref[0], 1.0, 0.0)
        eye = lax.broadcasted_iota(jnp.int32, (b, b), 0) == lax.broadcasted_iota(jnp.int32, (b, b), 1)
        lane = lax.broadcasted_iota(jnp.int32, (b, 128), 1)

        def step(r, start, carry):
            shared, weights = carry
            row_id = lax.broadcasted_iota(jnp.int32, (b, two), 0) + start
            found = jnp.where(index == row_id, 1.0, 0.0)
            gt = found.astype(BF16)
            gt_ref[r] = gt
            live = jnp.where(lax.broadcasted_iota(jnp.int32, (b, 1), 0) + start < rows_ref[0], 1.0, 0.0)
            share = live / (1.0 + jnp.sum(found, axis=1, keepdims=True))
            diag = jnp.sum(jnp.where(eye, s_ref[r, r], 0.0), axis=1, keepdims=True)
            sd = share / diag
            weights = weights + jnp.sum(found * sd, axis=0, keepdims=True)
            vec_ref[r] = jnp.where(lane == 0, live, sd)
            phi = share * (modes_ref[r] * mask)
            ph_ref[r], pl_ref[r] = split2(phi)
            parts = split3(phi.T)
            pth_ref[:, r], ptl_ref[:, r] = split2(phi.T)
            return shared + mm(jnp.concatenate(parts, 1), jnp.concatenate([gt] * 3, 0)), weights

        shared, weights = over_blocks(
            order, step, (jnp.zeros((nm, two), F32), jnp.zeros((1, two), F32))
        )
        tsh_ref[...], tsl_ref[...] = split2(shared)
        back = shared.T
        for i, ref in enumerate((x_ref, d_ref)):
            ref[:half] = back[i * half:(i + 1) * half]
            for t in range(pieces):
                at = i * half + t * nm
                ref[half + 8 * t:half + 8 * t + 8] = jnp.broadcast_to(weights[:, at:at + nm], (8, nm))

    half_type = dict(dtype=BF16)
    return call(
        body, "prepare", [left, right, schur, modes],
        [shape(order, two, **half_type), shape(order, nm, **half_type), shape(order, nm, **half_type),
         shape(nm, order, **half_type), shape(nm, order, **half_type), shape(order, 128),
         shape(tall, nm), shape(tall, nm), shape(nm, two, **half_type), shape(nm, two, **half_type)],
        6 * two * order * nm, [me, live_rows, live_modes], mb=10,
    )


def start(schur, phi, phi_t, load):
    order, nm = phi[0].shape
    k = load.shape[1]

    def body(s_ref, h_ref, l_ref, th_ref, tl_ref, f_ref, q_ref, m_ref):
        m_ref[...] = mm3((th_ref[...], tl_ref[...]), split2(f_ref[...]))

        def step(r, _, carry):
            q_ref[r] = mm3(split2(s_ref[r]), (h_ref[...], l_ref[...]))
            return carry

        over_blocks(order, step)

    return call(
        body, "start", [schur, *phi, *phi_t, load], [shape(order, nm), shape(nm, k)],
        6 * order * order * nm + 6 * nm * order * k, mb=12,
    )


def extend(onehot_t, vec, load, recv, phi_recv):
    order, two = onehot_t.shape
    half = two // 2
    k = load.shape[1]
    nm = phi_recv[0].shape[1]
    pieces = half // nm

    def body(gt_ref, vec_ref, f_ref, rx_ref, rd_ref, px_ref, pd_ref, r_ref, w_ref, xh_ref, xl_ref, nh_ref, nl_ref):
        field = [jnp.concatenate(p, 0) for p in zip(split3(rx_ref[...]), split3(rd_ref[...]))]
        weights = jnp.concatenate(
            [ref[half + 8 * t:half + 8 * t + 1] for ref in (px_ref, pd_ref) for t in range(pieces)], axis=1
        )
        modes = [jnp.concatenate(split2(ref[:half]), 0) for ref in (px_ref, pd_ref)]

        def step(r, _, carry):
            gt = gt_ref[r]
            w = vec_ref[r, 1:2] + jnp.sum(gt.astype(F32) * weights, axis=1, keepdims=True)
            w_ref[r] = jnp.broadcast_to(w, (w.shape[0], 128))
            rhs = vec_ref[r, 0:1] * f_ref[r] + pick(gt, field)
            r_ref[r] = rhs
            xh_ref[r], xl_ref[r] = split2(w * rhs)
            for i in range(2):
                side = gt[:, i * half:(i + 1) * half]
                part = mm(jnp.concatenate([side, side], 1), modes[i])
                nh_ref[r, i * nm:(i + 1) * nm], nl_ref[r, i * nm:(i + 1) * nm] = split2(part)
            return carry

        over_blocks(order, step)

    return call(
        body, "extend", [onehot_t, vec, load, *recv, *phi_recv],
        [shape(order, k), shape(order, 128)] + [shape(order, k, dtype=BF16)] * 2
        + [shape(order, 2 * nm, dtype=BF16)] * 2,
        2 * order * two * (3 * k + 2 * nm), mb=12,
    )


def schur_first(me, left, right, schur, x, phi_n, q_own):
    order, k = x[0].shape
    half = left.shape[1]
    nm = q_own.shape[1]
    n = 3 * nm

    def body(me_ref, ls_ref, rs_ref, s_ref, xh_ref, xl_ref, nh_ref, nl_ref, qo_ref, y_ref, ys_ref, q_ref, qs_ref):
        rhs = (jnp.concatenate([xh_ref[...], nh_ref[...]], 1), jnp.concatenate([xl_ref[...], nl_ref[...]], 1))

        def block(r, _, carry):
            both = mm3(split2(s_ref[r]), rhs)
            y_ref[r] = both[:, :k]
            q_ref[r, nm:] = both[:, k:]
            q_ref[r, :nm] = qo_ref[r]
            return carry

        over_blocks(order, block, unroll=True)
        index = sides(me_ref, ls_ref, rs_ref)
        group = 8 if half % 8 == 0 else 1
        for side in range(2):

            def step(j, _, side=side):
                for u in range(group):
                    slot = j * group + u
                    row = jnp.minimum(index(side, slot), order - 1)
                    ys_ref[pl.ds(side * half + slot, 1), :] = y_ref[pl.ds(row, 1), :]
                    qs_ref[pl.ds(side * half + slot, 1), :] = q_ref[pl.ds(row, 1), :]
                return 0

            lax.fori_loop(0, half // group, step, 0)

    return call(
        body, "schur_first", [schur, *x, *phi_n, q_own],
        [shape(order, k), shape(2 * half, k), shape(order, n), shape(2 * half, n)],
        6 * order * order * (k + 2 * nm), [me, left, right], mb=14,
    )


def schur_apply(me, left, right, schur, x):
    order, k = x[0].shape
    half = left.shape[1]

    def body(me_ref, ls_ref, rs_ref, s_ref, xh_ref, xl_ref, y_ref, ys_ref):
        x = (xh_ref[...], xl_ref[...])

        def block(r, _, carry):
            y_ref[r] = mm3(split2(s_ref[r]), x)
            return carry

        over_blocks(order, block, unroll=True)
        gather_rows(y_ref, sides(me_ref, ls_ref, rs_ref), (ys_ref.at[:half], ys_ref.at[half:]), half, order)

    return call(
        body, "schur_apply", [schur, *x], [shape(order, k), shape(2 * half, k)],
        6 * order * order * k, [me, left, right], mb=12,
    )


def coarse(me, inverses, modal):
    nm, co = inverses[0].shape
    rows, k = modal[0].shape
    n = len(modal)
    ordered = direct(2 * n)

    def body(me_ref, own_ref, x_ref, d_ref, z_ref, *rest):
        send_ref, keep_ref, xh, xl = rest[n:]
        pos = me_ref[0] // 2
        sums = jnp.zeros((SUMS, k), F32)
        for d in range(n):
            at = pl.ds(pl.multiple_of(((pos ^ d) if ordered else d) * nm, nm), nm)
            xh[at], xl[at] = split2(rest[d][:nm])
            sums = sums + rest[d][nm:]
        a = split2(jnp.concatenate([own_ref[...], x_ref[...], d_ref[...], z_ref[...]], 0))
        part = mm3(a, (xh[...], xl[...]))
        keep_ref[:3 * nm] = part[:3 * nm]
        keep_ref[3 * nm:] = sums
        send_ref[:nm] = part[nm:2 * nm]
        send_ref[nm:2 * nm] = part[:nm]
        send_ref[2 * nm:3 * nm] = part[3 * nm:]
        send_ref[3 * nm:] = sums

    return call(
        body, "coarse", [*inverses, *modal], [shape(3 * nm + SUMS, k)] * 2,
        24 * nm * co * k, [me], scratch=[pltpu.VMEM((co, k), BF16)] * 2, mb=12,
    )


def shared_image(me, last_sub, left, right, order, q_shared, y_shared, keep, recv, edge):
    two, n = q_shared.shape
    half = two // 2
    nm, k = edge.shape

    def body(me_ref, lv_ref, rv_ref, q_ref, y_ref, keep_ref, recv_ref, edge_ref, x_ref, d_ref, st_ref):
        rows = row_sides(me_ref, lv_ref, rv_ref)
        at_edge = jnp.logical_or(me_ref[0] == 0, me_ref[0] == last_sub)
        total = keep_ref[:3 * nm] + recv_ref[:3 * nm]
        st_ref[:2 * nm] = total[:2 * nm]
        st_ref[2 * nm:] = jnp.where(at_edge, edge_ref[...], total[2 * nm:])
        c = split2(st_ref[...])
        for i, ref in enumerate((x_ref, d_ref)):
            at = slice(i * half, (i + 1) * half)
            found = y_ref[at] + mm3(split2(q_ref[at]), c)
            slot = lax.broadcasted_iota(jnp.int32, (half, k), 0)
            ref[...] = jnp.where(slot < used_count(rows[i], order), found, 0.0)

    return call(
        body, "shared_image", [left, right, q_shared, y_shared, keep, recv, edge],
        [shape(half, k)] * 2 + [shape(3 * nm, k)], 6 * two * n * k, [me], mb=10,
    )


def local_image(q, y, vec, phi_t, stack, chain, restrict):
    order, n = q.shape
    k = stack.shape[1]
    nm = phi_t[0].shape[0]
    chained = len(chain) == 4

    def body(q_ref, y_ref, vec_ref, th_ref, tl_ref, st_ref, *refs):
        ins, outs = refs[:len(chain)], list(refs[len(chain):])
        c = split2(st_ref[...])
        p_ref = outs.pop(0)
        r_ref = outs.pop(0) if chained else None

        def step(at, _, carry):
            num, den, modal = carry
            p = vec_ref[at, 0:1] * (y_ref[at] + mm3(split2(q_ref[at]), c))
            r = ins[0][at]
            if chained:
                scale = ins[1][0:1]
                p = ins[2][at] - scale * p
                r = r - scale * ins[3][at]
                r_ref[at] = r
            p_ref[at] = p
            num = num + jnp.sum(r * p, axis=0, keepdims=True)
            den = den + jnp.sum(p * p, axis=0, keepdims=True)
            if restrict:
                modal = modal + mm3((th_ref[:, at], tl_ref[:, at]), split2(p))
            return num, den, modal

        zero = jnp.zeros((1, k), F32)
        num, den, modal = over_blocks(order, step, (zero, zero, jnp.zeros((nm, k), F32)))
        row = lax.broadcasted_iota(jnp.int32, (SUMS, k), 0)
        m_ref = outs.pop(0)
        m_ref[:nm] = modal
        m_ref[nm:] = jnp.where(row == 0, num, jnp.where(row == 1, den, 0.0))

    outs = [shape(order, k)] + ([shape(order, k)] if chained else []) + [shape(nm + SUMS, k)]
    return call(
        body, "local_image", [q, y, vec, *phi_t, stack, *chain], outs,
        6 * order * n * k + 6 * nm * order * k, mb=12,
    )


def finish(phi_ts, own, recv, sent=(), chain=()):
    nm, two = phi_ts[0].shape
    half = two // 2
    k = own.shape[1]
    plain = len(sent) == 0

    def body(h_ref, l_ref, m_ref, *refs):
        ins, outs = refs[:2 + len(sent) + len(chain)], refs[2 + len(sent) + len(chain):]
        got = jnp.concatenate([ins[0][...], ins[1][...]], 0)
        cross = jnp.zeros((1, k), F32)
        if not plain:
            put = jnp.concatenate([ins[2][...], ins[3][...]], 0)
            if chain:
                scale = ins[4][0:1]
                got = ins[5][...] - scale * got
                put = ins[6][...] - scale * put
            outs[1][...] = got
            outs[2][...] = put
            cross = jnp.sum(got * put, axis=0, keepdims=True)
        outs[0][:nm] = m_ref[:nm] + mm3((h_ref[...], l_ref[...]), split2(got))
        row = lax.broadcasted_iota(jnp.int32, (SUMS, k), 0)
        base = m_ref[nm:] if not plain else jnp.zeros((SUMS, k), F32)
        outs[0][nm:] = base + jnp.where(row == 1, cross, 0.0)

    outs = [shape(nm + SUMS, k)] + ([] if plain else [shape(two, k)] * 2)
    return call(body, "finish", [*phi_ts, own, *recv, *sent, *chain], outs, 6 * nm * two * k, mb=10)


def assemble(onehot_t, p, got, w=None):
    order, two = onehot_t.shape
    k = p.shape[1]

    def body(gt_ref, p_ref, g_ref, *refs):
        parts = jnp.concatenate(split2(g_ref[...]), 0)

        def step(r, _, carry):
            gt = gt_ref[r]
            new = p_ref[r] + mm(jnp.concatenate([gt, gt], 1), parts)
            if w is None:
                refs[0][r] = new
            else:
                w_ref, i_ref, xh_ref, xl_ref = refs
                i_ref[r] = new
                xh_ref[r], xl_ref[r] = split2(w_ref[r, 0:1] * new)
            return carry

        over_blocks(order, step)

    ins = [onehot_t, p, got] + ([] if w is None else [w])
    outs = [shape(order, k)] + ([] if w is None else [shape(order, k, dtype=BF16)] * 2)
    return call(body, "assemble", ins, outs, 4 * order * two * k, mb=10)


def directions(phi, phi_n, w, scales, resids, stacks):
    order, nm = phi[0].shape
    n, k = stacks[0].shape

    def body(h_ref, l_ref, nh_ref, nl_ref, w_ref, a0_ref, a1_ref, r0_ref, r1_ref, r2_ref,
             c0_ref, e0_ref, e1_ref, sol_ref, dir_ref):
        s0, s1 = a0_ref[0:1], a1_ref[0:1]
        c0 = c0_ref[...]
        c1 = c0 - s0 * e0_ref[...]
        first = s0 * c0 + s1 * c1
        c = split2(jnp.concatenate([first, c1 - s1 * e1_ref[...]], 1))

        def step(r, _, carry):
            p = (jnp.concatenate([h_ref[r], nh_ref[r]], 1), jnp.concatenate([l_ref[r], nl_ref[r]], 1))
            both = mm3(p, c)
            wc = w_ref[r, 0:1]
            sol_ref[r] = both[:, :k] + wc * (s0 * r0_ref[r] + s1 * r1_ref[r])
            dir_ref[r] = both[:, k:] + wc * r2_ref[r]
            return carry

        over_blocks(order, step)

    return call(
        body, "directions", [*phi, *phi_n, w, *scales, *resids, *stacks], [shape(order, k)] * 2,
        12 * order * n * k, mb=12,
    )


def swap_x(value):
    n = lax.axis_size("sub")
    return lax.ppermute(value, "sub", [(i, i ^ 1) for i in range(n)])


def swap_d(value):
    n = lax.axis_size(BOTH)
    pairs = [(i, i + 1) for i in range(1, n - 1, 2)]
    return lax.ppermute(value, BOTH, pairs + [(b, a) for a, b in pairs])


def coarse_rows(me, inverse):
    n = lax.axis_size("sub")
    same, other = halves(me, inverse)
    ring = [((i + 1) % n, (i + 2) % n) for i in range(0, n, 2)]
    at_d = lax.ppermute(other, "sub", ring + [(b, a) for a, b in ring])
    at_x = swap_x(other)
    at_z = lax.ppermute(same, "sub", [(i, (i - 2) % n if i % 2 == 0 else (i + 2) % n) for i in range(n)])
    return same, at_x, at_d, at_z


def direct(n):
    return n & (n - 1) == 0 and n <= 8


def parity_blocks(modal):
    n = lax.axis_size("sub")
    if not direct(n):
        groups = [list(range(p, n, 2)) for p in range(2)]
        every = lax.all_gather(modal, "sub", axis=0, axis_index_groups=groups)
        return [every[d] for d in range(n // 2)]
    return [modal] + [
        lax.ppermute(modal, "sub", [(i, i ^ (2 * d)) for i in range(n)]) for d in range(1, n // 2)
    ]


def over_axis(value, axis):
    n = lax.axis_size(axis)
    if n & (n - 1):
        return lax.psum(value, axis)
    step = 1
    while step < n:
        value = value + lax.ppermute(value, axis, [(i, i ^ step) for i in range(n)])
        step *= 2
    return value


def edge_blocks(block):
    n, m = lax.axis_size("sub"), lax.axis_size("cluster")
    up = [(n * c, n * (c + 1)) for c in range(m - 1)]
    down = [(n * (c + 1) + n - 1, n * c + n - 1) for c in range(m - 1)]
    return lax.ppermute(block, BOTH, up + down)


def scale_of(sums):
    value = sums[0:1] / (sums[1:2] + 1e-06)
    return jnp.broadcast_to(value, (8, value.shape[1]))


def local(load, schur, modes, coarse_inverse, interface_rows, mode_count, left_rows, right_rows):
    nm = modes.shape[1]
    n_sub = lax.axis_size("sub")
    me = lax.axis_index("sub").astype(jnp.int32).reshape(1)

    to_x, to_d = gather_load(me, left_rows, right_rows, load)
    recv = swap_x(to_x), swap_d(to_d)
    onehot_t, p_hi, p_lo, pt_hi, pt_lo, vec, phi_x, phi_d, ts_hi, ts_lo = prepare(
        me, interface_rows, mode_count, left_rows, right_rows, schur, modes
    )
    phi, phi_t, phi_ts = (p_hi, p_lo), (pt_hi, pt_lo), (ts_hi, ts_lo)
    phi_recv = swap_x(phi_x), swap_d(phi_d)
    inverses = coarse_rows(me, coarse_inverse)
    q_own, own = start(schur, phi, phi_t, load)
    own = jnp.concatenate([own, jnp.zeros((SUMS, own.shape[1]), F32)], 0)
    (modal,) = finish(phi_ts, own, recv)
    blocks = parity_blocks(modal)
    resid, w, x_hi, x_lo, n_hi, n_lo = extend(onehot_t, vec, load, recv, phi_recv)
    phi_n = (n_hi, n_lo)
    y, y_shared, q, q_shared = schur_first(me, left_rows, right_rows, schur, (x_hi, x_lo), phi_n, q_own)

    scales, resids, stacks = [], [resid], []
    for iteration in range(ITERS):
        last = iteration == ITERS - 1
        send, keep = coarse(me, inverses, blocks)
        got = swap_x(send)
        edge = edge_blocks(keep[2 * nm:3 * nm] + got[2 * nm:3 * nm])
        to_x, to_d, stack = shared_image(
            me, n_sub - 1, left_rows, right_rows, schur.shape[0], q_shared, y_shared, keep, got, edge
        )
        stacks.append(stack)
        recv = swap_x(to_x), swap_d(to_d)
        if iteration == 0:
            p, own = local_image(q, y, vec, phi_t, stack, (resid,), True)
            modal, far, near = finish(phi_ts, own, recv, (to_x, to_d))
        else:
            scale = scale_of(over_axis(keep[3 * nm:] + got[3 * nm:], "cluster"))
            scales.append(scale)
            p, resid, own = local_image(q, y, vec, phi_t, stack, (resid, scale, p, image), not last)
            resids.append(resid)
            modal, far, near = finish(phi_ts, own, recv, (to_x, to_d), (scale, far, near))
        if not last:
            blocks = parity_blocks(modal)
            image, x_hi, x_lo = assemble(onehot_t, p, far, w)
            y, y_shared = schur_apply(me, left_rows, right_rows, schur, (x_hi, x_lo))
    sums = over_axis(over_axis(modal[nm:], "cluster"), "sub")
    sol, final = directions(phi, phi_n, w, scales, resids, stacks)
    (image,) = assemble(onehot_t, p, far)
    scale = scale_of(sums)[0:1]
    return sol + scale * final, resid - scale * image


def solution(mesh):
    rows = P(BOTH, None)
    return jax.shard_map(
        local,
        mesh=mesh,
        in_specs=(rows, rows, rows, rows, P(BOTH), P(BOTH), rows, rows),
        out_specs=(rows, rows),
        check_vma=False,
    )
```

time: 690 us -> 240 us (0.35); the launches traced: 679 us -> 239 us
  other arithmetic: 119 us -> 2.43 us
  blocking collectives: 116 us -> 0 us
  matrix products: 110 us -> 0 us
  local copies, waits for them, and re-layouts: 110 us -> 10.1 us
  Pallas kernels: 0 us -> 86.9 us
  waiting for transfers between devices: 168 us -> 82 us
  starting transfers between devices: 39.4 us -> 55.2 us
  between operations: 15.9 us -> 2.41 us
    psum x3 -> x0, blocking collectives: 116 us -> none  [local(): lax.psum((jnp.sum(share * residual * image, axis=0), jnp.sum(share * imag...]
    dot_general x12 -> x0, matrix products: 110 us -> none  [the longest x3 82.9 us: local(): jnp.dot(schur, direction, precision=highest, preferred_element_type=jnp.f...]
    all_gather x3 -> x0, waiting for transfers between devices: 93.3 us -> none  [local(): lax.all_gather(modal, 'sub', axis=0, tiled=True)]
    pallas_call x0 -> x25, Pallas kernels: none -> 86.9 us  [call(): pl.pallas_call(body, name=name, in_specs=[pl.BlockSpec(memory_space=pltpu...]
    scatter-add x16 -> x0, other arithmetic: 80 us -> none  [the longest x7 36.5 us: assemble(): return merged.at[right_index].add(from_right, mode='drop')]
    gather x15 -> x0, local copies, waits for them, and re-layouts: 71 us -> none  [the longest x14 43 us: take_rows(): return jnp.take(field, indices, axis=0, mode='fill', fill_value=0.0)]
    select_n x18 -> x0, other arithmetic: 18.8 us -> none  [the longest x16 17.4 us: take_rows(): return jnp.take(field, indices, axis=0, mode='fill', fill_value=0.0)]
    scatter-add x7 -> x0, local copies, waits for them, and re-layouts: 16.4 us -> none  [assemble(): return merged.at[right_index].add(from_right, mode='drop')]
  transfers between devices with their start and end apart: 17 -> 37, of which waited for: 10 -> 19; matrix products, arithmetic and copies ran while one was open for 14% -> 0% of each run, Pallas kernels for 0% -> 32%
where the time goes in v2:
time: 240 us; the launch traced here: 239 us
  Pallas kernels  86.9 us (36%)
  waiting for transfers between devices  82 us (34%)
  starting transfers between devices  55.2 us (23%)
  local copies, waits for them, and re-layouts  10.1 us (4%)
  other arithmetic  2.43 us (1%)
  between operations  2.41 us (1%)
    pallas_call x25, Pallas kernels, call(): pl.pallas_call(body, name=name, in_specs=[pl.BlockSpec(memory_space=pltpu...  86.9 us
    ppermute x9, waiting for transfers between devices, swap_x(): return lax.ppermute(value, 'sub', [(i, i ^ 1) for i in range(n)])  39.1 us
    ppermute x9, waiting for transfers between devices, parity_blocks(): lax.ppermute(modal, 'sub', [(i, i ^ 2 * d) for i in range(n)])  29.5 us
    ppermute x9, waiting for transfers between devices, over_axis(): value = value + lax.ppermute(value, axis, [(i, i ^ step) for i in range(n)])  13.4 us
    ppermute x9, starting transfers between devices, parity_blocks(): lax.ppermute(modal, 'sub', [(i, i ^ 2 * d) for i in range(n)])  13.4 us
    ppermute x9, starting transfers between devices, over_axis(): value = value + lax.ppermute(value, axis, [(i, i ^ step) for i in range(n)])  13.1 us
    ppermute x9, starting transfers between devices, swap_x(): return lax.ppermute(value, 'sub', [(i, i ^ 1) for i in range(n)])  13 us
    unnamed x20, local copies, waits for them, and re-layouts  10.1 us
  transfers between devices with their start and end apart: 37, of which 19 were waited for; matrix products, arithmetic and copies ran while one was open for 0% of the time, Pallas kernels for 32%

profile of v2, /device:TPU:0, one launch (start us, length us, event | category | flops | bytes accessed | tf_op | source)
XLA Modules:
  0.0 239.0 jit_solution(1517714376832529913)
XLA Ops:
  3.5 4.3 %gather_load.1 = (f32[384,256]{1,0:T(8,128)S(1)}, f32[384,256]{1,0:T(8,128)S(1)}) custom-call(s32[1]{0:T(128)} %bitcast.me_ref, s32[1,384]{1,0:T(1,128)S(1)} %copy-done.6, s32[1,384]{1,0:T(1,128)S(1)} %copy-done.8, s32[1,384]{1,0:T(1,128)S(1)} %copy-done.6, s32[1,384]{1,0:T(1,128)S(1)} %copy-done.8, f32[1792,256]{1,0:T(8,128)S(1)} %copy-done.2), custom_call_target="tpu_custom_call" | custom-call | bytes 2624512 | tf_op jit(solution)/shard_map/gather_load/pallas_call | solution.py:46
  7.8 3.0 %collective-permute-start = (f32[384,256]{1,0:T(8,128)S(1)}, f32[384,256]{1,0:T(8,128)S(1)}, u32[]{:S(2)}, u32[]{:S(2)}) collective-permute-start(f32[384,256]{1,0:T(8,128)S(1)} %get-tuple-element.75), channel_id=1, source_target_pairs={{0,1},{1,0},{2,3},{3,2},{4,5},{5,4},{6,7},{7,6},{8,9},{9,8},{10,11... | collective-permute-start | bytes 1179656 | tf_op jit(solution)/shard_map/ppermute | solution.py:490
  12.7 5.2 %collective-permute-start.5 = (f32[128,512]{1,0:T(8,128)S(1)}, f32[128,512]{1,0:T(8,128)S(1)}, u32[]{:S(2)}, u32[]{:S(2)}) collective-permute-start(f32[128,512]{1,0:T(8,128)S(1)} %get-tuple-element.83), channel_id=1, source_target_pairs={{1,2},{3,4},{5,6},{7,0},{2,1},{4,3},{6,5},{0,7},{9,10},{11,12},{13... | collective-permute-start | bytes 786440 | tf_op jit(solution)/shard_map/ppermute | solution.py:503
  21.8 4.6 %copy-done = f32[1792,1792]{1,0:T(8,128)S(1)} copy-done((f32[1792,1792]{1,0:T(8,128)S(1)}, f32[1792,1792]{1,0:T(8,128)}, u32[]{:S(2)}) %copy-start) | copy-done | bytes 12845080
  27.7 4.3 %prepare.1 = (bf16[1792,768]{1,0:T(8,128)(2,1)S(1)}, bf16[1792,128]{1,0:T(8,128)(2,1)S(1)}, bf16[1792,128]{1,0:T(8,128)(2,1)S(1)}, bf16[128,1792]{1,0:T(8,128)(2...) custom-call(s32[1]{0:T(128)} %bitcast.me_ref, ...), custom_call_target="tpu_custom_call" | custom-call | flops 1056964608 | bytes 20081664 | tf_op jit(solution)/shard_map/prepare/pallas_call | solution.py:46
  32.3 6.9 %start.1 = (f32[1792,128]{1,0:T(8,128)S(1)}, f32[128,256]{1,0:T(8,128)S(1)}) custom-call(f32[1792,1792]{1,0:T(8,128)S(1)} %copy-done.1, bf16[1792,128]{1,0:T(8,128)(2,1)S(1)} %get-tuple-element.71.h_ref, bf16[1792,128]{1,0:T(8,128)(2,1)S(1)} %get-tuple-element.72.l_ref, bf16[128,1792]{1,0:T(8,128)(2,1)S(1)} %get-tuple-element.88.th_ref, ...), custom_call_target="tpu_custom_call" | custom-call | flops 2818572288 | bytes 17563648 | tf_op jit(solution)/shard_map/start/pallas_call | solution.py:46
  40.7 3.4 %collective-permute-start.7 = (f32[136,256]{1,0:T(8,128)S(1)}, f32[136,256]{1,0:T(8,128)S(1)}, u32[]{:S(2)}, u32[]{:S(2)}) collective-permute-start(f32[136,256]{1,0:T(8,128)S(1)} %finish.4.rest_0_), channel_id=1, source_target_pairs={{0,2},{1,3},{2,0},{3,1},{4,6},{5,7},{6,4},{7,5},{8,10},{9,11},{10,... | collective-permute-start | bytes 417800 | tf_op jit(solution)/shard_map/ppermute | solution.py:520
  44.7 2.8 %collective-permute-done.9.rest_3_ = f32[136,256]{1,0:T(8,128)S(1)} collective-permute-done((f32[136,256]{1,0:T(8,128)S(1)}, f32[136,256]{1,0:T(8,128)S(1)}, u32[]{:S(2)}, u32[]{:S(2)}) %collective-permute-start.9) | collective-permute-done | bytes 139296 | tf_op jit(solution)/shard_map/ppermute | solution.py:520
  47.6 6.6 %collective-permute-done.8.rest_2_ = f32[136,256]{1,0:T(8,128)S(1)} collective-permute-done((f32[136,256]{1,0:T(8,128)S(1)}, f32[136,256]{1,0:T(8,128)S(1)}, u32[]{:S(2)}, u32[]{:S(2)}) %collective-permute-start.8) | collective-permute-done | bytes 139296 | tf_op jit(solution)/shard_map/ppermute | solution.py:520
  54.8 5.3 %collective-permute-start.10 = (f32[392,256]{1,0:T(8,128)S(1)}, f32[392,256]{1,0:T(8,128)S(1)}, u32[]{:S(2)}, u32[]{:S(2)}) collective-permute-start(f32[392,256]{1,0:T(8,128)S(1)} %get-tuple-element.97), channel_id=1, source_target_pairs={{0,1},{1,0},{2,3},{3,2},{4,5},{5,4},{6,7},{7,6},{8,9},{9,8},{10,11... | collective-permute-start | bytes 1204232 | tf_op jit(solution)/shard_map/ppermute | solution.py:490
  60.1 5.8 %extend.1 = (f32[1792,256]{1,0:T(8,128)S(1)}, f32[1792,128]{1,0:T(8,128)S(1)}, bf16[1792,256]{1,0:T(8,128)(2,1)S(1)}, bf16[1792,256]{1,0:T(8,128)(2,1)S(1)}, bf1...) custom-call(bf16[1792,768]{1,0:T(8,128)(2,1)S(1)} %get-tuple-element.73.gt_ref, ...), custom_call_target="tpu_custom_call" | custom-call | flops 2818572288 | bytes 13131776 | tf_op jit(solution)/shard_map/extend/pallas_call | solution.py:46
  67.9 16.0 %schur_first.1 = (f32[1792,256]{1,0:T(8,128)S(1)}, f32[768,256]{1,0:T(8,128)S(1)}, f32[1792,384]{1,0:T(8,128)S(1)}, f32[768,384]{1,0:T(8,128)S(1)}) custom-call(s32[1]{0:T(128)} %bitcast.me_ref, s32[1,384]{1,0:T(1,128)S(1)} %copy-done.7, s32[1,384]{1,0:T(1,128)S(1)} %copy-done.9, f32[1792,1792]{1,0:T(8,128)S(1)} %copy-done.1, ...), custom_call_target="tpu_custom_call" | custom-call | flops 9865003008 | bytes 23986176 | tf_op jit(solution)/shard_map/schur_first/pallas_call | solution.py:46
  86.9 4.6 %local_image.3 = (f32[1792,256]{1,0:T(8,128)S(1)}, f32[136,256]{1,0:T(8,128)S(1)}) custom-call(f32[1792,384]{1,0:T(8,128)S(1)} %get-tuple-element.91.q_ref, f32[1792,256]{1,0:T(8,128)S(1)} %get-tuple-element.92.y_ref, f32[1792,128]{1,0:T(8,128)S(1)} %get-tuple-element.74.vec_ref, bf16[128,1792]{1,0:T(8,128)(2,1)S(1)} %get-tuple-element.88.th_ref, ...), custom_call_target="tpu_custom_call" | custom-call | flops 1409286144 | bytes 10625024 | tf_op jit(solution)/shard_map/local_image/pallas_call | solution.py:46
  91.4 11.8 %collective-permute-done.12.refs_0_ = f32[384,256]{1,0:T(8,128)S(1)} collective-permute-done((f32[384,256]{1,0:T(8,128)S(1)}, f32[384,256]{1,0:T(8,128)S(1)}, u32[]{:S(2)}, u32[]{:S(2)}) %collective-permute-start.12) | collective-permute-done | bytes 393248 | tf_op jit(solution)/shard_map/ppermute | solution.py:490
  103.7 2.9 %collective-permute-start.16 = (f32[136,256]{1,0:T(8,128)S(1)}, f32[136,256]{1,0:T(8,128)S(1)}, u32[]{:S(2)}, u32[]{:S(2)}) collective-permute-start(f32[136,256]{1,0:T(8,128)S(1)} %get-tuple-element.103.rest_0_), channel_id=1, source_target_pairs={{0,6},{1,7},{2,4},{3,5},{4,2},{5,3},{6,0},{7,1},{8,14},{9,15},{10,... | collective-permute-start | bytes 417800 | tf_op jit(solution)/shard_map/ppermute | solution.py:520
  108.1 3.4 %collective-permute-done.16.rest_3_ = f32[136,256]{1,0:T(8,128)S(1)} collective-permute-done((f32[136,256]{1,0:T(8,128)S(1)}, f32[136,256]{1,0:T(8,128)S(1)}, u32[]{:S(2)}, u32[]{:S(2)}) %collective-permute-start.16) | collective-permute-done | bytes 139296 | tf_op jit(solution)/shard_map/ppermute | solution.py:520
  111.5 7.6 %collective-permute-done.15.rest_2_ = f32[136,256]{1,0:T(8,128)S(1)} collective-permute-done((f32[136,256]{1,0:T(8,128)S(1)}, f32[136,256]{1,0:T(8,128)S(1)}, u32[]{:S(2)}, u32[]{:S(2)}) %collective-permute-start.15) | collective-permute-done | bytes 139296 | tf_op jit(solution)/shard_map/ppermute | solution.py:520
  121.0 2.8 %assemble.3 = (f32[1792,256]{1,0:T(8,128)S(1)}, bf16[1792,256]{1,0:T(8,128)(2,1)S(1)}, bf16[1792,256]{1,0:T(8,128)(2,1)S(1)}) custom-call(bf16[1792,768]{1,0:T(8,128)(2,1)S(1)} %get-tuple-element.73.gt_ref, f32[1792,256]{1,0:T(8,128)S(1)} %get-tuple-element.106.p_ref.refs_2_, f32[768,256]{1,0:T(8,128)S(1)} %get-tuple-element.107.g_ref.refs_5_, ...), custom_call_target="tpu_custom_call" | custom-call | flops 1409286144 | bytes 9961472 | tf_op jit(solution)/shard_map/assemble/pallas_call | solution.py:46
  123.8 6.2 %collective-permute-done.17.recv_ref = f32[392,256]{1,0:T(8,128)S(1)} collective-permute-done((f32[392,256]{1,0:T(8,128)S(1)}, f32[392,256]{1,0:T(8,128)S(1)}, u32[]{:S(2)}, u32[]{:S(2)}) %collective-permute-start.17) | collective-permute-done | bytes 401440 | tf_op jit(solution)/shard_map/ppermute | solution.py:490
  131.6 9.4 %schur_apply.2 = (f32[1792,256]{1,0:T(8,128)S(1)}, f32[768,256]{1,0:T(8,128)S(1)}) custom-call(s32[1]{0:T(128)} %bitcast.me_ref, s32[1,384]{1,0:T(1,128)S(1)} %copy-done.7, s32[1,384]{1,0:T(1,128)S(1)} %copy-done.9, f32[1792,1792]{1,0:T(8,128)S(1)} %copy-done.1, bf16[1792,256]{1,0:T(8,128)(2,1)S(1)} %get-tuple-element.108.xh_ref, ...), custom_call_target="tpu_custom_call" | custom-call | flops 4932501504 | bytes 17301504 | tf_op jit(solution)/shard_map/schur_apply/pallas_call | solution.py:46
  151.0 4.7 %local_image.4 = (f32[1792,256]{1,0:T(8,128)S(1)}, f32[1792,256]{1,0:T(8,128)S(1)}, f32[136,256]{1,0:T(8,128)S(1)}) custom-call(f32[1792,384]{1,0:T(8,128)S(1)} %get-tuple-element.91.q_ref, f32[1792,256]{1,0:T(8,128)S(1)} %get-tuple-element.110.y_ref, f32[1792,128]{1,0:T(8,128)S(1)} %get-tuple-element.74.vec_ref, ...), custom_call_target="tpu_custom_call" | custom-call | flops 1409286144 | bytes 16138240 | tf_op jit(solution)/shard_map/local_image/pallas_call | solution.py:46
  155.7 5.6 %collective-permute-done.21.refs_0_ = f32[384,256]{1,0:T(8,128)S(1)} collective-permute-done((f32[384,256]{1,0:T(8,128)S(1)}, f32[384,256]{1,0:T(8,128)S(1)}, u32[]{:S(2)}, u32[]{:S(2)}) %collective-permute-start.21) | collective-permute-done | bytes 393248 | tf_op jit(solution)/shard_map/ppermute | solution.py:490
  163.0 3.3 %collective-permute-start.23 = (f32[136,256]{1,0:T(8,128)S(1)}, f32[136,256]{1,0:T(8,128)S(1)}, u32[]{:S(2)}, u32[]{:S(2)}) collective-permute-start(f32[136,256]{1,0:T(8,128)S(1)} %get-tuple-element.118.rest_0_), channel_id=1, source_target_pairs={{0,2},{1,3},{2,0},{3,1},{4,6},{5,7},{6,4},{7,5},{8,10},{9,11},{10,... | collective-permute-start | bytes 417800 | tf_op jit(solution)/shard_map/ppermute | solution.py:520
  166.3 4.1 %collective-permute-done.25.rest_3_ = f32[136,256]{1,0:T(8,128)S(1)} collective-permute-done((f32[136,256]{1,0:T(8,128)S(1)}, f32[136,256]{1,0:T(8,128)S(1)}, u32[]{:S(2)}, u32[]{:S(2)}) %collective-permute-start.25) | collective-permute-done | bytes 139296 | tf_op jit(solution)/shard_map/ppermute | solution.py:520
  170.4 5.0 %collective-permute-done.24.rest_2_ = f32[136,256]{1,0:T(8,128)S(1)} collective-permute-done((f32[136,256]{1,0:T(8,128)S(1)}, f32[136,256]{1,0:T(8,128)S(1)}, u32[]{:S(2)}, u32[]{:S(2)}) %collective-permute-start.24) | collective-permute-done | bytes 139296 | tf_op jit(solution)/shard_map/ppermute | solution.py:520
  179.7 7.2 %collective-permute-done.26.recv_ref = f32[392,256]{1,0:T(8,128)S(1)} collective-permute-done((f32[392,256]{1,0:T(8,128)S(1)}, f32[392,256]{1,0:T(8,128)S(1)}, u32[]{:S(2)}, u32[]{:S(2)}) %collective-permute-start.26) | collective-permute-done | bytes 401440 | tf_op jit(solution)/shard_map/ppermute | solution.py:490
  188.1 9.4 %schur_apply.3 = (f32[1792,256]{1,0:T(8,128)S(1)}, f32[768,256]{1,0:T(8,128)S(1)}) custom-call(s32[1]{0:T(128)} %bitcast.me_ref, s32[1,384]{1,0:T(1,128)S(1)} %copy-done.7, s32[1,384]{1,0:T(1,128)S(1)} %copy-done.9, f32[1792,1792]{1,0:T(8,128)S(1)} %copy-done.1, bf16[1792,256]{1,0:T(8,128)(2,1)S(1)} %get-tuple-element.124.xh_ref, ...), custom_call_target="tpu_custom_call" | custom-call | flops 4932501504 | bytes 17301504 | tf_op jit(solution)/shard_map/schur_apply/pallas_call | solution.py:46
  199.4 4.0 %collective-permute-start.27 = (f32[8,256]{1,0:T(8,128)S(1)}, f32[8,256]{1,0:T(8,128)S(1)}, u32[]{:S(2)}, u32[]{:S(2)}) collective-permute-start(f32[8,256]{1,0:T(8,128)S(1)} %slice_add_fusion.3), channel_id=1, source_target_pairs={{0,8},{8,0},{16,24},{24,16},{1,9},{9,1},{17,25},{25,17},{2,10},{10... | collective-permute-start | bytes 24584 | tf_op jit(solution)/shard_map/ppermute | solution.py:530
  210.6 7.8 %collective-permute-done.30.refs_0_ = f32[384,256]{1,0:T(8,128)S(1)} collective-permute-done((f32[384,256]{1,0:T(8,128)S(1)}, f32[384,256]{1,0:T(8,128)S(1)}, u32[]{:S(2)}, u32[]{:S(2)}) %collective-permute-start.30) | collective-permute-done | bytes 393248 | tf_op jit(solution)/shard_map/ppermute | solution.py:490
  220.8 3.6 %collective-permute-done.33 = f32[8,256]{1,0:T(8,128)S(1)} collective-permute-done((f32[8,256]{1,0:T(8,128)S(1)}, f32[8,256]{1,0:T(8,128)S(1)}, u32[]{:S(2)}, u32[]{:S(2)}) %collective-permute-start.33) | collective-permute-done | bytes 8224 | tf_op jit(solution)/shard_map/ppermute | solution.py:530
  224.4 3.6 %collective-permute-done.34 = f32[8,256]{1,0:T(8,128)S(1)} collective-permute-done((f32[8,256]{1,0:T(8,128)S(1)}, f32[8,256]{1,0:T(8,128)S(1)}, u32[]{:S(2)}, u32[]{:S(2)}) %collective-permute-start.34) | collective-permute-done | bytes 8224 | tf_op jit(solution)/shard_map/ppermute | solution.py:530
  228.1 3.8 %directions.1 = (f32[1792,256]{1,0:T(8,128)S(1)}, f32[1792,256]{1,0:T(8,128)S(1)}) custom-call(bf16[1792,128]{1,0:T(8,128)(2,1)S(1)} %get-tuple-element.71.h_ref, bf16[1792,128]{1,0:T(8,128)(2,1)S(1)} %get-tuple-element.72.l_ref, bf16[1792,256]{1,0:T(8,128)(2,1)S(1)} %get-tuple-element.79.nh_ref, bf16[1792,256]{1,0:T(8,128)(2,1)S(1)} %get-tuple-element.80.nl_ref, ...), custom_call_target="tpu_custom_call" | custom-call | flops 2113929216 | bytes 14041088 | tf_op jit(solution)/shard_map/directions/pallas_call | solution.py:46
  (109 shorter events, 57.6 us)
Async XLA Ops:
  7.8 31.4 %collective-permute-start = (f32[384,256]{1,0:T(8,128)S(1)}, f32[384,256]{1,0:T(8,128)S(1)}, u32[]{:S(2)}, u32[]{:S(2)}) collective-permute-start(f32[384,256]{1,0:T(8,128)S(1)} %get-tuple-element.75), channel_id=1, source_target_pairs={{0,1},{1,0},{2,3},{3,2},{4,5},{5,4},{6,7},{7,6},{8,9},{9,8},{10,11... | collective-permute-start | bytes 1179656 | tf_op jit(solution)/shard_map/ppermute | solution.py:490
  10.9 28.4 %collective-permute-start.1 = (f32[384,256]{1,0:T(8,128)S(1)}, f32[384,256]{1,0:T(8,128)S(1)}, u32[]{:S(2)}, u32[]{:S(2)}) collective-permute-start(f32[384,256]{1,0:T(8,128)S(1)} %get-tuple-element.76), channel_id=1, source_target_pairs={{1,2},{3,4},{5,6},{7,8},{9,10},{11,12},{13,14},{15,16},{17,18},{19... | collective-permute-start | bytes 1179656 | tf_op jit(solution)/shard_map/ppermute | solution.py:496
  12.7 28.0 %collective-permute-start.5 = (f32[128,512]{1,0:T(8,128)S(1)}, f32[128,512]{1,0:T(8,128)S(1)}, u32[]{:S(2)}, u32[]{:S(2)}) collective-permute-start(f32[128,512]{1,0:T(8,128)S(1)} %get-tuple-element.83), channel_id=1, source_target_pairs={{1,2},{3,4},{5,6},{7,0},{2,1},{4,3},{6,5},{0,7},{9,10},{11,12},{13... | collective-permute-start | bytes 786440 | tf_op jit(solution)/shard_map/ppermute | solution.py:503
  17.9 26.2 %collective-permute-start.4 = (f32[128,512]{1,0:T(8,128)S(1)}, f32[128,512]{1,0:T(8,128)S(1)}, u32[]{:S(2)}, u32[]{:S(2)}) collective-permute-start(f32[128,512]{1,0:T(8,128)S(1)} %get-tuple-element.83), channel_id=1, source_target_pairs={{0,1},{1,0},{2,3},{3,2},{4,5},{5,4},{6,7},{7,6},{8,9},{9,8},{10,11... | collective-permute-start | bytes 786440 | tf_op jit(solution)/shard_map/ppermute | solution.py:490
  17.9 26.2 %collective-permute-start.6 = (f32[128,512]{1,0:T(8,128)S(1)}, f32[128,512]{1,0:T(8,128)S(1)}, u32[]{:S(2)}, u32[]{:S(2)}) collective-permute-start(f32[128,512]{1,0:T(8,128)S(1)} %get-tuple-element.82.own_ref), channel_id=1, source_target_pairs={{0,6},{1,3},{2,0},{3,5},{4,2},{5,7},{6,4},{7,1},{8,14},{9,11},{10,... | collective-permute-start | bytes 786440 | tf_op jit(solution)/shard_map/ppermute | solution.py:505
  39.6 8.0 %collective-permute-start.9 = (f32[136,256]{1,0:T(8,128)S(1)}, f32[136,256]{1,0:T(8,128)S(1)}, u32[]{:S(2)}, u32[]{:S(2)}) collective-permute-start(f32[136,256]{1,0:T(8,128)S(1)} %finish.4.rest_0_), channel_id=1, source_target_pairs={{0,6},{1,7},{2,4},{3,5},{4,2},{5,3},{6,0},{7,1},{8,14},{9,15},{10,... | collective-permute-start | bytes 417800 | tf_op jit(solution)/shard_map/ppermute | solution.py:520
  40.6 13.5 %collective-permute-start.8 = (f32[136,256]{1,0:T(8,128)S(1)}, f32[136,256]{1,0:T(8,128)S(1)}, u32[]{:S(2)}, u32[]{:S(2)}) collective-permute-start(f32[136,256]{1,0:T(8,128)S(1)} %finish.4.rest_0_), channel_id=1, source_target_pairs={{0,4},{1,5},{2,6},{3,7},{4,0},{5,1},{6,2},{7,3},{8,12},{9,13},{10,... | collective-permute-start | bytes 417800 | tf_op jit(solution)/shard_map/ppermute | solution.py:520
  40.7 13.5 %collective-permute-start.7 = (f32[136,256]{1,0:T(8,128)S(1)}, f32[136,256]{1,0:T(8,128)S(1)}, u32[]{:S(2)}, u32[]{:S(2)}) collective-permute-start(f32[136,256]{1,0:T(8,128)S(1)} %finish.4.rest_0_), channel_id=1, source_target_pairs={{0,2},{1,3},{2,0},{3,1},{4,6},{5,7},{6,4},{7,5},{8,10},{9,11},{10,... | collective-permute-start | bytes 417800 | tf_op jit(solution)/shard_map/ppermute | solution.py:520
  44.1 16.1 %collective-permute-start.2 = (f32[408,128]{1,0:T(8,128)S(1)}, f32[408,128]{1,0:T(8,128)S(1)}, u32[]{:S(2)}, u32[]{:S(2)}) collective-permute-start(f32[408,128]{1,0:T(8,128)S(1)} %get-tuple-element.77), channel_id=1, source_target_pairs={{0,1},{1,0},{2,3},{3,2},{4,5},{5,4},{6,7},{7,6},{8,9},{9,8},{10,11... | collective-permute-start | bytes 626696 | tf_op jit(solution)/shard_map/ppermute | solution.py:490
  44.1 16.1 %collective-permute-start.3 = (f32[408,128]{1,0:T(8,128)S(1)}, f32[408,128]{1,0:T(8,128)S(1)}, u32[]{:S(2)}, u32[]{:S(2)}) collective-permute-start(f32[408,128]{1,0:T(8,128)S(1)} %get-tuple-element.78), channel_id=1, source_target_pairs={{1,2},{3,4},{5,6},{7,8},{9,10},{11,12},{13,14},{15,16},{17,18},{19... | collective-permute-start | bytes 626696 | tf_op jit(solution)/shard_map/ppermute | solution.py:496
  54.8 11.6 %collective-permute-start.10 = (f32[392,256]{1,0:T(8,128)S(1)}, f32[392,256]{1,0:T(8,128)S(1)}, u32[]{:S(2)}, u32[]{:S(2)}) collective-permute-start(f32[392,256]{1,0:T(8,128)S(1)} %get-tuple-element.97), channel_id=1, source_target_pairs={{0,1},{1,0},{2,3},{3,2},{4,5},{5,4},{6,7},{7,6},{8,9},{9,8},{10,11... | collective-permute-start | bytes 1204232 | tf_op jit(solution)/shard_map/ppermute | solution.py:490
  66.4 17.5 %collective-permute-start.11 = (f32[128,256]{1,0:T(8,128)S(1)}, f32[128,256]{1,0:T(8,128)S(1)}, u32[]{:S(2)}, u32[]{:S(2)}) collective-permute-start(f32[128,256]{1,0:T(8,128)S(1)} %slice_add_fusion.2), channel_id=1, source_target_pairs={{0,8},{8,16},{16,24},{15,7},{23,15},{31,23}} | collective-permute-start | bytes 393224 | tf_op jit(solution)/shard_map/ppermute | solution.py:539
  84.6 18.6 %collective-permute-start.12 = (f32[384,256]{1,0:T(8,128)S(1)}, f32[384,256]{1,0:T(8,128)S(1)}, u32[]{:S(2)}, u32[]{:S(2)}) collective-permute-start(f32[384,256]{1,0:T(8,128)S(1)} %get-tuple-element.101.refs_2_), channel_id=1, source_target_pairs={{0,1},{1,0},{2,3},{3,2},{4,5},{5,4},{6,7},{7,6},{8,9},{9,8},{10,11... | collective-permute-start | bytes 1179656 | tf_op jit(solution)/shard_map/ppermute | solution.py:490
  86.2 17.0 %collective-permute-start.13 = (f32[384,256]{1,0:T(8,128)S(1)}, f32[384,256]{1,0:T(8,128)S(1)}, u32[]{:S(2)}, u32[]{:S(2)}) collective-permute-start(f32[384,256]{1,0:T(8,128)S(1)} %get-tuple-element.102.refs_3_), channel_id=1, source_target_pairs={{1,2},{3,4},{5,6},{7,8},{9,10},{11,12},{13,14},{15,16},{17,18},{19... | collective-permute-start | bytes 1179656 | tf_op jit(solution)/shard_map/ppermute | solution.py:496
  103.7 7.8 %collective-permute-start.16 = (f32[136,256]{1,0:T(8,128)S(1)}, f32[136,256]{1,0:T(8,128)S(1)}, u32[]{:S(2)}, u32[]{:S(2)}) collective-permute-start(f32[136,256]{1,0:T(8,128)S(1)} %get-tuple-element.103.rest_0_), channel_id=1, source_target_pairs={{0,6},{1,7},{2,4},{3,5},{4,2},{5,3},{6,0},{7,1},{8,14},{9,15},{10,... | collective-permute-start | bytes 417800 | tf_op jit(solution)/shard_map/ppermute | solution.py:520
  106.6 12.5 %collective-permute-start.15 = (f32[136,256]{1,0:T(8,128)S(1)}, f32[136,256]{1,0:T(8,128)S(1)}, u32[]{:S(2)}, u32[]{:S(2)}) collective-permute-start(f32[136,256]{1,0:T(8,128)S(1)} %get-tuple-element.103.rest_0_), channel_id=1, source_target_pairs={{0,4},{1,5},{2,6},{3,7},{4,0},{5,1},{6,2},{7,3},{8,12},{9,13},{10,... | collective-permute-start | bytes 417800 | tf_op jit(solution)/shard_map/ppermute | solution.py:520
  107.1 12.0 %collective-permute-start.14 = (f32[136,256]{1,0:T(8,128)S(1)}, f32[136,256]{1,0:T(8,128)S(1)}, u32[]{:S(2)}, u32[]{:S(2)}) collective-permute-start(f32[136,256]{1,0:T(8,128)S(1)} %get-tuple-element.103.rest_0_), channel_id=1, source_target_pairs={{0,2},{1,3},{2,0},{3,1},{4,6},{5,7},{6,4},{7,5},{8,10},{9,11},{10,... | collective-permute-start | bytes 417800 | tf_op jit(solution)/shard_map/ppermute | solution.py:520
  119.8 10.3 %collective-permute-start.17 = (f32[392,256]{1,0:T(8,128)S(1)}, f32[392,256]{1,0:T(8,128)S(1)}, u32[]{:S(2)}, u32[]{:S(2)}) collective-permute-start(f32[392,256]{1,0:T(8,128)S(1)} %get-tuple-element.105), channel_id=1, source_target_pairs={{0,1},{1,0},{2,3},{3,2},{4,5},{5,4},{6,7},{7,6},{8,9},{9,8},{10,11... | collective-permute-start | bytes 1204232 | tf_op jit(solution)/shard_map/ppermute | solution.py:490
  130.1 10.9 %collective-permute-start.20 = (f32[128,256]{1,0:T(8,128)S(1)}, f32[128,256]{1,0:T(8,128)S(1)}, u32[]{:S(2)}, u32[]{:S(2)}) collective-permute-start(f32[128,256]{1,0:T(8,128)S(1)} %slice_add_fusion.1), channel_id=1, source_target_pairs={{0,8},{8,16},{16,24},{15,7},{23,15},{31,23}} | collective-permute-start | bytes 393224 | tf_op jit(solution)/shard_map/ppermute | solution.py:539
  141.7 19.6 %collective-permute-start.21 = (f32[384,256]{1,0:T(8,128)S(1)}, f32[384,256]{1,0:T(8,128)S(1)}, u32[]{:S(2)}, u32[]{:S(2)}) collective-permute-start(f32[384,256]{1,0:T(8,128)S(1)} %get-tuple-element.115.refs_2_), channel_id=1, source_target_pairs={{0,1},{1,0},{2,3},{3,2},{4,5},{5,4},{6,7},{7,6},{8,9},{9,8},{10,11... | collective-permute-start | bytes 1179656 | tf_op jit(solution)/shard_map/ppermute | solution.py:490
  142.7 18.6 %collective-permute-start.22 = (f32[384,256]{1,0:T(8,128)S(1)}, f32[384,256]{1,0:T(8,128)S(1)}, u32[]{:S(2)}, u32[]{:S(2)}) collective-permute-start(f32[384,256]{1,0:T(8,128)S(1)} %get-tuple-element.116.refs_3_), channel_id=1, source_target_pairs={{1,2},{3,4},{5,6},{7,8},{9,10},{11,12},{13,14},{15,16},{17,18},{19... | collective-permute-start | bytes 1179656 | tf_op jit(solution)/shard_map/ppermute | solution.py:496
  146.8 4.2 %collective-permute-start.19 = (f32[8,256]{1,0:T(8,128)S(1)}, f32[8,256]{1,0:T(8,128)S(1)}, u32[]{:S(2)}, u32[]{:S(2)}) collective-permute-start(f32[8,256]{1,0:T(8,128)S(1)} %add.58), channel_id=1, source_target_pairs={{0,16},{8,24},{16,0},{24,8},{1,17},{9,25},{17,1},{25,9},{2,18},{10... | collective-permute-start | bytes 24584 | tf_op jit(solution)/shard_map/ppermute | solution.py:530
  161.9 8.6 %collective-permute-start.25 = (f32[136,256]{1,0:T(8,128)S(1)}, f32[136,256]{1,0:T(8,128)S(1)}, u32[]{:S(2)}, u32[]{:S(2)}) collective-permute-start(f32[136,256]{1,0:T(8,128)S(1)} %get-tuple-element.118.rest_0_), channel_id=1, source_target_pairs={{0,6},{1,7},{2,4},{3,5},{4,2},{5,3},{6,0},{7,1},{8,14},{9,15},{10,... | collective-permute-start | bytes 417800 | tf_op jit(solution)/shard_map/ppermute | solution.py:520
  163.0 12.5 %collective-permute-start.24 = (f32[136,256]{1,0:T(8,128)S(1)}, f32[136,256]{1,0:T(8,128)S(1)}, u32[]{:S(2)}, u32[]{:S(2)}) collective-permute-start(f32[136,256]{1,0:T(8,128)S(1)} %get-tuple-element.118.rest_0_), channel_id=1, source_target_pairs={{0,4},{1,5},{2,6},{3,7},{4,0},{5,1},{6,2},{7,3},{8,12},{9,13},{10,... | collective-permute-start | bytes 417800 | tf_op jit(solution)/shard_map/ppermute | solution.py:520
  163.0 12.5 %collective-permute-start.23 = (f32[136,256]{1,0:T(8,128)S(1)}, f32[136,256]{1,0:T(8,128)S(1)}, u32[]{:S(2)}, u32[]{:S(2)}) collective-permute-start(f32[136,256]{1,0:T(8,128)S(1)} %get-tuple-element.118.rest_0_), channel_id=1, source_target_pairs={{0,2},{1,3},{2,0},{3,1},{4,6},{5,7},{6,4},{7,5},{8,10},{9,11},{10,... | collective-permute-start | bytes 417800 | tf_op jit(solution)/shard_map/ppermute | solution.py:520
  176.1 10.7 %collective-permute-start.26 = (f32[392,256]{1,0:T(8,128)S(1)}, f32[392,256]{1,0:T(8,128)S(1)}, u32[]{:S(2)}, u32[]{:S(2)}) collective-permute-start(f32[392,256]{1,0:T(8,128)S(1)} %get-tuple-element.120), channel_id=1, source_target_pairs={{0,1},{1,0},{2,3},{3,2},{4,5},{5,4},{6,7},{7,6},{8,9},{9,8},{10,11... | collective-permute-start | bytes 1204232 | tf_op jit(solution)/shard_map/ppermute | solution.py:490
  186.8 10.8 %collective-permute-start.29 = (f32[128,256]{1,0:T(8,128)S(1)}, f32[128,256]{1,0:T(8,128)S(1)}, u32[]{:S(2)}, u32[]{:S(2)}) collective-permute-start(f32[128,256]{1,0:T(8,128)S(1)} %slice_add_fusion), channel_id=1, source_target_pairs={{0,8},{8,16},{16,24},{15,7},{23,15},{31,23}} | collective-permute-start | bytes 393224 | tf_op jit(solution)/shard_map/ppermute | solution.py:539
  198.3 20.1 %collective-permute-start.30 = (f32[384,256]{1,0:T(8,128)S(1)}, f32[384,256]{1,0:T(8,128)S(1)}, u32[]{:S(2)}, u32[]{:S(2)}) collective-permute-start(f32[384,256]{1,0:T(8,128)S(1)} %get-tuple-element.133.refs_2_), channel_id=1, source_target_pairs={{0,1},{1,0},{2,3},{3,2},{4,5},{5,4},{6,7},{7,6},{8,9},{9,8},{10,11... | collective-permute-start | bytes 1179656 | tf_op jit(solution)/shard_map/ppermute | solution.py:490
  198.4 20.0 %collective-permute-start.31 = (f32[384,256]{1,0:T(8,128)S(1)}, f32[384,256]{1,0:T(8,128)S(1)}, u32[]{:S(2)}, u32[]{:S(2)}) collective-permute-start(f32[384,256]{1,0:T(8,128)S(1)} %get-tuple-element.134.refs_3_), channel_id=1, source_target_pairs={{1,2},{3,4},{5,6},{7,8},{9,10},{11,12},{13,14},{15,16},{17,18},{19... | collective-permute-start | bytes 1179656 | tf_op jit(solution)/shard_map/ppermute | solution.py:496
  199.4 4.8 %collective-permute-start.27 = (f32[8,256]{1,0:T(8,128)S(1)}, f32[8,256]{1,0:T(8,128)S(1)}, u32[]{:S(2)}, u32[]{:S(2)}) collective-permute-start(f32[8,256]{1,0:T(8,128)S(1)} %slice_add_fusion.3), channel_id=1, source_target_pairs={{0,8},{8,0},{16,24},{24,16},{1,9},{9,1},{17,25},{25,17},{2,10},{10... | collective-permute-start | bytes 24584 | tf_op jit(solution)/shard_map/ppermute | solution.py:530
  228.1 3.8 %collective-permute-start.35 = (f32[8,256]{1,0:T(8,128)S(1)}, f32[8,256]{1,0:T(8,128)S(1)}, u32[]{:S(2)}, u32[]{:S(2)}) collective-permute-start(f32[8,256]{1,0:T(8,128)S(1)} %add.69), channel_id=1, source_target_pairs={{0,2},{1,3},{2,0},{3,1},{4,6},{5,7},{6,4},{7,5},{8,10},{9,11},{10,... | collective-permute-start | bytes 24584 | tf_op jit(solution)/shard_map/ppermute | solution.py:530
  231.9 4.7 %collective-permute-start.36 = (f32[8,256]{1,0:T(8,128)S(1)}, f32[8,256]{1,0:T(8,128)S(1)}, u32[]{:S(2)}, u32[]{:S(2)}) collective-permute-start(f32[8,256]{1,0:T(8,128)S(1)} %add.70), channel_id=1, source_target_pairs={{0,4},{1,5},{2,6},{3,7},{4,0},{5,1},{6,2},{7,3},{8,12},{9,13},{10,... | collective-permute-start | bytes 24584 | tf_op jit(solution)/shard_map/ppermute | solution.py:530
  (15 other events, 100.8 us)

commit v3 on v2

v3 whole, which is shorter than its diff:
```python
import jax
import jax.numpy as jnp
from jax import lax
from jax.experimental import pallas as pl
from jax.experimental.pallas import tpu as pltpu
from jax.sharding import PartitionSpec as P


BOTH = ("cluster", "sub")
F32 = jnp.float32
BF16 = jnp.bfloat16
ITERS = 3
INTERPRET = False
SUMS = 8


def split2(x):
    hi = x.astype(BF16)
    return hi, (x - hi.astype(F32)).astype(BF16)


def split3(x):
    hi = x.astype(BF16)
    rest = x - hi.astype(F32)
    mid = rest.astype(BF16)
    return hi, mid, (rest - mid.astype(F32)).astype(BF16)


def mm(a, b):
    return jnp.dot(a, b, preferred_element_type=F32)


def mm3(a, b):
    return mm(jnp.concatenate([a[0], a[0]], 1), jnp.concatenate([b[0], b[1]], 0)) + mm(a[1], b[0])


def pick(onehot, parts):
    return mm(jnp.concatenate([onehot] * len(parts), 1), jnp.concatenate(parts, 0))


def shape(*dims, dtype=F32):
    return jax.ShapeDtypeStruct(dims, dtype)


def call(body, ins, outs, flops, scalars=(), scratch=(), mb=8, raw=(), after=()):
    moved = sum(a.size * a.dtype.itemsize for a in (*ins, *outs))
    lead = len(scalars) + len(raw) + len(ins)

    def run(*refs):
        body(*refs[:lead], *refs[lead + len(after):])

    anywhere = pl.BlockSpec(memory_space=pl.ANY)
    outside = pl.BlockSpec(memory_space=pltpu.HBM)
    on_chip = pl.BlockSpec(memory_space=pltpu.VMEM)
    return pl.pallas_call(
        run,
        in_specs=[pl.BlockSpec(memory_space=pltpu.SMEM)] * len(scalars) + [outside] * len(raw)
        + [on_chip] * len(ins) + [anywhere] * len(after),
        out_specs=[on_chip] * len(outs),
        out_shape=list(outs),
        scratch_shapes=list(scratch),
        cost_estimate=pl.CostEstimate(flops=int(flops), bytes_accessed=int(moved), transcendentals=0),
        compiler_params=pltpu.CompilerParams(vmem_limit_bytes=mb * 1024 * 1024),
        interpret=INTERPRET,
    )(*scalars, *[pltpu.with_memory_space_constraint(a, pltpu.HBM) for a in raw], *ins, *after)


def over_blocks(order, step, carry=0, unroll=False):
    b = block_of(order)
    if unroll:
        for k in range(0, order, b):
            carry = step(pl.ds(k, b), k, carry)
        return carry

    def one(k, carry):
        at = pl.multiple_of(k * b, b)
        return step(pl.ds(at, b), at, carry)

    return lax.fori_loop(0, order // b, one, carry)


def block_of(order):
    return 256 if order % 256 == 0 else order


def copy_rows(pairs, index_ref, base, half, order, masked):
    group = 8 if half % 8 == 0 else 1

    def step(j, _):
        for u in range(group):
            slot = j * group + u
            row = index_ref[0, slot]
            at = jnp.minimum(row, order - 1)
            for source, out in pairs:
                value = source[pl.ds(at, 1), :]
                out[pl.ds(base + slot, 1), :] = jnp.where(row < order, value, 0.0) if masked else value
        return 0

    lax.fori_loop(0, half // group, step, 0)


def by_parity(me, work):
    even = lax.rem(me, 2) == 0
    pl.when(even)(lambda: work(1, 0))
    pl.when(jnp.logical_not(even))(lambda: work(0, 1))


def row_sides(me_ref, left_ref, right_ref):
    even = lax.rem(me_ref[0], 2) == 0
    left, right = left_ref[...], right_ref[...]
    return jnp.where(even, right, left), jnp.where(even, left, right)


def used_count(row, order):
    return jnp.sum(jnp.where(row < order, 1, 0))


def gather_load(me, left, right, load):
    half = left.shape[1]
    order, k = load.shape

    def body(me_ref, l_hbm, r_hbm, load_hbm, x_ref, d_ref, l_ref, r_ref, load_ref, sems):
        moves = [
            pltpu.make_async_copy(source, target, sems.at[i])
            for i, (source, target) in enumerate(((l_hbm, l_ref), (r_hbm, r_ref), (load_hbm, load_ref)))
        ]
        for move in moves:
            move.start()
        for move in moves:
            move.wait()
        rows = (l_ref, r_ref)

        def work(first, second):
            copy_rows([(load_ref, x_ref)], rows[first], 0, half, order, True)
            copy_rows([(load_ref, d_ref)], rows[second], 0, half, order, True)

        by_parity(me_ref[0], work)

    return call(
        body, [], [shape(half, k)] * 2, 0, [me], raw=[left, right, load],
        scratch=[pltpu.SMEM((1, half), jnp.int32)] * 2 + [pltpu.VMEM((order, k), F32), pltpu.SemaphoreType.DMA((3,))],
    )


def gather_shared(me, left, right, fields, masked=False):
    half = left.shape[1]
    order = fields[0].shape[0]
    n = len(fields)

    def body(me_ref, l_ref, r_ref, *refs):
        rows = (l_ref, r_ref)

        def work(first, second):
            for side, index in enumerate((first, second)):
                outs = refs[n + side::2] if masked else refs[n:]
                pairs = list(zip(refs[:n], outs))
                copy_rows(pairs, rows[index], 0 if masked else side * half, half, order, masked)

        by_parity(me_ref[0], work)

    if masked:
        outs = [shape(half, f.shape[1]) for f in fields for _ in range(2)]
    else:
        outs = [shape(2 * half, f.shape[1]) for f in fields]
    return call(body, fields, outs, 2e9, [me, left, right], mb=4)


def halves(me, inverse, after):
    nm, co = inverse.shape

    def body(me_ref, c_ref, same_ref, other_ref):
        par = lax.rem(me_ref[0], 2)
        for j in range(co // nm // 2):
            to = slice(j * nm, (j + 1) * nm)
            same_ref[:, to] = c_ref[:, pl.ds(pl.multiple_of((2 * j + par) * nm, nm), nm)]
            other_ref[:, to] = c_ref[:, pl.ds(pl.multiple_of((2 * j + 1 - par) * nm, nm), nm)]

    return call(body, [inverse], [shape(nm, co // 2)] * 2, 0, [me], after=after)


def prepare(me, live_rows, live_modes, left, right, schur, modes, load):
    order, nm = modes.shape
    half = left.shape[1]
    two = 2 * half
    pieces = half // nm
    tall = half + 8 * pieces
    b = block_of(order)
    k_load = load.shape[1]

    def body(me_ref, rows_ref, count_ref, s_hbm, modes_hbm, load_hbm, l_ref, r_ref,
             gt_ref, ph_ref, pl_ref, pth_ref, ptl_ref, vec_ref, x_ref, d_ref, tsh_ref, tsl_ref, m_ref,
             square_ref, modes_ref, load_ref, sems):
        def moves(r, columns, k):
            return [
                pltpu.make_async_copy(source, target.at[r], sems.at[i, k])
                for i, (source, target) in enumerate((
                    (s_hbm.at[r, columns], square_ref), (modes_hbm.at[r], modes_ref), (load_hbm.at[r], load_ref)
                ))
            ]

        for k in range(order // b):
            for move in moves(pl.ds(k * b, b), pl.ds(k * b, b), k):
                move.start()
        index = jnp.concatenate(row_sides(me_ref, l_ref, r_ref), axis=1)
        mask = jnp.where(lax.broadcasted_iota(jnp.int32, (1, nm), 1) < count_ref[0], 1.0, 0.0)
        eye = lax.broadcasted_iota(jnp.int32, (b, b), 0) == lax.broadcasted_iota(jnp.int32, (b, b), 1)
        lane = lax.broadcasted_iota(jnp.int32, (b, 128), 1)

        def step(r, start, carry):
            shared, weights, modal = carry
            for move in moves(r, r, start // b):
                move.wait()
            row_id = lax.broadcasted_iota(jnp.int32, (b, two), 0) + start
            found = jnp.where(index == row_id, 1.0, 0.0)
            gt = found.astype(BF16)
            gt_ref[r] = gt
            live = jnp.where(lax.broadcasted_iota(jnp.int32, (b, 1), 0) + start < rows_ref[0], 1.0, 0.0)
            share = live / (1.0 + jnp.sum(found, axis=1, keepdims=True))
            diag = jnp.sum(jnp.where(eye, square_ref[r], 0.0), axis=1, keepdims=True)
            sd = share / diag
            weights = weights + jnp.sum(found * sd, axis=0, keepdims=True)
            vec_ref[r] = jnp.where(lane == 0, live, sd)
            phi = share * (modes_ref[r] * mask)
            ph_ref[r], pl_ref[r] = split2(phi)
            parts = split3(phi.T)
            pth_ref[:, r], ptl_ref[:, r] = parts[:2]
            shared = shared + mm(jnp.concatenate(parts, 1), jnp.concatenate([gt] * 3, 0))
            return shared, weights, modal + mm3(parts[:2], split2(load_ref[r]))

        shared, weights, modal = over_blocks(
            order, step, (jnp.zeros((nm, two), F32), jnp.zeros((1, two), F32), jnp.zeros((nm, k_load), F32))
        )
        m_ref[:nm] = modal
        m_ref[nm:] = jnp.zeros((SUMS, k_load), F32)
        tsh_ref[...], tsl_ref[...] = split2(shared)
        back = shared.T
        for i, ref in enumerate((x_ref, d_ref)):
            ref[:half] = back[i * half:(i + 1) * half]
            for t in range(pieces):
                at = i * half + t * nm
                ref[half + 8 * t:half + 8 * t + 8] = jnp.broadcast_to(weights[:, at:at + nm], (8, nm))

    half_type = dict(dtype=BF16)
    return call(
        body, [left, right],
        [shape(order, two, **half_type), shape(order, nm, **half_type), shape(order, nm, **half_type),
         shape(nm, order, **half_type), shape(nm, order, **half_type), shape(order, 128),
         shape(tall, nm), shape(tall, nm), shape(nm, two, **half_type), shape(nm, two, **half_type),
         shape(nm + SUMS, k_load)],
        6 * two * order * nm, [me, live_rows, live_modes], raw=[schur, modes, load], mb=14,
        scratch=[pltpu.VMEM((order, b), F32), pltpu.VMEM((order, nm), F32), pltpu.VMEM((order, k_load), F32),
                 pltpu.SemaphoreType.DMA((3, order // b))],
    )


def extend(onehot_t, vec, load, recv, phi_recv):
    order, two = onehot_t.shape
    half = two // 2
    k = load.shape[1]
    nm = phi_recv[0].shape[1]
    pieces = half // nm

    def body(gt_ref, vec_ref, f_ref, rx_ref, rd_ref, px_ref, pd_ref, r_ref, w_ref, nh_ref, nl_ref):
        field = [jnp.concatenate(p, 0) for p in zip(split2(rx_ref[...]), split2(rd_ref[...]))]
        weights = jnp.concatenate(
            [ref[half + 8 * t:half + 8 * t + 1] for ref in (px_ref, pd_ref) for t in range(pieces)], axis=1
        )
        modes = [jnp.concatenate(split2(ref[:half]), 0) for ref in (px_ref, pd_ref)]

        def step(r, _, carry):
            gt = gt_ref[r]
            w = vec_ref[r, 1:2] + jnp.sum(gt.astype(F32) * weights, axis=1, keepdims=True)
            w_ref[r] = jnp.broadcast_to(w, (w.shape[0], 128))
            r_ref[r] = vec_ref[r, 0:1] * f_ref[r] + pick(gt, field)
            for i in range(2):
                side = gt[:, i * half:(i + 1) * half]
                part = mm(jnp.concatenate([side, side], 1), modes[i])
                nh_ref[r, i * nm:(i + 1) * nm], nl_ref[r, i * nm:(i + 1) * nm] = split2(part)
            return carry

        over_blocks(order, step)

    return call(
        body, [onehot_t, vec, load, *recv, *phi_recv],
        [shape(order, k), shape(order, 128)] + [shape(order, 2 * nm, dtype=BF16)] * 2,
        2 * order * two * (3 * k + 2 * nm), mb=12,
    )


def schur_modes(schur, modes, after=()):
    order, n = modes[0].shape

    def body(s_ref, h_ref, l_ref, q_ref):
        rhs = (h_ref[...], l_ref[...])

        def block(r, _, carry):
            q_ref[r] = mm3(split2(s_ref[r]), rhs)
            return carry

        over_blocks(order, block, unroll=True)

    return call(body, [schur, *modes], [shape(order, n)], 6 * order * order * n, mb=10, after=after)[0]


def schur_apply(schur, x):
    order, k = x[0].shape

    def body(s_ref, xh_ref, xl_ref, y_ref):
        x = (xh_ref[...], xl_ref[...])

        def block(r, _, carry):
            y_ref[r] = mm3(split2(s_ref[r]), x)
            return carry

        over_blocks(order, block, unroll=True)

    return call(body, [schur, *x], [shape(order, k)], 6 * order * order * k, mb=10)[0]


def coarse(me, inverses, modal, after):
    nm, co = inverses[0].shape
    _, k = modal[0].shape
    n = len(modal)
    ordered = direct(2 * n)

    def body(me_ref, own_ref, x_ref, d_ref, z_ref, *rest):
        send_ref, keep_ref, d_out, z_out, xh, xl = rest[n:]
        pos = me_ref[0] // 2
        sums = jnp.zeros((SUMS, k), F32)
        for d in range(n):
            at = pl.ds(pl.multiple_of(((pos ^ d) if ordered else d) * nm, nm), nm)
            xh[at], xl[at] = split2(rest[d][:nm])
            sums = sums + rest[d][nm:]
        a = split2(jnp.concatenate([own_ref[...], x_ref[...], d_ref[...], z_ref[...]], 0))
        part = mm3(a, (xh[...], xl[...]))
        keep_ref[:3 * nm] = part[:3 * nm]
        keep_ref[3 * nm:] = sums
        send_ref[:nm] = part[nm:2 * nm]
        send_ref[nm:2 * nm] = part[:nm]
        send_ref[2 * nm:3 * nm] = part[3 * nm:]
        send_ref[3 * nm:] = sums
        d_out[...] = part[2 * nm:3 * nm]
        z_out[...] = part[3 * nm:]

    return call(
        body, [*inverses, *modal], [shape(3 * nm + SUMS, k)] * 2 + [shape(nm, k)] * 2,
        24 * nm * co * k, [me], scratch=[pltpu.VMEM((co, k), BF16)] * 2, mb=12, after=after,
    )


def whole_stack(me, last_sub, keep, recv, edges, out):
    nm = edges[0].shape[0]
    at_edge = jnp.logical_or(me == 0, me == last_sub)
    total = keep[:3 * nm] + recv[:3 * nm]
    out[:2 * nm] = total[:2 * nm]
    out[2 * nm:] = jnp.where(at_edge, edges[0][...] + edges[1][...], total[2 * nm:])


def first_direction(me, last_sub, keep, recv, edges, phi, phi_n, w, resid):
    order, nm = phi[0].shape
    k = resid.shape[1]

    def body(me_ref, keep_ref, recv_ref, e1_ref, e2_ref, h_ref, l_ref, nh_ref, nl_ref, w_ref, r_ref,
             st_ref, xh_ref, xl_ref):
        whole_stack(me_ref[0], last_sub, keep_ref, recv_ref, (e1_ref, e2_ref), st_ref)
        c = split2(st_ref[...])

        def step(r, _, carry):
            p = (jnp.concatenate([h_ref[r], nh_ref[r]], 1), jnp.concatenate([l_ref[r], nl_ref[r]], 1))
            xh_ref[r], xl_ref[r] = split2(mm3(p, c) + w_ref[r, 0:1] * r_ref[r])
            return carry

        over_blocks(order, step)

    return call(
        body, [keep, recv, *edges, *phi, *phi_n, w, resid],
        [shape(3 * nm, k)] + [shape(order, k, dtype=BF16)] * 2, 18 * order * nm * k, [me], mb=10,
    )


def first_image(y, vec, phi_t, resid):
    order, k = y.shape
    nm = phi_t[0].shape[0]

    def body(y_ref, vec_ref, th_ref, tl_ref, r_ref, p_ref, m_ref):
        def step(at, _, carry):
            num, den, modal = carry
            p = vec_ref[at, 0:1] * y_ref[at]
            p_ref[at] = p
            num = num + jnp.sum(r_ref[at] * p, axis=0, keepdims=True)
            den = den + jnp.sum(p * p, axis=0, keepdims=True)
            return num, den, modal + mm3((th_ref[:, at], tl_ref[:, at]), split2(p))

        zero = jnp.zeros((1, k), F32)
        num, den, modal = over_blocks(order, step, (zero, zero, jnp.zeros((nm, k), F32)))
        row = lax.broadcasted_iota(jnp.int32, (SUMS, k), 0)
        m_ref[:nm] = modal
        m_ref[nm:] = jnp.where(row == 0, num, jnp.where(row == 1, den, 0.0))

    return call(body, [y, vec, *phi_t, resid], [shape(order, k), shape(nm + SUMS, k)], 6 * nm * order * k, mb=8)


def shared_image(me, last_sub, left, right, order, q_shared, y_shared, keep, recv, edges):
    two = y_shared.shape[0]
    half = two // 2
    nm, k = edges[0].shape
    n = 3 * nm

    def body(me_ref, lv_ref, rv_ref, qo_ref, qn_ref, y_ref, keep_ref, recv_ref, e1_ref, e2_ref, x_ref, d_ref, st_ref):
        rows = row_sides(me_ref, lv_ref, rv_ref)
        whole_stack(me_ref[0], last_sub, keep_ref, recv_ref, (e1_ref, e2_ref), st_ref)
        c = split2(st_ref[...])
        for i, ref in enumerate((x_ref, d_ref)):
            at = slice(i * half, (i + 1) * half)
            found = y_ref[at] + mm3(split2(jnp.concatenate([qo_ref[at], qn_ref[at]], 1)), c)
            slot = lax.broadcasted_iota(jnp.int32, (half, k), 0)
            ref[...] = jnp.where(slot < used_count(rows[i], order), found, 0.0)

    return call(
        body, [left, right, *q_shared, y_shared, keep, recv, *edges],
        [shape(half, k)] * 2 + [shape(3 * nm, k)], 6 * two * n * k, [me], mb=10,
    )


def local_image(q, y, vec, phi_t, stack, chain, restrict):
    order = y.shape[0]
    n, k = stack.shape
    nm = phi_t[0].shape[0]

    def body(qo_ref, qn_ref, y_ref, vec_ref, th_ref, tl_ref, st_ref, *refs):
        ins, outs = refs[:len(chain)], list(refs[len(chain):])
        c = split2(st_ref[...])
        p_ref = outs.pop(0)
        r_ref = outs.pop(0)

        def step(at, _, carry):
            num, den, modal = carry
            p = vec_ref[at, 0:1] * (y_ref[at] + mm3(split2(jnp.concatenate([qo_ref[at], qn_ref[at]], 1)), c))
            scale = ins[1][0:1]
            p = ins[2][at] - scale * p
            r = ins[0][at] - scale * ins[3][at]
            r_ref[at] = r
            p_ref[at] = p
            num = num + jnp.sum(r * p, axis=0, keepdims=True)
            den = den + jnp.sum(p * p, axis=0, keepdims=True)
            if restrict:
                modal = modal + mm3((th_ref[:, at], tl_ref[:, at]), split2(p))
            return num, den, modal

        zero = jnp.zeros((1, k), F32)
        num, den, modal = over_blocks(order, step, (zero, zero, jnp.zeros((nm, k), F32)))
        row = lax.broadcasted_iota(jnp.int32, (SUMS, k), 0)
        m_ref = outs.pop(0)
        m_ref[:nm] = modal
        m_ref[nm:] = jnp.where(row == 0, num, jnp.where(row == 1, den, 0.0))

    outs = [shape(order, k)] * 2 + [shape(nm + SUMS, k)]
    return call(
        body, [*q, y, vec, *phi_t, stack, *chain], outs,
        6 * order * n * k + 6 * nm * order * k, mb=12,
    )


def finish(phi_ts, own, recv, sent=(), chain=(), after=()):
    nm, two = phi_ts[0].shape
    k = own.shape[1]
    plain = len(sent) == 0

    def body(h_ref, l_ref, m_ref, *refs):
        ins, outs = refs[:2 + len(sent) + len(chain)], refs[2 + len(sent) + len(chain):]
        got = jnp.concatenate([ins[0][...], ins[1][...]], 0)
        cross = jnp.zeros((1, k), F32)
        if not plain:
            put = jnp.concatenate([ins[2][...], ins[3][...]], 0)
            if chain:
                scale = ins[4][0:1]
                got = ins[5][...] - scale * got
                put = ins[6][...] - scale * put
            outs[1][...] = got
            outs[2][...] = put
            cross = jnp.sum(got * put, axis=0, keepdims=True)
        outs[0][:nm] = m_ref[:nm] + mm3((h_ref[...], l_ref[...]), split2(got))
        row = lax.broadcasted_iota(jnp.int32, (SUMS, k), 0)
        base = m_ref[nm:] if not plain else jnp.zeros((SUMS, k), F32)
        outs[0][nm:] = base + jnp.where(row == 1, cross, 0.0)

    outs = [shape(nm + SUMS, k)] + ([] if plain else [shape(two, k)] * 2)
    return call(body, [*phi_ts, own, *recv, *sent, *chain], outs, 6 * nm * two * k, mb=10, after=after)


def assemble(onehot_t, p, got, w=None):
    order, two = onehot_t.shape
    k = p.shape[1]

    def body(gt_ref, p_ref, g_ref, *refs):
        parts = jnp.concatenate(split2(g_ref[...]), 0)

        def step(r, _, carry):
            gt = gt_ref[r]
            new = p_ref[r] + mm(jnp.concatenate([gt, gt], 1), parts)
            if w is None:
                refs[0][r] = new
            else:
                w_ref, i_ref, xh_ref, xl_ref = refs
                i_ref[r] = new
                xh_ref[r], xl_ref[r] = split2(w_ref[r, 0:1] * new)
            return carry

        over_blocks(order, step)

    ins = [onehot_t, p, got] + ([] if w is None else [w])
    outs = [shape(order, k)] + ([] if w is None else [shape(order, k, dtype=BF16)] * 2)
    return call(body, ins, outs, 4 * order * two * k, mb=10)


def directions(phi, phi_n, w, scales, resids, stacks):
    order, _ = phi[0].shape
    n, k = stacks[0].shape

    def body(h_ref, l_ref, nh_ref, nl_ref, w_ref, a0_ref, a1_ref, r0_ref, r1_ref, r2_ref,
             c0_ref, e0_ref, e1_ref, sol_ref, dir_ref):
        s0, s1 = a0_ref[0:1], a1_ref[0:1]
        c0 = c0_ref[...]
        c1 = c0 - s0 * e0_ref[...]
        first = s0 * c0 + s1 * c1
        c = split2(jnp.concatenate([first, c1 - s1 * e1_ref[...]], 1))

        def step(r, _, carry):
            p = (jnp.concatenate([h_ref[r], nh_ref[r]], 1), jnp.concatenate([l_ref[r], nl_ref[r]], 1))
            both = mm3(p, c)
            wc = w_ref[r, 0:1]
            sol_ref[r] = both[:, :k] + wc * (s0 * r0_ref[r] + s1 * r1_ref[r])
            dir_ref[r] = both[:, k:] + wc * r2_ref[r]
            return carry

        over_blocks(order, step)

    return call(
        body, [*phi, *phi_n, w, *scales, *resids, *stacks], [shape(order, k)] * 2,
        12 * order * n * k, mb=12,
    )


def swap_x(value):
    n = lax.axis_size("sub")
    return lax.ppermute(value, "sub", [(i, i ^ 1) for i in range(n)])


def swap_d(value):
    n = lax.axis_size(BOTH)
    pairs = [(i, i + 1) for i in range(1, n - 1, 2)]
    return lax.ppermute(value, BOTH, pairs + [(b, a) for a, b in pairs])


def coarse_rows(me, inverse, after):
    n = lax.axis_size("sub")
    same, other = halves(me, inverse, after)
    ring = [((i + 1) % n, (i + 2) % n) for i in range(0, n, 2)]
    at_d = lax.ppermute(other, "sub", ring + [(b, a) for a, b in ring])
    at_x = swap_x(other)
    at_z = lax.ppermute(same, "sub", [(i, (i - 2) % n if i % 2 == 0 else (i + 2) % n) for i in range(n)])
    return same, at_x, at_d, at_z


def direct(n):
    return n & (n - 1) == 0 and n <= 8


def parity_blocks(modal):
    n = lax.axis_size("sub")
    if not direct(n):
        groups = [list(range(p, n, 2)) for p in range(2)]
        every = lax.all_gather(modal, "sub", axis=0, axis_index_groups=groups)
        return [every[d] for d in range(n // 2)]
    return [modal] + [
        lax.ppermute(modal, "sub", [(i, i ^ (2 * d)) for i in range(n)]) for d in range(1, n // 2)
    ]


def over_axis(value, axis):
    n = lax.axis_size(axis)
    if n & (n - 1):
        return lax.psum(value, axis)
    step = 1
    while step < n:
        value = value + lax.ppermute(value, axis, [(i, i ^ step) for i in range(n)])
        step *= 2
    return value


def edge_blocks(block, partner):
    n, m = lax.axis_size("sub"), lax.axis_size("cluster")
    out = []
    for value, shift in ((block, 0), (partner, 1)):
        up = [(n * c + shift, n * (c + 1)) for c in range(m - 1)]
        down = [(n * (c + 1) + n - 1 - shift, n * c + n - 1) for c in range(m - 1)]
        out.append(lax.ppermute(value, BOTH, up + down))
    return out


def scale_of(sums):
    value = sums[0:1] / (sums[1:2] + 1e-06)
    return jnp.broadcast_to(value, (8, value.shape[1]))


def program(load, schur, modes, coarse_inverse, interface_rows, mode_count, left_rows, right_rows):
    nm = modes.shape[1]
    n_sub = lax.axis_size("sub")
    me = lax.axis_index("sub").astype(jnp.int32).reshape(1)

    to_x, to_d = gather_load(me, left_rows, right_rows, load)
    recv = swap_x(to_x), swap_d(to_d)
    onehot_t, p_hi, p_lo, pt_hi, pt_lo, vec, phi_x, phi_d, ts_hi, ts_lo, own = prepare(
        me, interface_rows, mode_count, left_rows, right_rows, schur, modes, load
    )
    phi, phi_t, phi_ts = (p_hi, p_lo), (pt_hi, pt_lo), (ts_hi, ts_lo)
    inverses = coarse_rows(me, coarse_inverse, (own,))
    phi_recv = swap_x(phi_x), swap_d(phi_d)
    (modal,) = finish(phi_ts, own, recv)
    blocks = parity_blocks(modal)
    q_own = schur_modes(schur, phi, (modal,))
    resid, w, n_hi, n_lo = extend(onehot_t, vec, load, recv, phi_recv)
    phi_n = (n_hi, n_lo)

    scales, resids, stacks = [], [resid], []
    for iteration in range(ITERS):
        first, last = iteration == 0, iteration == ITERS - 1
        send, keep, end_d, end_z = coarse(me, inverses, blocks, (q_own,) if first else (y,))
        got = swap_x(send)
        edges = edge_blocks(end_d, end_z)
        if first:
            stack, x_hi, x_lo = first_direction(me, n_sub - 1, keep, got, edges, phi, phi_n, w, resid)
            y = schur_apply(schur, (x_hi, x_lo))
            to_x, to_d = gather_shared(me, left_rows, right_rows, [y], True)
        else:
            (y_shared,) = gather_shared(me, left_rows, right_rows, [y])
            to_x, to_d, stack = shared_image(
                me, n_sub - 1, left_rows, right_rows, schur.shape[0], q_shared, y_shared, keep, got, edges
            )
        stacks.append(stack)
        recv = swap_x(to_x), swap_d(to_d)
        if first:
            p, own = first_image(y, vec, phi_t, resid)
            q = (q_own, schur_modes(schur, phi_n))
            q_shared = gather_shared(me, left_rows, right_rows, list(q))
            modal, far, near = finish(phi_ts, own, recv, (to_x, to_d), (), tuple(q_shared))
        else:
            scale = scale_of(over_axis(keep[3 * nm:] + got[3 * nm:], "cluster"))
            scales.append(scale)
            p, resid, own = local_image(q, y, vec, phi_t, stack, (resid, scale, p, image), not last)
            resids.append(resid)
            early = ()
            if last:
                early = sol, final = directions(phi, phi_n, w, scales, resids, stacks)
            modal, far, near = finish(phi_ts, own, recv, (to_x, to_d), (scale, far, near), early)
        if not last:
            blocks = parity_blocks(modal)
            image, x_hi, x_lo = assemble(onehot_t, p, far, w)
            y = schur_apply(schur, (x_hi, x_lo))
    sums = over_axis(over_axis(modal[nm:], "cluster"), "sub")
    (image,) = assemble(onehot_t, p, far)
    scale = scale_of(sums)[0:1]
    return sol + scale * final, resid - scale * image


def solution(mesh):
    rows = P(BOTH, None)
    return jax.shard_map(
        program,
        mesh=mesh,
        in_specs=(rows, rows, rows, rows, P(BOTH), P(BOTH), rows, rows),
        out_specs=(rows, rows),
        check_vma=False,
    )
```

time: 240 us -> 218 us (0.908)
  waiting for transfers between devices: 82 us -> 71.7 us
  local copies, waits for them, and re-layouts: 10.1 us -> 0.04 us
    ppermute x9, waiting for transfers between devices: 29.5 us -> 2.38 us  [parity_blocks(): lax.ppermute(modal, 'sub', [(i, i ^ 2 * d) for i in range(n)])]
    ppermute x9, waiting for transfers between devices: 39.1 us -> 51 us  [swap_x(): return lax.ppermute(value, 'sub', [(i, i ^ 1) for i in range(n)])]
    unnamed x20 -> x10, local copies, waits for them, and re-layouts: 10.1 us -> 0.03 us
    ppermute x9, starting transfers between devices: 13.1 us -> 4.45 us  [over_axis(): value = value + lax.ppermute(value, axis, [(i, i ^ step) for i in range(n)])]
    ppermute x9, starting transfers between devices: 13.4 us -> 19.5 us  [parity_blocks(): lax.ppermute(modal, 'sub', [(i, i ^ 2 * d) for i in range(n)])]
    ppermute x9, waiting for transfers between devices: 13.4 us -> 18.2 us  [over_axis(): value = value + lax.ppermute(value, axis, [(i, i ^ step) for i in range(n)])]
    ppermute x3 -> x6, starting transfers between devices: 4.29 us -> 6.15 us  [edge_blocks(): out.append(lax.ppermute(value, BOTH, up + down))]
    pallas_call x25 -> x30, Pallas kernels: 86.9 us -> 88.5 us  [call(): pl.pallas_call(run, in_specs=[pl.BlockSpec(memory_space=pltpu.SMEM)] * le...]
  transfers between devices with their start and end apart: 37 -> 40, of which waited for: 19 -> 19; matrix products, arithmetic and copies ran while one was open for 0% -> 0% of each run, Pallas kernels for 32% -> 31%
where the time goes in v3:
time: 218 us
  Pallas kernels  88.5 us (41%)
  waiting for transfers between devices  71.7 us (33%)
  starting transfers between devices  52.9 us (24%)
  between operations  2.5 us (1%)
  other arithmetic  2.39 us (1%)
    pallas_call x30, Pallas kernels, call(): pl.pallas_call(run, in_specs=[pl.BlockSpec(memory_space=pltpu.SMEM)] * le...  88.5 us
    ppermute x9, waiting for transfers between devices, swap_x(): return lax.ppermute(value, 'sub', [(i, i ^ 1) for i in range(n)])  51 us
    ppermute x9, starting transfers between devices, parity_blocks(): lax.ppermute(modal, 'sub', [(i, i ^ 2 * d) for i in range(n)])  19.5 us
    ppermute x9, waiting for transfers between devices, over_axis(): value = value + lax.ppermute(value, axis, [(i, i ^ step) for i in range(n)])  18.2 us
    ppermute x9, starting transfers between devices, swap_x(): return lax.ppermute(value, 'sub', [(i, i ^ 1) for i in range(n)])  11.3 us
    ppermute x6, starting transfers between devices, edge_blocks(): out.append(lax.ppermute(value, BOTH, up + down))  6.15 us
    ppermute x1, starting transfers between devices, coarse_rows(): at_d = lax.ppermute(other, 'sub', ring + [(b, a) for a, b in ring])  5.17 us
    ppermute x9, starting transfers between devices, over_axis(): value = value + lax.ppermute(value, axis, [(i, i ^ step) for i in range(n)])  4.45 us
  transfers between devices with their start and end apart: 40, of which 19 were waited for; matrix products, arithmetic and copies ran while one was open for 0% of the time, Pallas kernels for 31%

profile of v3, /device:TPU:0, one launch (start us, length us, event | category | flops | bytes accessed | tf_op | source)
XLA Modules:
  0.0 218.0 jit_solution(9356756554404946115)
XLA Ops:
  0.7 5.3 %shard_map.96 = (f32[384,256]{1,0:T(8,128)S(1)}, f32[384,256]{1,0:T(8,128)S(1)}) custom-call(s32[1]{0:T(128)} %bitcast.refs_0_, s32[1,384]{1,0:T(1,128)} %refs_1_.16, s32[1,384]{1,0:T(1,128)} %refs_2_.16, f32[1792,256]{1,0:T(8,128)} %refs_2_.10), custom_call_target="tpu_custom_call" | custom-call | bytes 786432 | tf_op jit(solution)/shard_map/pallas_call | solution.py:55
  6.0 3.0 %collective-permute-start = (f32[384,256]{1,0:T(8,128)S(1)}, f32[384,256]{1,0:T(8,128)S(1)}, u32[]{:S(2)}, u32[]{:S(2)}) collective-permute-start(f32[384,256]{1,0:T(8,128)S(1)} %get-tuple-element.74), channel_id=1, source_target_pairs={{0,1},{1,0},{2,3},{3,2},{4,5},{5,4},{6,7},{7,6},{8,9},{9,8},{10,11... | collective-permute-start | bytes 1179656 | tf_op jit(solution)/shard_map/ppermute | solution.py:546
  11.0 6.4 %shard_map.95 = (bf16[1792,768]{1,0:T(8,128)(2,1)S(1)}, bf16[1792,128]{1,0:T(8,128)(2,1)S(1)}, bf16[1792,128]{1,0:T(8,128)(2,1)S(1)}, bf16[128,1792]{1,0:T(8,128...) custom-call(s32[1]{0:T(128)} %bitcast.refs_0_, ...), custom_call_target="tpu_custom_call" | custom-call | flops 1056964608 | bytes 6458368 | tf_op jit(solution)/shard_map/pallas_call | solution.py:55
  17.5 5.2 %collective-permute-start.5 = (f32[128,512]{1,0:T(8,128)S(1)}, f32[128,512]{1,0:T(8,128)S(1)}, u32[]{:S(2)}, u32[]{:S(2)}) collective-permute-start(f32[128,512]{1,0:T(8,128)S(1)} %get-tuple-element.83), channel_id=1, source_target_pairs={{1,2},{3,4},{5,6},{7,0},{2,1},{4,3},{6,5},{0,7},{9,10},{11,12},{13... | collective-permute-start | bytes 786440 | tf_op jit(solution)/shard_map/ppermute | solution.py:559
  25.3 7.7 %collective-permute-done.refs_3_ = f32[384,256]{1,0:T(8,128)S(1)} collective-permute-done((f32[384,256]{1,0:T(8,128)S(1)}, f32[384,256]{1,0:T(8,128)S(1)}, u32[]{:S(2)}, u32[]{:S(2)}) %collective-permute-start) | collective-permute-done | bytes 393248 | tf_op jit(solution)/shard_map/ppermute | solution.py:546
  36.0 5.4 %collective-permute-start.9 = (f32[136,256]{1,0:T(8,128)S(1)}, f32[136,256]{1,0:T(8,128)S(1)}, u32[]{:S(2)}, u32[]{:S(2)}) collective-permute-start(f32[136,256]{1,0:T(8,128)S(1)} %shard_map.99.refs_3_.refs_5_), channel_id=1, source_target_pairs={{0,6},{1,7},{2,4},{3,5},{4,2},{5,3},{6,0},{7,1},{8,14},{9,15},{10,... | collective-permute-start | bytes 417800 | tf_op jit(solution)/shard_map/ppermute | solution.py:576
  47.8 5.2 %shard_map.100.refs_9_.refs_3_.refs_0_ = f32[1792,128]{1,0:T(8,128)S(1)} custom-call(f32[1792,1792]{1,0:T(8,128)S(1)} %copy-done, bf16[1792,128]{1,0:T(8,128)(2,1)S(1)} %get-tuple-element.70.refs_1_.refs_5_.refs_0_, bf16[1792,128]{1,0:T(8,128)(2,1)S(1)} %get-tuple-element.71.refs_2_.refs_6_.refs_1_, f32[136,256]{1,0:T(8,128)S(1)} %shard_map.99.refs_3_.refs_5_), custom_call_target="tpu_custom_call" | custom-call | flops 2466250752 | bytes 14680064 | tf_op jit(solution)/shard_map/pallas_call | solution.py:55
  55.3 3.1 %collective-permute-start.10 = (f32[392,256]{1,0:T(8,128)S(1)}, f32[392,256]{1,0:T(8,128)S(1)}, u32[]{:S(2)}, u32[]{:S(2)}) collective-permute-start(f32[392,256]{1,0:T(8,128)S(1)} %get-tuple-element.87), channel_id=1, source_target_pairs={{0,1},{1,0},{2,3},{3,2},{4,5},{5,4},{6,7},{7,6},{8,9},{9,8},{10,11... | collective-permute-start | bytes 1204232 | tf_op jit(solution)/shard_map/ppermute | solution.py:546
  60.6 4.6 %shard_map.97 = (f32[1792,256]{1,0:T(8,128)S(1)}, f32[1792,128]{1,0:T(8,128)S(1)}, bf16[1792,256]{1,0:T(8,128)(2,1)S(1)}, bf16[1792,256]{1,0:T(8,128)(2,1)S(1)}) custom-call(bf16[1792,768]{1,0:T(8,128)(2,1)S(1)} %get-tuple-element.72.refs_0_, f32[1792,128]{1,0:T(8,128)S(1)} %get-tuple-element.73.refs_1_.refs_3_, f32[1792,256]{1,0:T(8,128)S(1)} %copy-done.1, ...), custom_call_target="tpu_custom_call" | custom-call | flops 2818572288 | bytes 11296768 | tf_op jit(solution)/shard_map/pallas_call | solution.py:55
  70.4 5.1 %shard_map.103.refs_0_.refs_3_ = f32[1792,256]{1,0:T(8,128)S(1)} custom-call(f32[1792,1792]{1,0:T(8,128)S(1)} %copy-done, bf16[1792,256]{1,0:T(8,128)(2,1)S(1)} %get-tuple-element.91.refs_1_, bf16[1792,256]{1,0:T(8,128)(2,1)S(1)} %get-tuple-element.92.refs_2_), custom_call_target="tpu_custom_call" | custom-call | flops 4932501504 | bytes 16515072 | tf_op jit(solution)/shard_map/pallas_call | solution.py:55
  75.5 4.3 %shard_map.105 = (f32[384,256]{1,0:T(8,128)S(1)}, f32[384,256]{1,0:T(8,128)S(1)}) custom-call(s32[1]{0:T(128)} %bitcast.refs_0_, s32[1,384]{1,0:T(1,128)S(1)} %copy-done.3, s32[1,384]{1,0:T(1,128)S(1)} %copy-done.4, f32[1792,256]{1,0:T(8,128)S(1)} %shard_map.103.refs_0_.refs_3_), custom_call_target="tpu_custom_call" | custom-call | flops 2000000000 | bytes 2621440 | tf_op jit(solution)/shard_map/pallas_call | solution.py:55
  81.5 5.1 %shard_map.106.refs_4_.refs_1_ = f32[1792,256]{1,0:T(8,128)S(1)} custom-call(f32[1792,1792]{1,0:T(8,128)S(1)} %copy-done, bf16[1792,256]{1,0:T(8,128)(2,1)S(1)} %get-tuple-element.78.refs_7_.refs_1_.refs_2_, bf16[1792,256]{1,0:T(8,128)(2,1)S(1)} %get-tuple-element.79.refs_8_.refs_2_.refs_3_), custom_call_target="tpu_custom_call" | custom-call | flops 4932501504 | bytes 16515072 | tf_op jit(solution)/shard_map/pallas_call | solution.py:55
  86.7 4.3 %shard_map.107 = (f32[768,128]{1,0:T(8,128)S(1)}, f32[768,256]{1,0:T(8,128)S(1)}) custom-call(s32[1]{0:T(128)} %bitcast.refs_0_, s32[1,384]{1,0:T(1,128)S(1)} %copy-done.3, s32[1,384]{1,0:T(1,128)S(1)} %copy-done.4, f32[1792,128]{1,0:T(8,128)S(1)} %shard_map.100.refs_9_.refs_3_.refs_0_, f32[1792,256]{1,0:T(8,128)S(1)} %shard_map.106.refs_4_.refs_1_), custom_call_target="tpu_custom_call" | custom-call | flops 2000000000 | bytes 3932160 | tf_op jit(solution)/shard_map/pallas_call | solution.py:55
  93.3 6.8 %collective-permute-done.13.refs_3_ = f32[384,256]{1,0:T(8,128)S(1)} collective-permute-done((f32[384,256]{1,0:T(8,128)S(1)}, f32[384,256]{1,0:T(8,128)S(1)}, u32[]{:S(2)}, u32[]{:S(2)}) %collective-permute-start.13) | collective-permute-done | bytes 393248 | tf_op jit(solution)/shard_map/ppermute | solution.py:546
  100.7 4.3 %collective-permute-start.15 = (f32[136,256]{1,0:T(8,128)S(1)}, f32[136,256]{1,0:T(8,128)S(1)}, u32[]{:S(2)}, u32[]{:S(2)}) collective-permute-start(f32[136,256]{1,0:T(8,128)S(1)} %get-tuple-element.100.refs_5_), channel_id=1, source_target_pairs={{0,2},{1,3},{2,0},{3,1},{4,6},{5,7},{6,4},{7,5},{8,10},{9,11},{10,... | collective-permute-start | bytes 417800 | tf_op jit(solution)/shard_map/ppermute | solution.py:576
  105.0 2.8 %shard_map.109 = (f32[1792,256]{1,0:T(8,128)S(1)}, bf16[1792,256]{1,0:T(8,128)(2,1)S(1)}, bf16[1792,256]{1,0:T(8,128)(2,1)S(1)}) custom-call(bf16[1792,768]{1,0:T(8,128)(2,1)S(1)} %get-tuple-element.72.refs_0_, f32[1792,256]{1,0:T(8,128)S(1)} %get-tuple-element.101.refs_1_.refs_9_, f32[768,256]{1,0:T(8,128)S(1)} %get-tuple-element.102.refs_2_.refs_8_, ...), custom_call_target="tpu_custom_call" | custom-call | flops 1409286144 | bytes 9961472 | tf_op jit(solution)/shard_map/pallas_call | solution.py:55
  107.8 5.1 %shard_map.110.refs_9_.refs_3_.refs_2_ = f32[1792,256]{1,0:T(8,128)S(1)} custom-call(f32[1792,1792]{1,0:T(8,128)S(1)} %copy-done, bf16[1792,256]{1,0:T(8,128)(2,1)S(1)} %get-tuple-element.103.refs_1_, bf16[1792,256]{1,0:T(8,128)(2,1)S(1)} %get-tuple-element.104.refs_2_), custom_call_target="tpu_custom_call" | custom-call | flops 4932501504 | bytes 16515072 | tf_op jit(solution)/shard_map/pallas_call | solution.py:55
  116.5 3.8 %shard_map.112.refs_5_ = f32[768,256]{1,0:T(8,128)S(1)} custom-call(s32[1]{0:T(128)} %bitcast.refs_0_, s32[1,384]{1,0:T(1,128)S(1)} %copy-done.3, s32[1,384]{1,0:T(1,128)S(1)} %copy-done.4, f32[1792,256]{1,0:T(8,128)S(1)} %shard_map.110.refs_9_.refs_3_.refs_2_), custom_call_target="tpu_custom_call" | custom-call | flops 2000000000 | bytes 2621440 | tf_op jit(solution)/shard_map/pallas_call | solution.py:55
  120.4 6.1 %collective-permute-done.18.refs_7_ = f32[392,256]{1,0:T(8,128)S(1)} collective-permute-done((f32[392,256]{1,0:T(8,128)S(1)}, f32[392,256]{1,0:T(8,128)S(1)}, u32[]{:S(2)}, u32[]{:S(2)}) %collective-permute-start.18) | collective-permute-done | bytes 401440 | tf_op jit(solution)/shard_map/ppermute | solution.py:546
  135.8 4.6 %shard_map.114 = (f32[1792,256]{1,0:T(8,128)S(1)}, f32[1792,256]{1,0:T(8,128)S(1)}, f32[136,256]{1,0:T(8,128)S(1)}) custom-call(f32[1792,128]{1,0:T(8,128)S(1)} %shard_map.100.refs_9_.refs_3_.refs_0_, f32[1792,256]{1,0:T(8,128)S(1)} %shard_map.106.refs_4_.refs_1_, f32[1792,256]{1,0:T(8,128)S(1)} %shard_map.110.refs_9_.refs_3_.refs_2_, ...), custom_call_target="tpu_custom_call" | custom-call | flops 1409286144 | bytes 16138240 | tf_op jit(solution)/shard_map/pallas_call | solution.py:55
  140.4 7.0 %collective-permute-done.23.refs_3_ = f32[384,256]{1,0:T(8,128)S(1)} collective-permute-done((f32[384,256]{1,0:T(8,128)S(1)}, f32[384,256]{1,0:T(8,128)S(1)}, u32[]{:S(2)}, u32[]{:S(2)}) %collective-permute-start.23) | collective-permute-done | bytes 393248 | tf_op jit(solution)/shard_map/ppermute | solution.py:546
  148.4 4.0 %collective-permute-start.25 = (f32[136,256]{1,0:T(8,128)S(1)}, f32[136,256]{1,0:T(8,128)S(1)}, u32[]{:S(2)}, u32[]{:S(2)}) collective-permute-start(f32[136,256]{1,0:T(8,128)S(1)} %get-tuple-element.115.refs_5_), channel_id=1, source_target_pairs={{0,2},{1,3},{2,0},{3,1},{4,6},{5,7},{6,4},{7,5},{8,10},{9,11},{10,... | collective-permute-start | bytes 417800 | tf_op jit(solution)/shard_map/ppermute | solution.py:576
  152.3 2.8 %shard_map.116 = (f32[1792,256]{1,0:T(8,128)S(1)}, bf16[1792,256]{1,0:T(8,128)(2,1)S(1)}, bf16[1792,256]{1,0:T(8,128)(2,1)S(1)}) custom-call(bf16[1792,768]{1,0:T(8,128)(2,1)S(1)} %get-tuple-element.72.refs_0_, f32[1792,256]{1,0:T(8,128)S(1)} %get-tuple-element.116.refs_1_.refs_9_, f32[768,256]{1,0:T(8,128)S(1)} %get-tuple-element.117.refs_2_.refs_8_, ...), custom_call_target="tpu_custom_call" | custom-call | flops 1409286144 | bytes 9961472 | tf_op jit(solution)/shard_map/pallas_call | solution.py:55
  155.1 5.4 %shard_map.117.refs_9_.refs_3_.refs_2_ = f32[1792,256]{1,0:T(8,128)S(1)} custom-call(f32[1792,1792]{1,0:T(8,128)S(1)} %copy-done, bf16[1792,256]{1,0:T(8,128)(2,1)S(1)} %get-tuple-element.118.refs_1_, bf16[1792,256]{1,0:T(8,128)(2,1)S(1)} %get-tuple-element.119.refs_2_), custom_call_target="tpu_custom_call" | custom-call | flops 4932501504 | bytes 16515072 | tf_op jit(solution)/shard_map/pallas_call | solution.py:55
  164.1 9.0 %collective-permute-done.28.refs_7_ = f32[392,256]{1,0:T(8,128)S(1)} collective-permute-done((f32[392,256]{1,0:T(8,128)S(1)}, f32[392,256]{1,0:T(8,128)S(1)}, u32[]{:S(2)}, u32[]{:S(2)}) %collective-permute-start.28) | collective-permute-done | bytes 401440 | tf_op jit(solution)/shard_map/ppermute | solution.py:546
  173.2 3.8 %shard_map.119.refs_5_ = f32[768,256]{1,0:T(8,128)S(1)} custom-call(s32[1]{0:T(128)} %bitcast.refs_0_, s32[1,384]{1,0:T(1,128)S(1)} %copy-done.3, s32[1,384]{1,0:T(1,128)S(1)} %copy-done.4, f32[1792,256]{1,0:T(8,128)S(1)} %shard_map.117.refs_9_.refs_3_.refs_2_), custom_call_target="tpu_custom_call" | custom-call | flops 2000000000 | bytes 2621440 | tf_op jit(solution)/shard_map/pallas_call | solution.py:55
  180.8 2.7 %shard_map.121 = (f32[1792,256]{1,0:T(8,128)S(1)}, f32[1792,256]{1,0:T(8,128)S(1)}, f32[136,256]{1,0:T(8,128)S(1)}) custom-call(f32[1792,128]{1,0:T(8,128)S(1)} %shard_map.100.refs_9_.refs_3_.refs_0_, f32[1792,256]{1,0:T(8,128)S(1)} %shard_map.106.refs_4_.refs_1_, f32[1792,256]{1,0:T(8,128)S(1)} %shard_map.117.refs_9_.refs_3_.refs_2_, ...), custom_call_target="tpu_custom_call" | custom-call | flops 1409286144 | bytes 16138240 | tf_op jit(solution)/shard_map/pallas_call | solution.py:55
  183.5 3.8 %shard_map.122 = (f32[1792,256]{1,0:T(8,128)S(1)}, f32[1792,256]{1,0:T(8,128)S(1)}) custom-call(bf16[1792,128]{1,0:T(8,128)(2,1)S(1)} %get-tuple-element.70.refs_1_.refs_5_.refs_0_, bf16[1792,128]{1,0:T(8,128)(2,1)S(1)} %get-tuple-element.71.refs_2_.refs_6_.refs_1_, bf16[1792,256]{1,0:T(8,128)(2,1)S(1)} %get-tuple-element.78.refs_7_.refs_1_.refs_2_, ...), custom_call_target="tpu_custom_call" | custom-call | flops 2113929216 | bytes 14041088 | tf_op jit(solution)/shard_map/pallas_call | solution.py:55
  187.3 10.5 %collective-permute-done.33.refs_3_ = f32[384,256]{1,0:T(8,128)S(1)} collective-permute-done((f32[384,256]{1,0:T(8,128)S(1)}, f32[384,256]{1,0:T(8,128)S(1)}, u32[]{:S(2)}, u32[]{:S(2)}) %collective-permute-start.33) | collective-permute-done | bytes 393248 | tf_op jit(solution)/shard_map/ppermute | solution.py:546
  200.2 3.6 %collective-permute-done.36 = f32[8,256]{1,0:T(8,128)S(1)} collective-permute-done((f32[8,256]{1,0:T(8,128)S(1)}, f32[8,256]{1,0:T(8,128)S(1)}, u32[]{:S(2)}, u32[]{:S(2)}) %collective-permute-start.36) | collective-permute-done | bytes 8224 | tf_op jit(solution)/shard_map/ppermute | solution.py:586
  204.1 3.4 %collective-permute-done.37 = f32[8,256]{1,0:T(8,128)S(1)} collective-permute-done((f32[8,256]{1,0:T(8,128)S(1)}, f32[8,256]{1,0:T(8,128)S(1)}, u32[]{:S(2)}, u32[]{:S(2)}) %collective-permute-start.37) | collective-permute-done | bytes 8224 | tf_op jit(solution)/shard_map/ppermute | solution.py:586
  207.5 3.6 %collective-permute-done.38 = f32[8,256]{1,0:T(8,128)S(1)} collective-permute-done((f32[8,256]{1,0:T(8,128)S(1)}, f32[8,256]{1,0:T(8,128)S(1)}, u32[]{:S(2)}, u32[]{:S(2)}) %collective-permute-start.38) | collective-permute-done | bytes 8224 | tf_op jit(solution)/shard_map/ppermute | solution.py:586
  (106 shorter events, 57.6 us)
Async XLA Ops:
  6.0 27.0 %collective-permute-start = (f32[384,256]{1,0:T(8,128)S(1)}, f32[384,256]{1,0:T(8,128)S(1)}, u32[]{:S(2)}, u32[]{:S(2)}) collective-permute-start(f32[384,256]{1,0:T(8,128)S(1)} %get-tuple-element.74), channel_id=1, source_target_pairs={{0,1},{1,0},{2,3},{3,2},{4,5},{5,4},{6,7},{7,6},{8,9},{9,8},{10,11... | collective-permute-start | bytes 1179656 | tf_op jit(solution)/shard_map/ppermute | solution.py:546
  9.0 26.0 %collective-permute-start.1 = (f32[384,256]{1,0:T(8,128)S(1)}, f32[384,256]{1,0:T(8,128)S(1)}, u32[]{:S(2)}, u32[]{:S(2)}) collective-permute-start(f32[384,256]{1,0:T(8,128)S(1)} %get-tuple-element.75), channel_id=1, source_target_pairs={{1,2},{3,4},{5,6},{7,8},{9,10},{11,12},{13,14},{15,16},{17,18},{19... | collective-permute-start | bytes 1179656 | tf_op jit(solution)/shard_map/ppermute | solution.py:552
  17.5 18.5 %collective-permute-start.5 = (f32[128,512]{1,0:T(8,128)S(1)}, f32[128,512]{1,0:T(8,128)S(1)}, u32[]{:S(2)}, u32[]{:S(2)}) collective-permute-start(f32[128,512]{1,0:T(8,128)S(1)} %get-tuple-element.83), channel_id=1, source_target_pairs={{1,2},{3,4},{5,6},{7,0},{2,1},{4,3},{6,5},{0,7},{9,10},{11,12},{13... | collective-permute-start | bytes 786440 | tf_op jit(solution)/shard_map/ppermute | solution.py:559
  22.7 19.9 %collective-permute-start.4 = (f32[128,512]{1,0:T(8,128)S(1)}, f32[128,512]{1,0:T(8,128)S(1)}, u32[]{:S(2)}, u32[]{:S(2)}) collective-permute-start(f32[128,512]{1,0:T(8,128)S(1)} %get-tuple-element.83), channel_id=1, source_target_pairs={{0,1},{1,0},{2,3},{3,2},{4,5},{5,4},{6,7},{7,6},{8,9},{9,8},{10,11... | collective-permute-start | bytes 786440 | tf_op jit(solution)/shard_map/ppermute | solution.py:546
  22.7 22.5 %collective-permute-start.6 = (f32[128,512]{1,0:T(8,128)S(1)}, f32[128,512]{1,0:T(8,128)S(1)}, u32[]{:S(2)}, u32[]{:S(2)}) collective-permute-start(f32[128,512]{1,0:T(8,128)S(1)} %get-tuple-element.82.refs_1_), channel_id=1, source_target_pairs={{0,6},{1,3},{2,0},{3,5},{4,2},{5,7},{6,4},{7,1},{8,14},{9,11},{10,... | collective-permute-start | bytes 786440 | tf_op jit(solution)/shard_map/ppermute | solution.py:561
  33.0 27.6 %collective-permute-start.2 = (f32[408,128]{1,0:T(8,128)S(1)}, f32[408,128]{1,0:T(8,128)S(1)}, u32[]{:S(2)}, u32[]{:S(2)}) collective-permute-start(f32[408,128]{1,0:T(8,128)S(1)} %get-tuple-element.76), channel_id=1, source_target_pairs={{0,1},{1,0},{2,3},{3,2},{4,5},{5,4},{6,7},{7,6},{8,9},{9,8},{10,11... | collective-permute-start | bytes 626696 | tf_op jit(solution)/shard_map/ppermute | solution.py:546
  35.0 25.6 %collective-permute-start.3 = (f32[408,128]{1,0:T(8,128)S(1)}, f32[408,128]{1,0:T(8,128)S(1)}, u32[]{:S(2)}, u32[]{:S(2)}) collective-permute-start(f32[408,128]{1,0:T(8,128)S(1)} %get-tuple-element.77), channel_id=1, source_target_pairs={{1,2},{3,4},{5,6},{7,8},{9,10},{11,12},{13,14},{15,16},{17,18},{19... | collective-permute-start | bytes 626696 | tf_op jit(solution)/shard_map/ppermute | solution.py:552
  36.0 17.0 %collective-permute-start.9 = (f32[136,256]{1,0:T(8,128)S(1)}, f32[136,256]{1,0:T(8,128)S(1)}, u32[]{:S(2)}, u32[]{:S(2)}) collective-permute-start(f32[136,256]{1,0:T(8,128)S(1)} %shard_map.99.refs_3_.refs_5_), channel_id=1, source_target_pairs={{0,6},{1,7},{2,4},{3,5},{4,2},{5,3},{6,0},{7,1},{8,14},{9,15},{10,... | collective-permute-start | bytes 417800 | tf_op jit(solution)/shard_map/ppermute | solution.py:576
  42.6 12.0 %collective-permute-start.8 = (f32[136,256]{1,0:T(8,128)S(1)}, f32[136,256]{1,0:T(8,128)S(1)}, u32[]{:S(2)}, u32[]{:S(2)}) collective-permute-start(f32[136,256]{1,0:T(8,128)S(1)} %shard_map.99.refs_3_.refs_5_), channel_id=1, source_target_pairs={{0,4},{1,5},{2,6},{3,7},{4,0},{5,1},{6,2},{7,3},{8,12},{9,13},{10,... | collective-permute-start | bytes 417800 | tf_op jit(solution)/shard_map/ppermute | solution.py:576
  45.2 9.4 %collective-permute-start.7 = (f32[136,256]{1,0:T(8,128)S(1)}, f32[136,256]{1,0:T(8,128)S(1)}, u32[]{:S(2)}, u32[]{:S(2)}) collective-permute-start(f32[136,256]{1,0:T(8,128)S(1)} %shard_map.99.refs_3_.refs_5_), channel_id=1, source_target_pairs={{0,2},{1,3},{2,0},{3,1},{4,6},{5,7},{6,4},{7,5},{8,10},{9,11},{10,... | collective-permute-start | bytes 417800 | tf_op jit(solution)/shard_map/ppermute | solution.py:576
  55.3 12.6 %collective-permute-start.10 = (f32[392,256]{1,0:T(8,128)S(1)}, f32[392,256]{1,0:T(8,128)S(1)}, u32[]{:S(2)}, u32[]{:S(2)}) collective-permute-start(f32[392,256]{1,0:T(8,128)S(1)} %get-tuple-element.87), channel_id=1, source_target_pairs={{0,1},{1,0},{2,3},{3,2},{4,5},{5,4},{6,7},{7,6},{8,9},{9,8},{10,11... | collective-permute-start | bytes 1204232 | tf_op jit(solution)/shard_map/ppermute | solution.py:546
  58.4 6.8 %collective-permute-start.11 = (f32[128,256]{1,0:T(8,128)S(1)}, f32[128,256]{1,0:T(8,128)S(1)}, u32[]{:S(2)}, u32[]{:S(2)}) collective-permute-start(f32[128,256]{1,0:T(8,128)S(1)} %get-tuple-element.88), channel_id=1, source_target_pairs={{0,8},{8,16},{16,24},{15,7},{23,15},{31,23}} | collective-permute-start | bytes 393224 | tf_op jit(solution)/shard_map/ppermute | solution.py:597
  59.7 5.5 %collective-permute-start.12 = (f32[128,256]{1,0:T(8,128)S(1)}, f32[128,256]{1,0:T(8,128)S(1)}, u32[]{:S(2)}, u32[]{:S(2)}) collective-permute-start(f32[128,256]{1,0:T(8,128)S(1)} %get-tuple-element.89), channel_id=1, source_target_pairs={{1,8},{9,16},{17,24},{14,7},{22,15},{30,23}} | collective-permute-start | bytes 393224 | tf_op jit(solution)/shard_map/ppermute | solution.py:597
  79.8 20.2 %collective-permute-start.13 = (f32[384,256]{1,0:T(8,128)S(1)}, f32[384,256]{1,0:T(8,128)S(1)}, u32[]{:S(2)}, u32[]{:S(2)}) collective-permute-start(f32[384,256]{1,0:T(8,128)S(1)} %get-tuple-element.96.refs_5_), channel_id=1, source_target_pairs={{0,1},{1,0},{2,3},{3,2},{4,5},{5,4},{6,7},{7,6},{8,9},{9,8},{10,11... | collective-permute-start | bytes 1179656 | tf_op jit(solution)/shard_map/ppermute | solution.py:546
  80.9 19.2 %collective-permute-start.14 = (f32[384,256]{1,0:T(8,128)S(1)}, f32[384,256]{1,0:T(8,128)S(1)}, u32[]{:S(2)}, u32[]{:S(2)}) collective-permute-start(f32[384,256]{1,0:T(8,128)S(1)} %get-tuple-element.97.refs_6_), channel_id=1, source_target_pairs={{1,2},{3,4},{5,6},{7,8},{9,10},{11,12},{13,14},{15,16},{17,18},{19... | collective-permute-start | bytes 1179656 | tf_op jit(solution)/shard_map/ppermute | solution.py:552
  100.5 12.4 %collective-permute-start.17 = (f32[136,256]{1,0:T(8,128)S(1)}, f32[136,256]{1,0:T(8,128)S(1)}, u32[]{:S(2)}, u32[]{:S(2)}) collective-permute-start(f32[136,256]{1,0:T(8,128)S(1)} %get-tuple-element.100.refs_5_), channel_id=1, source_target_pairs={{0,6},{1,7},{2,4},{3,5},{4,2},{5,3},{6,0},{7,1},{8,14},{9,15},{10,... | collective-permute-start | bytes 417800 | tf_op jit(solution)/shard_map/ppermute | solution.py:576
  100.6 13.0 %collective-permute-start.16 = (f32[136,256]{1,0:T(8,128)S(1)}, f32[136,256]{1,0:T(8,128)S(1)}, u32[]{:S(2)}, u32[]{:S(2)}) collective-permute-start(f32[136,256]{1,0:T(8,128)S(1)} %get-tuple-element.100.refs_5_), channel_id=1, source_target_pairs={{0,4},{1,5},{2,6},{3,7},{4,0},{5,1},{6,2},{7,3},{8,12},{9,13},{10,... | collective-permute-start | bytes 417800 | tf_op jit(solution)/shard_map/ppermute | solution.py:576
  100.7 12.9 %collective-permute-start.15 = (f32[136,256]{1,0:T(8,128)S(1)}, f32[136,256]{1,0:T(8,128)S(1)}, u32[]{:S(2)}, u32[]{:S(2)}) collective-permute-start(f32[136,256]{1,0:T(8,128)S(1)} %get-tuple-element.100.refs_5_), channel_id=1, source_target_pairs={{0,2},{1,3},{2,0},{3,1},{4,6},{5,7},{6,4},{7,5},{8,10},{9,11},{10,... | collective-permute-start | bytes 417800 | tf_op jit(solution)/shard_map/ppermute | solution.py:576
  114.3 12.2 %collective-permute-start.18 = (f32[392,256]{1,0:T(8,128)S(1)}, f32[392,256]{1,0:T(8,128)S(1)}, u32[]{:S(2)}, u32[]{:S(2)}) collective-permute-start(f32[392,256]{1,0:T(8,128)S(1)} %get-tuple-element.106), channel_id=1, source_target_pairs={{0,1},{1,0},{2,3},{3,2},{4,5},{5,4},{6,7},{7,6},{8,9},{9,8},{10,11... | collective-permute-start | bytes 1204232 | tf_op jit(solution)/shard_map/ppermute | solution.py:546
  114.5 5.9 %collective-permute-start.21 = (f32[128,256]{1,0:T(8,128)S(1)}, f32[128,256]{1,0:T(8,128)S(1)}, u32[]{:S(2)}, u32[]{:S(2)}) collective-permute-start(f32[128,256]{1,0:T(8,128)S(1)} %get-tuple-element.107), channel_id=1, source_target_pairs={{0,8},{8,16},{16,24},{15,7},{23,15},{31,23}} | collective-permute-start | bytes 393224 | tf_op jit(solution)/shard_map/ppermute | solution.py:597
  115.9 4.5 %collective-permute-start.22 = (f32[128,256]{1,0:T(8,128)S(1)}, f32[128,256]{1,0:T(8,128)S(1)}, u32[]{:S(2)}, u32[]{:S(2)}) collective-permute-start(f32[128,256]{1,0:T(8,128)S(1)} %get-tuple-element.108), channel_id=1, source_target_pairs={{1,8},{9,16},{17,24},{14,7},{22,15},{30,23}} | collective-permute-start | bytes 393224 | tf_op jit(solution)/shard_map/ppermute | solution.py:597
  127.2 20.2 %collective-permute-start.23 = (f32[384,256]{1,0:T(8,128)S(1)}, f32[384,256]{1,0:T(8,128)S(1)}, u32[]{:S(2)}, u32[]{:S(2)}) collective-permute-start(f32[384,256]{1,0:T(8,128)S(1)} %get-tuple-element.112.refs_5_), channel_id=1, source_target_pairs={{0,1},{1,0},{2,3},{3,2},{4,5},{5,4},{6,7},{7,6},{8,9},{9,8},{10,11... | collective-permute-start | bytes 1179656 | tf_op jit(solution)/shard_map/ppermute | solution.py:546
  128.3 19.1 %collective-permute-start.24 = (f32[384,256]{1,0:T(8,128)S(1)}, f32[384,256]{1,0:T(8,128)S(1)}, u32[]{:S(2)}, u32[]{:S(2)}) collective-permute-start(f32[384,256]{1,0:T(8,128)S(1)} %get-tuple-element.113.refs_6_), channel_id=1, source_target_pairs={{1,2},{3,4},{5,6},{7,8},{9,10},{11,12},{13,14},{15,16},{17,18},{19... | collective-permute-start | bytes 1179656 | tf_op jit(solution)/shard_map/ppermute | solution.py:552
  147.9 12.7 %collective-permute-start.27 = (f32[136,256]{1,0:T(8,128)S(1)}, f32[136,256]{1,0:T(8,128)S(1)}, u32[]{:S(2)}, u32[]{:S(2)}) collective-permute-start(f32[136,256]{1,0:T(8,128)S(1)} %get-tuple-element.115.refs_5_), channel_id=1, source_target_pairs={{0,6},{1,7},{2,4},{3,5},{4,2},{5,3},{6,0},{7,1},{8,14},{9,15},{10,... | collective-permute-start | bytes 417800 | tf_op jit(solution)/shard_map/ppermute | solution.py:576
  148.4 12.3 %collective-permute-start.26 = (f32[136,256]{1,0:T(8,128)S(1)}, f32[136,256]{1,0:T(8,128)S(1)}, u32[]{:S(2)}, u32[]{:S(2)}) collective-permute-start(f32[136,256]{1,0:T(8,128)S(1)} %get-tuple-element.115.refs_5_), channel_id=1, source_target_pairs={{0,4},{1,5},{2,6},{3,7},{4,0},{5,1},{6,2},{7,3},{8,12},{9,13},{10,... | collective-permute-start | bytes 417800 | tf_op jit(solution)/shard_map/ppermute | solution.py:576
  148.4 12.3 %collective-permute-start.25 = (f32[136,256]{1,0:T(8,128)S(1)}, f32[136,256]{1,0:T(8,128)S(1)}, u32[]{:S(2)}, u32[]{:S(2)}) collective-permute-start(f32[136,256]{1,0:T(8,128)S(1)} %get-tuple-element.115.refs_5_), channel_id=1, source_target_pairs={{0,2},{1,3},{2,0},{3,1},{4,6},{5,7},{6,4},{7,5},{8,10},{9,11},{10,... | collective-permute-start | bytes 417800 | tf_op jit(solution)/shard_map/ppermute | solution.py:576
  161.3 11.9 %collective-permute-start.28 = (f32[392,256]{1,0:T(8,128)S(1)}, f32[392,256]{1,0:T(8,128)S(1)}, u32[]{:S(2)}, u32[]{:S(2)}) collective-permute-start(f32[392,256]{1,0:T(8,128)S(1)} %get-tuple-element.121), channel_id=1, source_target_pairs={{0,1},{1,0},{2,3},{3,2},{4,5},{5,4},{6,7},{7,6},{8,9},{9,8},{10,11... | collective-permute-start | bytes 1204232 | tf_op jit(solution)/shard_map/ppermute | solution.py:546
  162.2 14.9 %collective-permute-start.31 = (f32[128,256]{1,0:T(8,128)S(1)}, f32[128,256]{1,0:T(8,128)S(1)}, u32[]{:S(2)}, u32[]{:S(2)}) collective-permute-start(f32[128,256]{1,0:T(8,128)S(1)} %get-tuple-element.123), channel_id=1, source_target_pairs={{0,8},{8,16},{16,24},{15,7},{23,15},{31,23}} | collective-permute-start | bytes 393224 | tf_op jit(solution)/shard_map/ppermute | solution.py:597
  163.5 13.7 %collective-permute-start.32 = (f32[128,256]{1,0:T(8,128)S(1)}, f32[128,256]{1,0:T(8,128)S(1)}, u32[]{:S(2)}, u32[]{:S(2)}) collective-permute-start(f32[128,256]{1,0:T(8,128)S(1)} %get-tuple-element.124), channel_id=1, source_target_pairs={{1,8},{9,16},{17,24},{14,7},{22,15},{30,23}} | collective-permute-start | bytes 393224 | tf_op jit(solution)/shard_map/ppermute | solution.py:597
  177.8 20.0 %collective-permute-start.33 = (f32[384,256]{1,0:T(8,128)S(1)}, f32[384,256]{1,0:T(8,128)S(1)}, u32[]{:S(2)}, u32[]{:S(2)}) collective-permute-start(f32[384,256]{1,0:T(8,128)S(1)} %get-tuple-element.131.refs_5_), channel_id=1, source_target_pairs={{0,1},{1,0},{2,3},{3,2},{4,5},{5,4},{6,7},{7,6},{8,9},{9,8},{10,11... | collective-permute-start | bytes 1179656 | tf_op jit(solution)/shard_map/ppermute | solution.py:546
  177.9 19.9 %collective-permute-start.34 = (f32[384,256]{1,0:T(8,128)S(1)}, f32[384,256]{1,0:T(8,128)S(1)}, u32[]{:S(2)}, u32[]{:S(2)}) collective-permute-start(f32[384,256]{1,0:T(8,128)S(1)} %get-tuple-element.132.refs_6_), channel_id=1, source_target_pairs={{1,2},{3,4},{5,6},{7,8},{9,10},{11,12},{13,14},{15,16},{17,18},{19... | collective-permute-start | bytes 1179656 | tf_op jit(solution)/shard_map/ppermute | solution.py:552
  211.1 4.5 %collective-permute-start.39 = (f32[8,256]{1,0:T(8,128)S(1)}, f32[8,256]{1,0:T(8,128)S(1)}, u32[]{:S(2)}, u32[]{:S(2)}) collective-permute-start(f32[8,256]{1,0:T(8,128)S(1)} %add.56), channel_id=1, source_target_pairs={{0,4},{1,5},{2,6},{3,7},{4,0},{5,1},{6,2},{7,3},{8,12},{9,13},{10,... | collective-permute-start | bytes 24584 | tf_op jit(solution)/shard_map/ppermute | solution.py:586
  (13 other events, 97.7 us)

commit v4 on v3

--- a/solution.py
+++ b/solution.py
@@ -142,27 +142,36 @@
     )
 
 
-def gather_shared(me, left, right, fields, masked=False):
+def gather_shared(me, left, right, fields):
     half = left.shape[1]
     order = fields[0].shape[0]
     n = len(fields)
 
     def body(me_ref, l_ref, r_ref, *refs):
         rows = (l_ref, r_ref)
+        pairs = list(zip(refs[:n], refs[n:]))
 
         def work(first, second):
-            for side, index in enumerate((first, second)):
-                outs = refs[n + side::2] if masked else refs[n:]
-                pairs = list(zip(refs[:n], outs))
-                copy_rows(pairs, rows[index], 0 if masked else side * half, half, order, masked)
+            copy_rows(pairs, rows[first], 0, half, order, False)
+            copy_rows(pairs, rows[second], half, half, order, False)
 
         by_parity(me_ref[0], work)
 
-    if masked:
-        outs = [shape(half, f.shape[1]) for f in fields for _ in range(2)]
-    else:
-        outs = [shape(2 * half, f.shape[1]) for f in fields]
+    outs = [shape(2 * half, f.shape[1]) for f in fields]
     return call(body, fields, outs, 2e9, [me, left, right], mb=4)
+
+
+def gather_side(me, left, right, field, side):
+    half = left.shape[1]
+    order, k = field.shape
+
+    def body(me_ref, l_ref, r_ref, field_ref, out_ref):
+        rows = (l_ref, r_ref)
+        by_parity(
+            me_ref[0], lambda *sides: copy_rows([(field_ref, out_ref)], rows[sides[side]], 0, half, order, True)
+        )
+
+    return call(body, [field], [shape(half, k)], 1e9, [me, left, right], mb=4)[0]
 
 
 def halves(me, inverse, after):
@@ -555,11 +564,14 @@
 def coarse_rows(me, inverse, after):
     n = lax.axis_size("sub")
     same, other = halves(me, inverse, after)
+    at_z = lax.ppermute(same, "sub", [(i, (i - 2) % n if i % 2 == 0 else (i + 2) % n) for i in range(n)])
+    return same, at_z, other
+
+
+def coarse_partners(other):
+    n = lax.axis_size("sub")
     ring = [((i + 1) % n, (i + 2) % n) for i in range(0, n, 2)]
-    at_d = lax.ppermute(other, "sub", ring + [(b, a) for a, b in ring])
-    at_x = swap_x(other)
-    at_z = lax.ppermute(same, "sub", [(i, (i - 2) % n if i % 2 == 0 else (i + 2) % n) for i in range(n)])
-    return same, at_x, at_d, at_z
+    return swap_x(other), lax.ppermute(other, "sub", ring + [(b, a) for a, b in ring])
 
 
 def direct(n):
@@ -588,6 +600,25 @@
     return value
 
 
+def over_mesh(value):
+    m, n = lax.axis_size("cluster"), lax.axis_size("sub")
+    if m < 4 or n < 2 or m & (m - 1) or n & (n - 1):
+        return over_axis(over_axis(value, "cluster"), "sub")
+    value = value + lax.ppermute(value, "cluster", [(i, i ^ 1) for i in range(m)])
+    here = [(c, s) for c in range(m) for s in range(n)]
+    round_of = [(2, 0), (0, 1), (2, 1)]
+    got = [
+        lax.ppermute(value, BOTH, [(c * n + s, (c ^ up) * n + (s ^ along)) for c, s in here])
+        for up, along in round_of
+    ]
+    value = (value + got[0]) + (got[1] + got[2])
+    for step in [4 << i for i in range(8) if 4 << i < m]:
+        value = value + lax.ppermute(value, "cluster", [(i, i ^ step) for i in range(m)])
+    for step in [2 << i for i in range(8) if 2 << i < n]:
+        value = value + lax.ppermute(value, "sub", [(i, i ^ step) for i in range(n)])
+    return value
+
+
 def edge_blocks(block, partner):
     n, m = lax.axis_size("sub"), lax.axis_size("cluster")
     out = []
@@ -614,31 +645,35 @@
         me, interface_rows, mode_count, left_rows, right_rows, schur, modes, load
     )
     phi, phi_t, phi_ts = (p_hi, p_lo), (pt_hi, pt_lo), (ts_hi, ts_lo)
-    inverses = coarse_rows(me, coarse_inverse, (own,))
+    rows_own, rows_z, other = coarse_rows(me, coarse_inverse, (own,))
+    q_own = schur_modes(schur, phi)
+    (modal,) = finish(phi_ts, own, recv, after=(q_own,))
+    blocks = parity_blocks(modal)
+    other, _ = lax.optimization_barrier((other, modal))
+    inverses = (rows_own, *coarse_partners(other), rows_z)
     phi_recv = swap_x(phi_x), swap_d(phi_d)
-    (modal,) = finish(phi_ts, own, recv)
-    blocks = parity_blocks(modal)
-    q_own = schur_modes(schur, phi, (modal,))
     resid, w, n_hi, n_lo = extend(onehot_t, vec, load, recv, phi_recv)
     phi_n = (n_hi, n_lo)
 
     scales, resids, stacks = [], [resid], []
     for iteration in range(ITERS):
         first, last = iteration == 0, iteration == ITERS - 1
-        send, keep, end_d, end_z = coarse(me, inverses, blocks, (q_own,) if first else (y,))
+        send, keep, end_d, end_z = coarse(me, inverses, blocks, () if first else (y,))
         got = swap_x(send)
         edges = edge_blocks(end_d, end_z)
         if first:
             stack, x_hi, x_lo = first_direction(me, n_sub - 1, keep, got, edges, phi, phi_n, w, resid)
             y = schur_apply(schur, (x_hi, x_lo))
-            to_x, to_d = gather_shared(me, left_rows, right_rows, [y], True)
+            to_x = gather_side(me, left_rows, right_rows, y, 0)
+            to_d = gather_side(me, left_rows, right_rows, y, 1)
         else:
             (y_shared,) = gather_shared(me, left_rows, right_rows, [y])
             to_x, to_d, stack = shared_image(
                 me, n_sub - 1, left_rows, right_rows, schur.shape[0], q_shared, y_shared, keep, got, edges
             )
         stacks.append(stack)
-        recv = swap_x(to_x), swap_d(to_d)
+        from_x = swap_x(to_x)
+        recv = from_x, swap_d(to_d)
         if first:
             p, own = first_image(y, vec, phi_t, resid)
             q = (q_own, schur_modes(schur, phi_n))
@@ -657,7 +692,7 @@
             blocks = parity_blocks(modal)
             image, x_hi, x_lo = assemble(onehot_t, p, far, w)
             y = schur_apply(schur, (x_hi, x_lo))
-    sums = over_axis(over_axis(modal[nm:], "cluster"), "sub")
+    sums = over_mesh(modal[nm:])
     (image,) = assemble(onehot_t, p, far)
     scale = scale_of(sums)[0:1]
     return sol + scale * final, resid - scale * image

time: 218 us -> 218 us (level)
  waiting for transfers between devices: 71.7 us -> 68.2 us
  starting transfers between devices: 52.9 us -> 55.6 us
    ppermute x9 -> x4, waiting for transfers between devices: 18.2 us -> 4.59 us  [over_axis(): value = value + lax.ppermute(value, axis, [(i, i ^ step) for i in range(n)])]
    ppermute x9, waiting for transfers between devices: 2.38 us -> 15.1 us  [parity_blocks(): lax.ppermute(modal, 'sub', [(i, i ^ 2 * d) for i in range(n)])]
    ppermute x9, waiting for transfers between devices: 51 us -> 41.3 us  [swap_x(): return lax.ppermute(value, 'sub', [(i, i ^ 1) for i in range(n)])]
    ppermute x1 -> x7, waiting for transfers between devices: 0.01 us -> 7.22 us  [the longest x2 4.43 us: over_mesh(): lax.ppermute(value, 'sub', [(i, i ^ step) for i in range(n)])]
    ppermute x9, starting transfers between devices: 19.5 us -> 13.3 us  [parity_blocks(): lax.ppermute(modal, 'sub', [(i, i ^ 2 * d) for i in range(n)])]
    ppermute x9, starting transfers between devices: 11.3 us -> 14.6 us  [swap_x(): return lax.ppermute(value, 'sub', [(i, i ^ 1) for i in range(n)])]
    ppermute x1, starting transfers between devices: 2.65 us -> 5.35 us  [coarse_rows(): lax.ppermute(same, 'sub', [(i, (i - 2) % n if i % 2 == 0 else (i + 2) % n...]
    ppermute x1 -> x7, starting transfers between devices: 5.17 us -> 6.83 us  [the longest x3 3.49 us: over_mesh(): lax.ppermute(value, BOTH, [(c * n + s, (c ^ up) * n + (s ^ along)) for c,...]
  transfers between devices with their start and end apart: 40 -> 41, of which waited for: 19 -> 18; matrix products, arithmetic and copies ran while one was open for 0% -> 0% of each run, Pallas kernels for 31% -> 31%
where the time goes in v4:
time: 218 us
  Pallas kernels  89 us (41%)
  waiting for transfers between devices  68.2 us (31%)
  starting transfers between devices  55.6 us (26%)
  between operations  2.52 us (1%)
  other arithmetic  2.38 us (1%)
    pallas_call x31, Pallas kernels, call(): pl.pallas_call(run, in_specs=[pl.BlockSpec(memory_space=pltpu.SMEM)] * le...  89 us
    ppermute x9, waiting for transfers between devices, swap_x(): return lax.ppermute(value, 'sub', [(i, i ^ 1) for i in range(n)])  41.3 us
    ppermute x9, waiting for transfers between devices, parity_blocks(): lax.ppermute(modal, 'sub', [(i, i ^ 2 * d) for i in range(n)])  15.1 us
    ppermute x9, starting transfers between devices, swap_x(): return lax.ppermute(value, 'sub', [(i, i ^ 1) for i in range(n)])  14.6 us
    ppermute x9, starting transfers between devices, parity_blocks(): lax.ppermute(modal, 'sub', [(i, i ^ 2 * d) for i in range(n)])  13.3 us
    ppermute x6, starting transfers between devices, edge_blocks(): out.append(lax.ppermute(value, BOTH, up + down))  6.85 us
    ppermute x1, starting transfers between devices, coarse_rows(): lax.ppermute(same, 'sub', [(i, (i - 2) % n if i % 2 == 0 else (i + 2) % n...  5.35 us
    ppermute x4, starting transfers between devices, over_axis(): value = value + lax.ppermute(value, axis, [(i, i ^ step) for i in range(n)])  5.04 us
  transfers between devices with their start and end apart: 41, of which 18 were waited for; matrix products, arithmetic and copies ran while one was open for 0% of the time, Pallas kernels for 31%

profile of v4, /device:TPU:0, one launch (start us, length us, event | category | flops | bytes accessed | tf_op | source)
XLA Modules:
  0.0 217.8 jit_solution(11475367846938353084)
XLA Ops:
  0.7 5.3 %shard_map.96 = (f32[384,256]{1,0:T(8,128)S(1)}, f32[384,256]{1,0:T(8,128)S(1)}) custom-call(s32[1]{0:T(128)} %bitcast.refs_0_, s32[1,384]{1,0:T(1,128)} %refs_1_.18, s32[1,384]{1,0:T(1,128)} %refs_2_.18, f32[1792,256]{1,0:T(8,128)} %refs_2_.11), custom_call_target="tpu_custom_call" | custom-call | bytes 786432 | tf_op jit(solution)/shard_map/pallas_call | solution.py:55
  6.0 3.0 %collective-permute-start = (f32[384,256]{1,0:T(8,128)S(1)}, f32[384,256]{1,0:T(8,128)S(1)}, u32[]{:S(2)}, u32[]{:S(2)}) collective-permute-start(f32[384,256]{1,0:T(8,128)S(1)} %get-tuple-element.73), channel_id=1, source_target_pairs={{0,1},{1,0},{2,3},{3,2},{4,5},{5,4},{6,7},{7,6},{8,9},{9,8},{10,11... | collective-permute-start | bytes 1179656 | tf_op jit(solution)/shard_map/ppermute | solution.py:555
  11.0 6.4 %shard_map.95 = (bf16[1792,768]{1,0:T(8,128)(2,1)S(1)}, bf16[1792,128]{1,0:T(8,128)(2,1)S(1)}, bf16[1792,128]{1,0:T(8,128)(2,1)S(1)}, bf16[128,1792]{1,0:T(8,128...) custom-call(s32[1]{0:T(128)} %bitcast.refs_0_, ...), custom_call_target="tpu_custom_call" | custom-call | flops 1056964608 | bytes 6458368 | tf_op jit(solution)/shard_map/pallas_call | solution.py:55
  17.5 5.3 %collective-permute-start.6 = (f32[128,512]{1,0:T(8,128)S(1)}, f32[128,512]{1,0:T(8,128)S(1)}, u32[]{:S(2)}, u32[]{:S(2)}) collective-permute-start(f32[128,512]{1,0:T(8,128)S(1)} %get-tuple-element.81.refs_1_), channel_id=1, source_target_pairs={{0,6},{1,3},{2,0},{3,5},{4,2},{5,7},{6,4},{7,1},{8,14},{9,11},{10,... | collective-permute-start | bytes 786440 | tf_op jit(solution)/shard_map/ppermute | solution.py:567
  22.8 5.2 %shard_map.99.refs_5_.refs_3_.refs_0_ = f32[1792,128]{1,0:T(8,128)S(1)} custom-call(f32[1792,1792]{1,0:T(8,128)S(1)} %copy-done, bf16[1792,128]{1,0:T(8,128)(2,1)S(1)} %get-tuple-element.69.refs_1_.refs_5_.refs_0_, bf16[1792,128]{1,0:T(8,128)(2,1)S(1)} %get-tuple-element.70.refs_2_.refs_6_.refs_1_), custom_call_target="tpu_custom_call" | custom-call | flops 2466250752 | bytes 14680064 | tf_op jit(solution)/shard_map/pallas_call | solution.py:55
  30.7 3.1 %collective-permute-start.9 = (f32[136,256]{1,0:T(8,128)S(1)}, f32[136,256]{1,0:T(8,128)S(1)}, u32[]{:S(2)}, u32[]{:S(2)}) collective-permute-start(f32[136,256]{1,0:T(8,128)S(1)} %shard_map.100.refs_5_), channel_id=1, source_target_pairs={{0,6},{1,7},{2,4},{3,5},{4,2},{5,3},{6,0},{7,1},{8,14},{9,15},{10,... | collective-permute-start | bytes 417800 | tf_op jit(solution)/shard_map/ppermute | solution.py:588
  35.1 7.3 %collective-permute-done.9.refs_8_ = f32[136,256]{1,0:T(8,128)S(1)} collective-permute-done((f32[136,256]{1,0:T(8,128)S(1)}, f32[136,256]{1,0:T(8,128)S(1)}, u32[]{:S(2)}, u32[]{:S(2)}) %collective-permute-start.9) | collective-permute-done | bytes 139296 | tf_op jit(solution)/shard_map/ppermute | solution.py:588
  44.0 4.7 %collective-permute-done.8.refs_7_ = f32[136,256]{1,0:T(8,128)S(1)} collective-permute-done((f32[136,256]{1,0:T(8,128)S(1)}, f32[136,256]{1,0:T(8,128)S(1)}, u32[]{:S(2)}, u32[]{:S(2)}) %collective-permute-start.8) | collective-permute-done | bytes 139296 | tf_op jit(solution)/shard_map/ppermute | solution.py:588
  50.0 4.0 %collective-permute-start.10 = (f32[392,256]{1,0:T(8,128)S(1)}, f32[392,256]{1,0:T(8,128)S(1)}, u32[]{:S(2)}, u32[]{:S(2)}) collective-permute-start(f32[392,256]{1,0:T(8,128)S(1)} %get-tuple-element.87), channel_id=1, source_target_pairs={{0,1},{1,0},{2,3},{3,2},{4,5},{5,4},{6,7},{7,6},{8,9},{9,8},{10,11... | collective-permute-start | bytes 1204232 | tf_op jit(solution)/shard_map/ppermute | solution.py:555
  56.3 4.6 %shard_map.97 = (f32[1792,256]{1,0:T(8,128)S(1)}, f32[1792,128]{1,0:T(8,128)S(1)}, bf16[1792,256]{1,0:T(8,128)(2,1)S(1)}, bf16[1792,256]{1,0:T(8,128)(2,1)S(1)}) custom-call(bf16[1792,768]{1,0:T(8,128)(2,1)S(1)} %get-tuple-element.71.refs_0_, f32[1792,128]{1,0:T(8,128)S(1)} %get-tuple-element.72.refs_1_.refs_3_, f32[1792,256]{1,0:T(8,128)S(1)} %copy-done.1, ...), custom_call_target="tpu_custom_call" | custom-call | flops 2818572288 | bytes 11296768 | tf_op jit(solution)/shard_map/pallas_call | solution.py:55
  61.0 6.3 %collective-permute-done.10.refs_2_ = f32[392,256]{1,0:T(8,128)S(1)} collective-permute-done((f32[392,256]{1,0:T(8,128)S(1)}, f32[392,256]{1,0:T(8,128)S(1)}, u32[]{:S(2)}, u32[]{:S(2)}) %collective-permute-start.10) | collective-permute-done | bytes 401440 | tf_op jit(solution)/shard_map/ppermute | solution.py:555
  69.7 5.1 %shard_map.103.refs_0_.refs_3_ = f32[1792,256]{1,0:T(8,128)S(1)} custom-call(f32[1792,1792]{1,0:T(8,128)S(1)} %copy-done, bf16[1792,256]{1,0:T(8,128)(2,1)S(1)} %get-tuple-element.91.refs_1_, bf16[1792,256]{1,0:T(8,128)(2,1)S(1)} %get-tuple-element.92.refs_2_), custom_call_target="tpu_custom_call" | custom-call | flops 4932501504 | bytes 16515072 | tf_op jit(solution)/shard_map/pallas_call | solution.py:55
  82.9 5.1 %shard_map.107.refs_4_.refs_1_ = f32[1792,256]{1,0:T(8,128)S(1)} custom-call(f32[1792,1792]{1,0:T(8,128)S(1)} %copy-done, bf16[1792,256]{1,0:T(8,128)(2,1)S(1)} %get-tuple-element.77.refs_7_.refs_1_.refs_2_, bf16[1792,256]{1,0:T(8,128)(2,1)S(1)} %get-tuple-element.78.refs_8_.refs_2_.refs_3_), custom_call_target="tpu_custom_call" | custom-call | flops 4932501504 | bytes 16515072 | tf_op jit(solution)/shard_map/pallas_call | solution.py:55
  88.0 4.3 %shard_map.108 = (f32[768,128]{1,0:T(8,128)S(1)}, f32[768,256]{1,0:T(8,128)S(1)}) custom-call(s32[1]{0:T(128)} %bitcast.refs_0_, s32[1,384]{1,0:T(1,128)S(1)} %copy-done.3, s32[1,384]{1,0:T(1,128)S(1)} %copy-done.4, f32[1792,128]{1,0:T(8,128)S(1)} %shard_map.99.refs_5_.refs_3_.refs_0_, f32[1792,256]{1,0:T(8,128)S(1)} %shard_map.107.refs_4_.refs_1_), custom_call_target="tpu_custom_call" | custom-call | flops 2000000000 | bytes 3932160 | tf_op jit(solution)/shard_map/pallas_call | solution.py:55
  94.6 5.1 %collective-permute-done.13.refs_3_ = f32[384,256]{1,0:T(8,128)S(1)} collective-permute-done((f32[384,256]{1,0:T(8,128)S(1)}, f32[384,256]{1,0:T(8,128)S(1)}, u32[]{:S(2)}, u32[]{:S(2)}) %collective-permute-start.13) | collective-permute-done | bytes 393248 | tf_op jit(solution)/shard_map/ppermute | solution.py:555
  100.2 3.2 %collective-permute-start.17 = (f32[136,256]{1,0:T(8,128)S(1)}, f32[136,256]{1,0:T(8,128)S(1)}, u32[]{:S(2)}, u32[]{:S(2)}) collective-permute-start(f32[136,256]{1,0:T(8,128)S(1)} %get-tuple-element.98.refs_5_), channel_id=1, source_target_pairs={{0,6},{1,7},{2,4},{3,5},{4,2},{5,3},{6,0},{7,1},{8,14},{9,15},{10,... | collective-permute-start | bytes 417800 | tf_op jit(solution)/shard_map/ppermute | solution.py:588
  104.7 2.8 %shard_map.110 = (f32[1792,256]{1,0:T(8,128)S(1)}, bf16[1792,256]{1,0:T(8,128)(2,1)S(1)}, bf16[1792,256]{1,0:T(8,128)(2,1)S(1)}) custom-call(bf16[1792,768]{1,0:T(8,128)(2,1)S(1)} %get-tuple-element.71.refs_0_, f32[1792,256]{1,0:T(8,128)S(1)} %get-tuple-element.99.refs_1_.refs_9_, f32[768,256]{1,0:T(8,128)S(1)} %get-tuple-element.100.refs_2_.refs_8_, ...), custom_call_target="tpu_custom_call" | custom-call | flops 1409286144 | bytes 9961472 | tf_op jit(solution)/shard_map/pallas_call | solution.py:55
  107.4 5.1 %shard_map.111.refs_9_.refs_3_.refs_2_ = f32[1792,256]{1,0:T(8,128)S(1)} custom-call(f32[1792,1792]{1,0:T(8,128)S(1)} %copy-done, bf16[1792,256]{1,0:T(8,128)(2,1)S(1)} %get-tuple-element.101.refs_1_, bf16[1792,256]{1,0:T(8,128)(2,1)S(1)} %get-tuple-element.102.refs_2_), custom_call_target="tpu_custom_call" | custom-call | flops 4932501504 | bytes 16515072 | tf_op jit(solution)/shard_map/pallas_call | solution.py:55
  118.9 3.8 %shard_map.113.refs_5_ = f32[768,256]{1,0:T(8,128)S(1)} custom-call(s32[1]{0:T(128)} %bitcast.refs_0_, s32[1,384]{1,0:T(1,128)S(1)} %copy-done.3, s32[1,384]{1,0:T(1,128)S(1)} %copy-done.4, f32[1792,256]{1,0:T(8,128)S(1)} %shard_map.111.refs_9_.refs_3_.refs_2_), custom_call_target="tpu_custom_call" | custom-call | flops 2000000000 | bytes 2621440 | tf_op jit(solution)/shard_map/pallas_call | solution.py:55
  122.8 4.5 %collective-permute-done.18.refs_7_ = f32[392,256]{1,0:T(8,128)S(1)} collective-permute-done((f32[392,256]{1,0:T(8,128)S(1)}, f32[392,256]{1,0:T(8,128)S(1)}, u32[]{:S(2)}, u32[]{:S(2)}) %collective-permute-start.18) | collective-permute-done | bytes 401440 | tf_op jit(solution)/shard_map/ppermute | solution.py:555
  130.4 2.9 %collective-permute-start.19 = (f32[8,256]{1,0:T(8,128)S(1)}, f32[8,256]{1,0:T(8,128)S(1)}, u32[]{:S(2)}, u32[]{:S(2)}) collective-permute-start(f32[8,256]{1,0:T(8,128)S(1)} %slice_add_fusion.1), channel_id=1, source_target_pairs={{0,8},{8,0},{16,24},{24,16},{1,9},{9,1},{17,25},{25,17},{2,10},{10... | collective-permute-start | bytes 24584 | tf_op jit(solution)/shard_map/ppermute | solution.py:598
  137.9 4.5 %shard_map.115 = (f32[1792,256]{1,0:T(8,128)S(1)}, f32[1792,256]{1,0:T(8,128)S(1)}, f32[136,256]{1,0:T(8,128)S(1)}) custom-call(f32[1792,128]{1,0:T(8,128)S(1)} %shard_map.99.refs_5_.refs_3_.refs_0_, f32[1792,256]{1,0:T(8,128)S(1)} %shard_map.107.refs_4_.refs_1_, f32[1792,256]{1,0:T(8,128)S(1)} %shard_map.111.refs_9_.refs_3_.refs_2_, ...), custom_call_target="tpu_custom_call" | custom-call | flops 1409286144 | bytes 16138240 | tf_op jit(solution)/shard_map/pallas_call | solution.py:55
  142.4 5.3 %collective-permute-done.23.refs_3_ = f32[384,256]{1,0:T(8,128)S(1)} collective-permute-done((f32[384,256]{1,0:T(8,128)S(1)}, f32[384,256]{1,0:T(8,128)S(1)}, u32[]{:S(2)}, u32[]{:S(2)}) %collective-permute-start.23) | collective-permute-done | bytes 393248 | tf_op jit(solution)/shard_map/ppermute | solution.py:555
  152.7 2.8 %shard_map.117 = (f32[1792,256]{1,0:T(8,128)S(1)}, bf16[1792,256]{1,0:T(8,128)(2,1)S(1)}, bf16[1792,256]{1,0:T(8,128)(2,1)S(1)}) custom-call(bf16[1792,768]{1,0:T(8,128)(2,1)S(1)} %get-tuple-element.71.refs_0_, f32[1792,256]{1,0:T(8,128)S(1)} %get-tuple-element.114.refs_1_.refs_9_, f32[768,256]{1,0:T(8,128)S(1)} %get-tuple-element.115.refs_2_.refs_8_, ...), custom_call_target="tpu_custom_call" | custom-call | flops 1409286144 | bytes 9961472 | tf_op jit(solution)/shard_map/pallas_call | solution.py:55
  155.4 5.4 %shard_map.118.refs_9_.refs_3_.refs_2_ = f32[1792,256]{1,0:T(8,128)S(1)} custom-call(f32[1792,1792]{1,0:T(8,128)S(1)} %copy-done, bf16[1792,256]{1,0:T(8,128)(2,1)S(1)} %get-tuple-element.116.refs_1_, bf16[1792,256]{1,0:T(8,128)(2,1)S(1)} %get-tuple-element.117.refs_2_), custom_call_target="tpu_custom_call" | custom-call | flops 4932501504 | bytes 16515072 | tf_op jit(solution)/shard_map/pallas_call | solution.py:55
  165.6 9.5 %collective-permute-done.28.refs_7_ = f32[392,256]{1,0:T(8,128)S(1)} collective-permute-done((f32[392,256]{1,0:T(8,128)S(1)}, f32[392,256]{1,0:T(8,128)S(1)}, u32[]{:S(2)}, u32[]{:S(2)}) %collective-permute-start.28) | collective-permute-done | bytes 401440 | tf_op jit(solution)/shard_map/ppermute | solution.py:555
  175.1 3.8 %shard_map.120.refs_5_ = f32[768,256]{1,0:T(8,128)S(1)} custom-call(s32[1]{0:T(128)} %bitcast.refs_0_, s32[1,384]{1,0:T(1,128)S(1)} %copy-done.3, s32[1,384]{1,0:T(1,128)S(1)} %copy-done.4, f32[1792,256]{1,0:T(8,128)S(1)} %shard_map.118.refs_9_.refs_3_.refs_2_), custom_call_target="tpu_custom_call" | custom-call | flops 2000000000 | bytes 2621440 | tf_op jit(solution)/shard_map/pallas_call | solution.py:55
  182.7 2.7 %shard_map.122 = (f32[1792,256]{1,0:T(8,128)S(1)}, f32[1792,256]{1,0:T(8,128)S(1)}, f32[136,256]{1,0:T(8,128)S(1)}) custom-call(f32[1792,128]{1,0:T(8,128)S(1)} %shard_map.99.refs_5_.refs_3_.refs_0_, f32[1792,256]{1,0:T(8,128)S(1)} %shard_map.107.refs_4_.refs_1_, f32[1792,256]{1,0:T(8,128)S(1)} %shard_map.118.refs_9_.refs_3_.refs_2_, ...), custom_call_target="tpu_custom_call" | custom-call | flops 1409286144 | bytes 16138240 | tf_op jit(solution)/shard_map/pallas_call | solution.py:55
  185.4 3.8 %shard_map.123 = (f32[1792,256]{1,0:T(8,128)S(1)}, f32[1792,256]{1,0:T(8,128)S(1)}) custom-call(bf16[1792,128]{1,0:T(8,128)(2,1)S(1)} %get-tuple-element.69.refs_1_.refs_5_.refs_0_, bf16[1792,128]{1,0:T(8,128)(2,1)S(1)} %get-tuple-element.70.refs_2_.refs_6_.refs_1_, bf16[1792,256]{1,0:T(8,128)(2,1)S(1)} %get-tuple-element.77.refs_7_.refs_1_.refs_2_, ...), custom_call_target="tpu_custom_call" | custom-call | flops 2113929216 | bytes 14041088 | tf_op jit(solution)/shard_map/pallas_call | solution.py:55
  189.2 10.6 %collective-permute-done.33.refs_3_ = f32[384,256]{1,0:T(8,128)S(1)} collective-permute-done((f32[384,256]{1,0:T(8,128)S(1)}, f32[384,256]{1,0:T(8,128)S(1)}, u32[]{:S(2)}, u32[]{:S(2)}) %collective-permute-start.33) | collective-permute-done | bytes 393248 | tf_op jit(solution)/shard_map/ppermute | solution.py:555
  207.3 3.6 %collective-permute-done.39 = f32[8,256]{1,0:T(8,128)S(1)} collective-permute-done((f32[8,256]{1,0:T(8,128)S(1)}, f32[8,256]{1,0:T(8,128)S(1)}, u32[]{:S(2)}, u32[]{:S(2)}) %collective-permute-start.39) | collective-permute-done | bytes 8224 | tf_op jit(solution)/shard_map/ppermute | solution.py:618
  211.9 2.7 %shard_map.125 = f32[1792,256]{1,0:T(8,128)S(1)} custom-call(bf16[1792,768]{1,0:T(8,128)(2,1)S(1)} %get-tuple-element.71.refs_0_, f32[1792,256]{1,0:T(8,128)S(1)} %get-tuple-element.134.refs_1_, f32[768,256]{1,0:T(8,128)S(1)} %get-tuple-element.135.refs_2_), custom_call_target="tpu_custom_call" | custom-call | flops 1409286144 | bytes 7208960 | tf_op jit(solution)/shard_map/pallas_call | solution.py:55
  (108 shorter events, 63.3 us)
Async XLA Ops:
  6.0 22.1 %collective-permute-start = (f32[384,256]{1,0:T(8,128)S(1)}, f32[384,256]{1,0:T(8,128)S(1)}, u32[]{:S(2)}, u32[]{:S(2)}) collective-permute-start(f32[384,256]{1,0:T(8,128)S(1)} %get-tuple-element.73), channel_id=1, source_target_pairs={{0,1},{1,0},{2,3},{3,2},{4,5},{5,4},{6,7},{7,6},{8,9},{9,8},{10,11... | collective-permute-start | bytes 1179656 | tf_op jit(solution)/shard_map/ppermute | solution.py:555
  9.0 19.1 %collective-permute-start.1 = (f32[384,256]{1,0:T(8,128)S(1)}, f32[384,256]{1,0:T(8,128)S(1)}, u32[]{:S(2)}, u32[]{:S(2)}) collective-permute-start(f32[384,256]{1,0:T(8,128)S(1)} %get-tuple-element.74), channel_id=1, source_target_pairs={{1,2},{3,4},{5,6},{7,8},{9,10},{11,12},{13,14},{15,16},{17,18},{19... | collective-permute-start | bytes 1179656 | tf_op jit(solution)/shard_map/ppermute | solution.py:561
  17.5 16.3 %collective-permute-start.6 = (f32[128,512]{1,0:T(8,128)S(1)}, f32[128,512]{1,0:T(8,128)S(1)}, u32[]{:S(2)}, u32[]{:S(2)}) collective-permute-start(f32[128,512]{1,0:T(8,128)S(1)} %get-tuple-element.81.refs_1_), channel_id=1, source_target_pairs={{0,6},{1,3},{2,0},{3,5},{4,2},{5,7},{6,4},{7,1},{8,14},{9,11},{10,... | collective-permute-start | bytes 786440 | tf_op jit(solution)/shard_map/ppermute | solution.py:567
  28.4 20.9 %collective-permute-start.5 = (f32[128,512]{1,0:T(8,128)S(1)}, f32[128,512]{1,0:T(8,128)S(1)}, u32[]{:S(2)}, u32[]{:S(2)}) collective-permute-start(f32[128,512]{1,0:T(8,128)S(1)} %get-tuple-element.85), channel_id=1, source_target_pairs={{1,2},{3,4},{5,6},{7,0},{2,1},{4,3},{6,5},{0,7},{9,10},{11,12},{13... | collective-permute-start | bytes 786440 | tf_op jit(solution)/shard_map/ppermute | solution.py:574
  30.7 18.6 %collective-permute-start.4 = (f32[128,512]{1,0:T(8,128)S(1)}, f32[128,512]{1,0:T(8,128)S(1)}, u32[]{:S(2)}, u32[]{:S(2)}) collective-permute-start(f32[128,512]{1,0:T(8,128)S(1)} %get-tuple-element.85), channel_id=1, source_target_pairs={{0,1},{1,0},{2,3},{3,2},{4,5},{5,4},{6,7},{7,6},{8,9},{9,8},{10,11... | collective-permute-start | bytes 786440 | tf_op jit(solution)/shard_map/ppermute | solution.py:555
  30.7 11.7 %collective-permute-start.9 = (f32[136,256]{1,0:T(8,128)S(1)}, f32[136,256]{1,0:T(8,128)S(1)}, u32[]{:S(2)}, u32[]{:S(2)}) collective-permute-start(f32[136,256]{1,0:T(8,128)S(1)} %shard_map.100.refs_5_), channel_id=1, source_target_pairs={{0,6},{1,7},{2,4},{3,5},{4,2},{5,3},{6,0},{7,1},{8,14},{9,15},{10,... | collective-permute-start | bytes 417800 | tf_op jit(solution)/shard_map/ppermute | solution.py:588
  33.8 14.9 %collective-permute-start.8 = (f32[136,256]{1,0:T(8,128)S(1)}, f32[136,256]{1,0:T(8,128)S(1)}, u32[]{:S(2)}, u32[]{:S(2)}) collective-permute-start(f32[136,256]{1,0:T(8,128)S(1)} %shard_map.100.refs_5_), channel_id=1, source_target_pairs={{0,4},{1,5},{2,6},{3,7},{4,0},{5,1},{6,2},{7,3},{8,12},{9,13},{10,... | collective-permute-start | bytes 417800 | tf_op jit(solution)/shard_map/ppermute | solution.py:588
  33.8 15.6 %collective-permute-start.7 = (f32[136,256]{1,0:T(8,128)S(1)}, f32[136,256]{1,0:T(8,128)S(1)}, u32[]{:S(2)}, u32[]{:S(2)}) collective-permute-start(f32[136,256]{1,0:T(8,128)S(1)} %shard_map.100.refs_5_), channel_id=1, source_target_pairs={{0,2},{1,3},{2,0},{3,1},{4,6},{5,7},{6,4},{7,5},{8,10},{9,11},{10,... | collective-permute-start | bytes 417800 | tf_op jit(solution)/shard_map/ppermute | solution.py:588
  42.4 13.9 %collective-permute-start.2 = (f32[408,128]{1,0:T(8,128)S(1)}, f32[408,128]{1,0:T(8,128)S(1)}, u32[]{:S(2)}, u32[]{:S(2)}) collective-permute-start(f32[408,128]{1,0:T(8,128)S(1)} %get-tuple-element.75), channel_id=1, source_target_pairs={{0,1},{1,0},{2,3},{3,2},{4,5},{5,4},{6,7},{7,6},{8,9},{9,8},{10,11... | collective-permute-start | bytes 626696 | tf_op jit(solution)/shard_map/ppermute | solution.py:555
  48.6 7.7 %collective-permute-start.3 = (f32[408,128]{1,0:T(8,128)S(1)}, f32[408,128]{1,0:T(8,128)S(1)}, u32[]{:S(2)}, u32[]{:S(2)}) collective-permute-start(f32[408,128]{1,0:T(8,128)S(1)} %get-tuple-element.76), channel_id=1, source_target_pairs={{1,2},{3,4},{5,6},{7,8},{9,10},{11,12},{13,14},{15,16},{17,18},{19... | collective-permute-start | bytes 626696 | tf_op jit(solution)/shard_map/ppermute | solution.py:561
  50.0 17.3 %collective-permute-start.10 = (f32[392,256]{1,0:T(8,128)S(1)}, f32[392,256]{1,0:T(8,128)S(1)}, u32[]{:S(2)}, u32[]{:S(2)}) collective-permute-start(f32[392,256]{1,0:T(8,128)S(1)} %get-tuple-element.87), channel_id=1, source_target_pairs={{0,1},{1,0},{2,3},{3,2},{4,5},{5,4},{6,7},{7,6},{8,9},{9,8},{10,11... | collective-permute-start | bytes 1204232 | tf_op jit(solution)/shard_map/ppermute | solution.py:555
  54.0 7.0 %collective-permute-start.11 = (f32[128,256]{1,0:T(8,128)S(1)}, f32[128,256]{1,0:T(8,128)S(1)}, u32[]{:S(2)}, u32[]{:S(2)}) collective-permute-start(f32[128,256]{1,0:T(8,128)S(1)} %get-tuple-element.88), channel_id=1, source_target_pairs={{0,8},{8,16},{16,24},{15,7},{23,15},{31,23}} | collective-permute-start | bytes 393224 | tf_op jit(solution)/shard_map/ppermute | solution.py:628
  55.5 5.5 %collective-permute-start.12 = (f32[128,256]{1,0:T(8,128)S(1)}, f32[128,256]{1,0:T(8,128)S(1)}, u32[]{:S(2)}, u32[]{:S(2)}) collective-permute-start(f32[128,256]{1,0:T(8,128)S(1)} %get-tuple-element.89), channel_id=1, source_target_pairs={{1,8},{9,16},{17,24},{14,7},{22,15},{30,23}} | collective-permute-start | bytes 393224 | tf_op jit(solution)/shard_map/ppermute | solution.py:628
  79.8 20.0 %collective-permute-start.13 = (f32[384,256]{1,0:T(8,128)S(1)}, f32[384,256]{1,0:T(8,128)S(1)}, u32[]{:S(2)}, u32[]{:S(2)}) collective-permute-start(f32[384,256]{1,0:T(8,128)S(1)} %shard_map.105.refs_5_), channel_id=1, source_target_pairs={{0,1},{1,0},{2,3},{3,2},{4,5},{5,4},{6,7},{7,6},{8,9},{9,8},{10,11... | collective-permute-start | bytes 1179656 | tf_op jit(solution)/shard_map/ppermute | solution.py:555
  82.2 17.5 %collective-permute-start.14 = (f32[384,256]{1,0:T(8,128)S(1)}, f32[384,256]{1,0:T(8,128)S(1)}, u32[]{:S(2)}, u32[]{:S(2)}) collective-permute-start(f32[384,256]{1,0:T(8,128)S(1)} %shard_map.106.refs_6_), channel_id=1, source_target_pairs={{1,2},{3,4},{5,6},{7,8},{9,10},{11,12},{13,14},{15,16},{17,18},{19... | collective-permute-start | bytes 1179656 | tf_op jit(solution)/shard_map/ppermute | solution.py:561
  100.2 12.4 %collective-permute-start.17 = (f32[136,256]{1,0:T(8,128)S(1)}, f32[136,256]{1,0:T(8,128)S(1)}, u32[]{:S(2)}, u32[]{:S(2)}) collective-permute-start(f32[136,256]{1,0:T(8,128)S(1)} %get-tuple-element.98.refs_5_), channel_id=1, source_target_pairs={{0,6},{1,7},{2,4},{3,5},{4,2},{5,3},{6,0},{7,1},{8,14},{9,15},{10,... | collective-permute-start | bytes 417800 | tf_op jit(solution)/shard_map/ppermute | solution.py:588
  103.4 10.9 %collective-permute-start.16 = (f32[136,256]{1,0:T(8,128)S(1)}, f32[136,256]{1,0:T(8,128)S(1)}, u32[]{:S(2)}, u32[]{:S(2)}) collective-permute-start(f32[136,256]{1,0:T(8,128)S(1)} %get-tuple-element.98.refs_5_), channel_id=1, source_target_pairs={{0,4},{1,5},{2,6},{3,7},{4,0},{5,1},{6,2},{7,3},{8,12},{9,13},{10,... | collective-permute-start | bytes 417800 | tf_op jit(solution)/shard_map/ppermute | solution.py:588
  103.4 10.9 %collective-permute-start.15 = (f32[136,256]{1,0:T(8,128)S(1)}, f32[136,256]{1,0:T(8,128)S(1)}, u32[]{:S(2)}, u32[]{:S(2)}) collective-permute-start(f32[136,256]{1,0:T(8,128)S(1)} %get-tuple-element.98.refs_5_), channel_id=1, source_target_pairs={{0,2},{1,3},{2,0},{3,1},{4,6},{5,7},{6,4},{7,5},{8,10},{9,11},{10,... | collective-permute-start | bytes 417800 | tf_op jit(solution)/shard_map/ppermute | solution.py:588
  115.0 12.2 %collective-permute-start.18 = (f32[392,256]{1,0:T(8,128)S(1)}, f32[392,256]{1,0:T(8,128)S(1)}, u32[]{:S(2)}, u32[]{:S(2)}) collective-permute-start(f32[392,256]{1,0:T(8,128)S(1)} %get-tuple-element.104), channel_id=1, source_target_pairs={{0,1},{1,0},{2,3},{3,2},{4,5},{5,4},{6,7},{7,6},{8,9},{9,8},{10,11... | collective-permute-start | bytes 1204232 | tf_op jit(solution)/shard_map/ppermute | solution.py:555
  116.5 6.2 %collective-permute-start.21 = (f32[128,256]{1,0:T(8,128)S(1)}, f32[128,256]{1,0:T(8,128)S(1)}, u32[]{:S(2)}, u32[]{:S(2)}) collective-permute-start(f32[128,256]{1,0:T(8,128)S(1)} %get-tuple-element.105), channel_id=1, source_target_pairs={{0,8},{8,16},{16,24},{15,7},{23,15},{31,23}} | collective-permute-start | bytes 393224 | tf_op jit(solution)/shard_map/ppermute | solution.py:628
  128.0 19.7 %collective-permute-start.23 = (f32[384,256]{1,0:T(8,128)S(1)}, f32[384,256]{1,0:T(8,128)S(1)}, u32[]{:S(2)}, u32[]{:S(2)}) collective-permute-start(f32[384,256]{1,0:T(8,128)S(1)} %get-tuple-element.110.refs_5_), channel_id=1, source_target_pairs={{0,1},{1,0},{2,3},{3,2},{4,5},{5,4},{6,7},{7,6},{8,9},{9,8},{10,11... | collective-permute-start | bytes 1179656 | tf_op jit(solution)/shard_map/ppermute | solution.py:555
  129.5 18.2 %collective-permute-start.24 = (f32[384,256]{1,0:T(8,128)S(1)}, f32[384,256]{1,0:T(8,128)S(1)}, u32[]{:S(2)}, u32[]{:S(2)}) collective-permute-start(f32[384,256]{1,0:T(8,128)S(1)} %get-tuple-element.111.refs_6_), channel_id=1, source_target_pairs={{1,2},{3,4},{5,6},{7,8},{9,10},{11,12},{13,14},{15,16},{17,18},{19... | collective-permute-start | bytes 1179656 | tf_op jit(solution)/shard_map/ppermute | solution.py:561
  148.2 12.7 %collective-permute-start.27 = (f32[136,256]{1,0:T(8,128)S(1)}, f32[136,256]{1,0:T(8,128)S(1)}, u32[]{:S(2)}, u32[]{:S(2)}) collective-permute-start(f32[136,256]{1,0:T(8,128)S(1)} %get-tuple-element.113.refs_5_), channel_id=1, source_target_pairs={{0,6},{1,7},{2,4},{3,5},{4,2},{5,3},{6,0},{7,1},{8,14},{9,15},{10,... | collective-permute-start | bytes 417800 | tf_op jit(solution)/shard_map/ppermute | solution.py:588
  150.4 11.9 %collective-permute-start.26 = (f32[136,256]{1,0:T(8,128)S(1)}, f32[136,256]{1,0:T(8,128)S(1)}, u32[]{:S(2)}, u32[]{:S(2)}) collective-permute-start(f32[136,256]{1,0:T(8,128)S(1)} %get-tuple-element.113.refs_5_), channel_id=1, source_target_pairs={{0,4},{1,5},{2,6},{3,7},{4,0},{5,1},{6,2},{7,3},{8,12},{9,13},{10,... | collective-permute-start | bytes 417800 | tf_op jit(solution)/shard_map/ppermute | solution.py:588
  150.4 11.9 %collective-permute-start.25 = (f32[136,256]{1,0:T(8,128)S(1)}, f32[136,256]{1,0:T(8,128)S(1)}, u32[]{:S(2)}, u32[]{:S(2)}) collective-permute-start(f32[136,256]{1,0:T(8,128)S(1)} %get-tuple-element.113.refs_5_), channel_id=1, source_target_pairs={{0,2},{1,3},{2,0},{3,1},{4,6},{5,7},{6,4},{7,5},{8,10},{9,11},{10,... | collective-permute-start | bytes 417800 | tf_op jit(solution)/shard_map/ppermute | solution.py:588
  162.9 12.2 %collective-permute-start.28 = (f32[392,256]{1,0:T(8,128)S(1)}, f32[392,256]{1,0:T(8,128)S(1)}, u32[]{:S(2)}, u32[]{:S(2)}) collective-permute-start(f32[392,256]{1,0:T(8,128)S(1)} %get-tuple-element.119), channel_id=1, source_target_pairs={{0,1},{1,0},{2,3},{3,2},{4,5},{5,4},{6,7},{7,6},{8,9},{9,8},{10,11... | collective-permute-start | bytes 1204232 | tf_op jit(solution)/shard_map/ppermute | solution.py:555
  163.4 15.7 %collective-permute-start.31 = (f32[128,256]{1,0:T(8,128)S(1)}, f32[128,256]{1,0:T(8,128)S(1)}, u32[]{:S(2)}, u32[]{:S(2)}) collective-permute-start(f32[128,256]{1,0:T(8,128)S(1)} %get-tuple-element.121), channel_id=1, source_target_pairs={{0,8},{8,16},{16,24},{15,7},{23,15},{31,23}} | collective-permute-start | bytes 393224 | tf_op jit(solution)/shard_map/ppermute | solution.py:628
  164.9 14.2 %collective-permute-start.32 = (f32[128,256]{1,0:T(8,128)S(1)}, f32[128,256]{1,0:T(8,128)S(1)}, u32[]{:S(2)}, u32[]{:S(2)}) collective-permute-start(f32[128,256]{1,0:T(8,128)S(1)} %get-tuple-element.122), channel_id=1, source_target_pairs={{1,8},{9,16},{17,24},{14,7},{22,15},{30,23}} | collective-permute-start | bytes 393224 | tf_op jit(solution)/shard_map/ppermute | solution.py:628
  179.8 20.0 %collective-permute-start.33 = (f32[384,256]{1,0:T(8,128)S(1)}, f32[384,256]{1,0:T(8,128)S(1)}, u32[]{:S(2)}, u32[]{:S(2)}) collective-permute-start(f32[384,256]{1,0:T(8,128)S(1)} %get-tuple-element.129.refs_5_), channel_id=1, source_target_pairs={{0,1},{1,0},{2,3},{3,2},{4,5},{5,4},{6,7},{7,6},{8,9},{9,8},{10,11... | collective-permute-start | bytes 1179656 | tf_op jit(solution)/shard_map/ppermute | solution.py:555
  179.9 19.9 %collective-permute-start.34 = (f32[384,256]{1,0:T(8,128)S(1)}, f32[384,256]{1,0:T(8,128)S(1)}, u32[]{:S(2)}, u32[]{:S(2)}) collective-permute-start(f32[384,256]{1,0:T(8,128)S(1)} %get-tuple-element.130.refs_6_), channel_id=1, source_target_pairs={{1,2},{3,4},{5,6},{7,8},{9,10},{11,12},{13,14},{15,16},{17,18},{19... | collective-permute-start | bytes 1179656 | tf_op jit(solution)/shard_map/ppermute | solution.py:561
  202.1 4.5 %collective-permute-start.38 = (f32[8,256]{1,0:T(8,128)S(1)}, f32[8,256]{1,0:T(8,128)S(1)}, u32[]{:S(2)}, u32[]{:S(2)}) collective-permute-start(f32[8,256]{1,0:T(8,128)S(1)} %slice_add_fusion.5), channel_id=1, source_target_pairs={{0,17},{1,16},{2,19},{3,18},{4,21},{5,20},{6,23},{7,22},{8,25},{9,... | collective-permute-start | bytes 24584 | tf_op jit(solution)/shard_map/ppermute | solution.py:611
  210.9 4.5 %collective-permute-start.40 = (f32[8,256]{1,0:T(8,128)S(1)}, f32[8,256]{1,0:T(8,128)S(1)}, u32[]{:S(2)}, u32[]{:S(2)}) collective-permute-start(f32[8,256]{1,0:T(8,128)S(1)} %add.60), channel_id=1, source_target_pairs={{0,4},{1,5},{2,6},{3,7},{4,0},{5,1},{6,2},{7,3},{8,12},{9,13},{10,... | collective-permute-start | bytes 24584 | tf_op jit(solution)/shard_map/ppermute | solution.py:618
  (14 other events, 98.9 us)

commit v5 on v4

--- a/solution.py
+++ b/solution.py
@@ -87,13 +87,13 @@
     group = 8 if half % 8 == 0 else 1
 
     def step(j, _):
-        for u in range(group):
-            slot = j * group + u
-            row = index_ref[0, slot]
-            at = jnp.minimum(row, order - 1)
-            for source, out in pairs:
-                value = source[pl.ds(at, 1), :]
-                out[pl.ds(base + slot, 1), :] = jnp.where(row < order, value, 0.0) if masked else value
+        rows = [index_ref[0, j * group + u] for u in range(group)]
+        for source, out in pairs:
+            values = [source[pl.ds(jnp.minimum(row, order - 1), 1), :] for row in rows]
+            if masked:
+                values = [jnp.where(row < order, value, 0.0) for row, value in zip(rows, values)]
+            for u, value in enumerate(values):
+                out[pl.ds(base + j * group + u, 1), :] = value
         return 0
 
     lax.fori_loop(0, half // group, step, 0)
@@ -686,7 +686,7 @@
             resids.append(resid)
             early = ()
             if last:
-                early = sol, final = directions(phi, phi_n, w, scales, resids, stacks)
+                sol, final = directions(phi, phi_n, w, scales, resids, stacks)
             modal, far, near = finish(phi_ts, own, recv, (to_x, to_d), (scale, far, near), early)
         if not last:
             blocks = parity_blocks(modal)

time: 218 us -> 215 us (0.986)
  waiting for transfers between devices: 68.2 us -> 60.5 us
  starting transfers between devices: 55.6 us -> 59.8 us
    ppermute x9, waiting for transfers between devices: 41.3 us -> 35 us  [swap_x(): return lax.ppermute(value, 'sub', [(i, i ^ 1) for i in range(n)])]
    ppermute x2, waiting for transfers between devices: 4.43 us -> 1.06 us  [over_mesh(): lax.ppermute(value, 'sub', [(i, i ^ step) for i in range(n)])]
    ppermute x4, starting transfers between devices: 5.04 us -> 7.6 us  [over_axis(): value = value + lax.ppermute(value, axis, [(i, i ^ step) for i in range(n)])]
where the time goes in v5:
time: 215 us; the launch traced here: 214 us
  Pallas kernels  88.9 us (41%)
  waiting for transfers between devices  60.5 us (28%)
  starting transfers between devices  59.8 us (28%)
  between operations  2.51 us (1%)
  other arithmetic  2.39 us (1%)
    pallas_call x31, Pallas kernels, call(): pl.pallas_call(run, in_specs=[pl.BlockSpec(memory_space=pltpu.SMEM)] * le...  88.9 us
    ppermute x9, waiting for transfers between devices, swap_x(): return lax.ppermute(value, 'sub', [(i, i ^ 1) for i in range(n)])  35 us
    ppermute x9, starting transfers between devices, swap_x(): return lax.ppermute(value, 'sub', [(i, i ^ 1) for i in range(n)])  15.7 us
    ppermute x9, waiting for transfers between devices, parity_blocks(): lax.ppermute(modal, 'sub', [(i, i ^ 2 * d) for i in range(n)])  15.4 us
    ppermute x9, starting transfers between devices, parity_blocks(): lax.ppermute(modal, 'sub', [(i, i ^ 2 * d) for i in range(n)])  13.3 us
    ppermute x4, starting transfers between devices, over_axis(): value = value + lax.ppermute(value, axis, [(i, i ^ step) for i in range(n)])  7.6 us
    ppermute x6, starting transfers between devices, edge_blocks(): out.append(lax.ppermute(value, BOTH, up + down))  7.15 us
    ppermute x4, waiting for transfers between devices, over_axis(): value = value + lax.ppermute(value, axis, [(i, i ^ step) for i in range(n)])  6.47 us
  transfers between devices with their start and end apart: 41, of which 18 were waited for; matrix products, arithmetic and copies ran while one was open for 0% of the time, Pallas kernels for 31%

profile of v5, /device:TPU:0, one launch (start us, length us, event | category | flops | bytes accessed | tf_op | source)
XLA Modules:
  0.0 214.1 jit_solution(12210910206873583753)
XLA Ops:
  0.7 5.3 %shard_map.96 = (f32[384,256]{1,0:T(8,128)S(1)}, f32[384,256]{1,0:T(8,128)S(1)}) custom-call(s32[1]{0:T(128)} %bitcast.refs_0_, s32[1,384]{1,0:T(1,128)} %refs_1_.18, s32[1,384]{1,0:T(1,128)} %refs_2_.18, f32[1792,256]{1,0:T(8,128)} %refs_2_.11), custom_call_target="tpu_custom_call" | custom-call | bytes 786432 | tf_op jit(solution)/shard_map/pallas_call | solution.py:55
  6.0 3.0 %collective-permute-start = (f32[384,256]{1,0:T(8,128)S(1)}, f32[384,256]{1,0:T(8,128)S(1)}, u32[]{:S(2)}, u32[]{:S(2)}) collective-permute-start(f32[384,256]{1,0:T(8,128)S(1)} %get-tuple-element.73), channel_id=1, source_target_pairs={{0,1},{1,0},{2,3},{3,2},{4,5},{5,4},{6,7},{7,6},{8,9},{9,8},{10,11... | collective-permute-start | bytes 1179656 | tf_op jit(solution)/shard_map/ppermute | solution.py:555
  11.0 6.4 %shard_map.95 = (bf16[1792,768]{1,0:T(8,128)(2,1)S(1)}, bf16[1792,128]{1,0:T(8,128)(2,1)S(1)}, bf16[1792,128]{1,0:T(8,128)(2,1)S(1)}, bf16[128,1792]{1,0:T(8,128...) custom-call(s32[1]{0:T(128)} %bitcast.refs_0_, ...), custom_call_target="tpu_custom_call" | custom-call | flops 1056964608 | bytes 6458368 | tf_op jit(solution)/shard_map/pallas_call | solution.py:55
  17.5 5.3 %collective-permute-start.6 = (f32[128,512]{1,0:T(8,128)S(1)}, f32[128,512]{1,0:T(8,128)S(1)}, u32[]{:S(2)}, u32[]{:S(2)}) collective-permute-start(f32[128,512]{1,0:T(8,128)S(1)} %get-tuple-element.81.refs_1_), channel_id=1, source_target_pairs={{0,6},{1,3},{2,0},{3,5},{4,2},{5,7},{6,4},{7,1},{8,14},{9,11},{10,... | collective-permute-start | bytes 786440 | tf_op jit(solution)/shard_map/ppermute | solution.py:567
  22.8 5.2 %shard_map.99.refs_5_.refs_3_.refs_0_ = f32[1792,128]{1,0:T(8,128)S(1)} custom-call(f32[1792,1792]{1,0:T(8,128)S(1)} %copy-done, bf16[1792,128]{1,0:T(8,128)(2,1)S(1)} %get-tuple-element.69.refs_1_.refs_5_.refs_0_, bf16[1792,128]{1,0:T(8,128)(2,1)S(1)} %get-tuple-element.70.refs_2_.refs_6_.refs_1_), custom_call_target="tpu_custom_call" | custom-call | flops 2466250752 | bytes 14680064 | tf_op jit(solution)/shard_map/pallas_call | solution.py:55
  30.7 3.1 %collective-permute-start.9 = (f32[136,256]{1,0:T(8,128)S(1)}, f32[136,256]{1,0:T(8,128)S(1)}, u32[]{:S(2)}, u32[]{:S(2)}) collective-permute-start(f32[136,256]{1,0:T(8,128)S(1)} %shard_map.100.refs_5_), channel_id=1, source_target_pairs={{0,6},{1,7},{2,4},{3,5},{4,2},{5,3},{6,0},{7,1},{8,14},{9,15},{10,... | collective-permute-start | bytes 417800 | tf_op jit(solution)/shard_map/ppermute | solution.py:588
  35.1 7.3 %collective-permute-done.9.refs_8_ = f32[136,256]{1,0:T(8,128)S(1)} collective-permute-done((f32[136,256]{1,0:T(8,128)S(1)}, f32[136,256]{1,0:T(8,128)S(1)}, u32[]{:S(2)}, u32[]{:S(2)}) %collective-permute-start.9) | collective-permute-done | bytes 139296 | tf_op jit(solution)/shard_map/ppermute | solution.py:588
  44.0 4.7 %collective-permute-done.8.refs_7_ = f32[136,256]{1,0:T(8,128)S(1)} collective-permute-done((f32[136,256]{1,0:T(8,128)S(1)}, f32[136,256]{1,0:T(8,128)S(1)}, u32[]{:S(2)}, u32[]{:S(2)}) %collective-permute-start.8) | collective-permute-done | bytes 139296 | tf_op jit(solution)/shard_map/ppermute | solution.py:588
  50.0 4.0 %collective-permute-start.10 = (f32[392,256]{1,0:T(8,128)S(1)}, f32[392,256]{1,0:T(8,128)S(1)}, u32[]{:S(2)}, u32[]{:S(2)}) collective-permute-start(f32[392,256]{1,0:T(8,128)S(1)} %get-tuple-element.87), channel_id=1, source_target_pairs={{0,1},{1,0},{2,3},{3,2},{4,5},{5,4},{6,7},{7,6},{8,9},{9,8},{10,11... | collective-permute-start | bytes 1204232 | tf_op jit(solution)/shard_map/ppermute | solution.py:555
  56.3 4.6 %shard_map.97 = (f32[1792,256]{1,0:T(8,128)S(1)}, f32[1792,128]{1,0:T(8,128)S(1)}, bf16[1792,256]{1,0:T(8,128)(2,1)S(1)}, bf16[1792,256]{1,0:T(8,128)(2,1)S(1)}) custom-call(bf16[1792,768]{1,0:T(8,128)(2,1)S(1)} %get-tuple-element.71.refs_0_, f32[1792,128]{1,0:T(8,128)S(1)} %get-tuple-element.72.refs_1_.refs_3_, f32[1792,256]{1,0:T(8,128)S(1)} %copy-done.1, ...), custom_call_target="tpu_custom_call" | custom-call | flops 2818572288 | bytes 11296768 | tf_op jit(solution)/shard_map/pallas_call | solution.py:55
  61.0 6.3 %collective-permute-done.10.refs_2_ = f32[392,256]{1,0:T(8,128)S(1)} collective-permute-done((f32[392,256]{1,0:T(8,128)S(1)}, f32[392,256]{1,0:T(8,128)S(1)}, u32[]{:S(2)}, u32[]{:S(2)}) %collective-permute-start.10) | collective-permute-done | bytes 401440 | tf_op jit(solution)/shard_map/ppermute | solution.py:555
  69.7 5.1 %shard_map.103.refs_0_.refs_3_ = f32[1792,256]{1,0:T(8,128)S(1)} custom-call(f32[1792,1792]{1,0:T(8,128)S(1)} %copy-done, bf16[1792,256]{1,0:T(8,128)(2,1)S(1)} %get-tuple-element.91.refs_1_, bf16[1792,256]{1,0:T(8,128)(2,1)S(1)} %get-tuple-element.92.refs_2_), custom_call_target="tpu_custom_call" | custom-call | flops 4932501504 | bytes 16515072 | tf_op jit(solution)/shard_map/pallas_call | solution.py:55
  82.9 5.1 %shard_map.107.refs_4_.refs_1_ = f32[1792,256]{1,0:T(8,128)S(1)} custom-call(f32[1792,1792]{1,0:T(8,128)S(1)} %copy-done, bf16[1792,256]{1,0:T(8,128)(2,1)S(1)} %get-tuple-element.77.refs_7_.refs_1_.refs_2_, bf16[1792,256]{1,0:T(8,128)(2,1)S(1)} %get-tuple-element.78.refs_8_.refs_2_.refs_3_), custom_call_target="tpu_custom_call" | custom-call | flops 4932501504 | bytes 16515072 | tf_op jit(solution)/shard_map/pallas_call | solution.py:55
  88.0 4.3 %shard_map.108 = (f32[768,128]{1,0:T(8,128)S(1)}, f32[768,256]{1,0:T(8,128)S(1)}) custom-call(s32[1]{0:T(128)} %bitcast.refs_0_, s32[1,384]{1,0:T(1,128)S(1)} %copy-done.3, s32[1,384]{1,0:T(1,128)S(1)} %copy-done.4, f32[1792,128]{1,0:T(8,128)S(1)} %shard_map.99.refs_5_.refs_3_.refs_0_, f32[1792,256]{1,0:T(8,128)S(1)} %shard_map.107.refs_4_.refs_1_), custom_call_target="tpu_custom_call" | custom-call | flops 2000000000 | bytes 3932160 | tf_op jit(solution)/shard_map/pallas_call | solution.py:55
  94.6 5.1 %collective-permute-done.13.refs_3_ = f32[384,256]{1,0:T(8,128)S(1)} collective-permute-done((f32[384,256]{1,0:T(8,128)S(1)}, f32[384,256]{1,0:T(8,128)S(1)}, u32[]{:S(2)}, u32[]{:S(2)}) %collective-permute-start.13) | collective-permute-done | bytes 393248 | tf_op jit(solution)/shard_map/ppermute | solution.py:555
  100.2 3.2 %collective-permute-start.17 = (f32[136,256]{1,0:T(8,128)S(1)}, f32[136,256]{1,0:T(8,128)S(1)}, u32[]{:S(2)}, u32[]{:S(2)}) collective-permute-start(f32[136,256]{1,0:T(8,128)S(1)} %get-tuple-element.98.refs_5_), channel_id=1, source_target_pairs={{0,6},{1,7},{2,4},{3,5},{4,2},{5,3},{6,0},{7,1},{8,14},{9,15},{10,... | collective-permute-start | bytes 417800 | tf_op jit(solution)/shard_map/ppermute | solution.py:588
  104.7 2.8 %shard_map.110 = (f32[1792,256]{1,0:T(8,128)S(1)}, bf16[1792,256]{1,0:T(8,128)(2,1)S(1)}, bf16[1792,256]{1,0:T(8,128)(2,1)S(1)}) custom-call(bf16[1792,768]{1,0:T(8,128)(2,1)S(1)} %get-tuple-element.71.refs_0_, f32[1792,256]{1,0:T(8,128)S(1)} %get-tuple-element.99.refs_1_.refs_9_, f32[768,256]{1,0:T(8,128)S(1)} %get-tuple-element.100.refs_2_.refs_8_, ...), custom_call_target="tpu_custom_call" | custom-call | flops 1409286144 | bytes 9961472 | tf_op jit(solution)/shard_map/pallas_call | solution.py:55
  107.4 5.1 %shard_map.111.refs_9_.refs_3_.refs_2_ = f32[1792,256]{1,0:T(8,128)S(1)} custom-call(f32[1792,1792]{1,0:T(8,128)S(1)} %copy-done, bf16[1792,256]{1,0:T(8,128)(2,1)S(1)} %get-tuple-element.101.refs_1_, bf16[1792,256]{1,0:T(8,128)(2,1)S(1)} %get-tuple-element.102.refs_2_), custom_call_target="tpu_custom_call" | custom-call | flops 4932501504 | bytes 16515072 | tf_op jit(solution)/shard_map/pallas_call | solution.py:55
  118.9 3.8 %shard_map.113.refs_5_ = f32[768,256]{1,0:T(8,128)S(1)} custom-call(s32[1]{0:T(128)} %bitcast.refs_0_, s32[1,384]{1,0:T(1,128)S(1)} %copy-done.3, s32[1,384]{1,0:T(1,128)S(1)} %copy-done.4, f32[1792,256]{1,0:T(8,128)S(1)} %shard_map.111.refs_9_.refs_3_.refs_2_), custom_call_target="tpu_custom_call" | custom-call | flops 2000000000 | bytes 2621440 | tf_op jit(solution)/shard_map/pallas_call | solution.py:55
  122.8 4.5 %collective-permute-done.18.refs_7_ = f32[392,256]{1,0:T(8,128)S(1)} collective-permute-done((f32[392,256]{1,0:T(8,128)S(1)}, f32[392,256]{1,0:T(8,128)S(1)}, u32[]{:S(2)}, u32[]{:S(2)}) %collective-permute-start.18) | collective-permute-done | bytes 401440 | tf_op jit(solution)/shard_map/ppermute | solution.py:555
  130.4 2.9 %collective-permute-start.19 = (f32[8,256]{1,0:T(8,128)S(1)}, f32[8,256]{1,0:T(8,128)S(1)}, u32[]{:S(2)}, u32[]{:S(2)}) collective-permute-start(f32[8,256]{1,0:T(8,128)S(1)} %slice_add_fusion.1), channel_id=1, source_target_pairs={{0,8},{8,0},{16,24},{24,16},{1,9},{9,1},{17,25},{25,17},{2,10},{10... | collective-permute-start | bytes 24584 | tf_op jit(solution)/shard_map/ppermute | solution.py:598
  137.9 4.6 %shard_map.115 = (f32[1792,256]{1,0:T(8,128)S(1)}, f32[1792,256]{1,0:T(8,128)S(1)}, f32[136,256]{1,0:T(8,128)S(1)}) custom-call(f32[1792,128]{1,0:T(8,128)S(1)} %shard_map.99.refs_5_.refs_3_.refs_0_, f32[1792,256]{1,0:T(8,128)S(1)} %shard_map.107.refs_4_.refs_1_, f32[1792,256]{1,0:T(8,128)S(1)} %shard_map.111.refs_9_.refs_3_.refs_2_, ...), custom_call_target="tpu_custom_call" | custom-call | flops 1409286144 | bytes 16138240 | tf_op jit(solution)/shard_map/pallas_call | solution.py:55
  142.4 5.3 %collective-permute-done.23.refs_3_ = f32[384,256]{1,0:T(8,128)S(1)} collective-permute-done((f32[384,256]{1,0:T(8,128)S(1)}, f32[384,256]{1,0:T(8,128)S(1)}, u32[]{:S(2)}, u32[]{:S(2)}) %collective-permute-start.23) | collective-permute-done | bytes 393248 | tf_op jit(solution)/shard_map/ppermute | solution.py:555
  152.7 2.8 %shard_map.117 = (f32[1792,256]{1,0:T(8,128)S(1)}, bf16[1792,256]{1,0:T(8,128)(2,1)S(1)}, bf16[1792,256]{1,0:T(8,128)(2,1)S(1)}) custom-call(bf16[1792,768]{1,0:T(8,128)(2,1)S(1)} %get-tuple-element.71.refs_0_, f32[1792,256]{1,0:T(8,128)S(1)} %get-tuple-element.114.refs_1_.refs_9_, f32[768,256]{1,0:T(8,128)S(1)} %get-tuple-element.115.refs_2_.refs_8_, ...), custom_call_target="tpu_custom_call" | custom-call | flops 1409286144 | bytes 9961472 | tf_op jit(solution)/shard_map/pallas_call | solution.py:55
  155.5 5.1 %shard_map.118.refs_9_.refs_3_.refs_2_ = f32[1792,256]{1,0:T(8,128)S(1)} custom-call(f32[1792,1792]{1,0:T(8,128)S(1)} %copy-done, bf16[1792,256]{1,0:T(8,128)(2,1)S(1)} %get-tuple-element.116.refs_1_, bf16[1792,256]{1,0:T(8,128)(2,1)S(1)} %get-tuple-element.117.refs_2_), custom_call_target="tpu_custom_call" | custom-call | flops 4932501504 | bytes 16515072 | tf_op jit(solution)/shard_map/pallas_call | solution.py:55
  165.6 3.8 %shard_map.120.refs_5_ = f32[768,256]{1,0:T(8,128)S(1)} custom-call(s32[1]{0:T(128)} %bitcast.refs_0_, s32[1,384]{1,0:T(1,128)S(1)} %copy-done.3, s32[1,384]{1,0:T(1,128)S(1)} %copy-done.4, f32[1792,256]{1,0:T(8,128)S(1)} %shard_map.118.refs_9_.refs_3_.refs_2_), custom_call_target="tpu_custom_call" | custom-call | flops 2000000000 | bytes 2621440 | tf_op jit(solution)/shard_map/pallas_call | solution.py:55
  169.4 5.7 %collective-permute-done.28.refs_7_ = f32[392,256]{1,0:T(8,128)S(1)} collective-permute-done((f32[392,256]{1,0:T(8,128)S(1)}, f32[392,256]{1,0:T(8,128)S(1)}, u32[]{:S(2)}, u32[]{:S(2)}) %collective-permute-start.28) | collective-permute-done | bytes 401440 | tf_op jit(solution)/shard_map/ppermute | solution.py:555
  181.5 3.2 %collective-permute-done.30 = f32[8,256]{1,0:T(8,128)S(1)} collective-permute-done((f32[8,256]{1,0:T(8,128)S(1)}, f32[8,256]{1,0:T(8,128)S(1)}, u32[]{:S(2)}, u32[]{:S(2)}) %collective-permute-start.30) | collective-permute-done | bytes 8224 | tf_op jit(solution)/shard_map/ppermute | solution.py:598
  184.7 2.8 %shard_map.122 = (f32[1792,256]{1,0:T(8,128)S(1)}, f32[1792,256]{1,0:T(8,128)S(1)}, f32[136,256]{1,0:T(8,128)S(1)}) custom-call(f32[1792,128]{1,0:T(8,128)S(1)} %shard_map.99.refs_5_.refs_3_.refs_0_, f32[1792,256]{1,0:T(8,128)S(1)} %shard_map.107.refs_4_.refs_1_, f32[1792,256]{1,0:T(8,128)S(1)} %shard_map.118.refs_9_.refs_3_.refs_2_, ...), custom_call_target="tpu_custom_call" | custom-call | flops 1409286144 | bytes 16138240 | tf_op jit(solution)/shard_map/pallas_call | solution.py:55
  187.4 8.1 %collective-permute-done.33.refs_3_ = f32[384,256]{1,0:T(8,128)S(1)} collective-permute-done((f32[384,256]{1,0:T(8,128)S(1)}, f32[384,256]{1,0:T(8,128)S(1)}, u32[]{:S(2)}, u32[]{:S(2)}) %collective-permute-start.33) | collective-permute-done | bytes 393248 | tf_op jit(solution)/shard_map/ppermute | solution.py:555
  203.3 3.8 %shard_map.123 = (f32[1792,256]{1,0:T(8,128)S(1)}, f32[1792,256]{1,0:T(8,128)S(1)}) custom-call(bf16[1792,128]{1,0:T(8,128)(2,1)S(1)} %get-tuple-element.69.refs_1_.refs_5_.refs_0_, bf16[1792,128]{1,0:T(8,128)(2,1)S(1)} %get-tuple-element.70.refs_2_.refs_6_.refs_1_, bf16[1792,256]{1,0:T(8,128)(2,1)S(1)} %get-tuple-element.77.refs_7_.refs_1_.refs_2_, ...), custom_call_target="tpu_custom_call" | custom-call | flops 2113929216 | bytes 14041088 | tf_op jit(solution)/shard_map/pallas_call | solution.py:55
  208.0 2.7 %shard_map.125 = f32[1792,256]{1,0:T(8,128)S(1)} custom-call(bf16[1792,768]{1,0:T(8,128)(2,1)S(1)} %get-tuple-element.71.refs_0_, f32[1792,256]{1,0:T(8,128)S(1)} %get-tuple-element.134.refs_1_, f32[768,256]{1,0:T(8,128)S(1)} %get-tuple-element.135.refs_2_), custom_call_target="tpu_custom_call" | custom-call | flops 1409286144 | bytes 7208960 | tf_op jit(solution)/shard_map/pallas_call | solution.py:55
  (108 shorter events, 66.6 us)
Async XLA Ops:
  6.0 22.1 %collective-permute-start = (f32[384,256]{1,0:T(8,128)S(1)}, f32[384,256]{1,0:T(8,128)S(1)}, u32[]{:S(2)}, u32[]{:S(2)}) collective-permute-start(f32[384,256]{1,0:T(8,128)S(1)} %get-tuple-element.73), channel_id=1, source_target_pairs={{0,1},{1,0},{2,3},{3,2},{4,5},{5,4},{6,7},{7,6},{8,9},{9,8},{10,11... | collective-permute-start | bytes 1179656 | tf_op jit(solution)/shard_map/ppermute | solution.py:555
  9.0 19.1 %collective-permute-start.1 = (f32[384,256]{1,0:T(8,128)S(1)}, f32[384,256]{1,0:T(8,128)S(1)}, u32[]{:S(2)}, u32[]{:S(2)}) collective-permute-start(f32[384,256]{1,0:T(8,128)S(1)} %get-tuple-element.74), channel_id=1, source_target_pairs={{1,2},{3,4},{5,6},{7,8},{9,10},{11,12},{13,14},{15,16},{17,18},{19... | collective-permute-start | bytes 1179656 | tf_op jit(solution)/shard_map/ppermute | solution.py:561
  17.5 16.3 %collective-permute-start.6 = (f32[128,512]{1,0:T(8,128)S(1)}, f32[128,512]{1,0:T(8,128)S(1)}, u32[]{:S(2)}, u32[]{:S(2)}) collective-permute-start(f32[128,512]{1,0:T(8,128)S(1)} %get-tuple-element.81.refs_1_), channel_id=1, source_target_pairs={{0,6},{1,3},{2,0},{3,5},{4,2},{5,7},{6,4},{7,1},{8,14},{9,11},{10,... | collective-permute-start | bytes 786440 | tf_op jit(solution)/shard_map/ppermute | solution.py:567
  28.4 20.9 %collective-permute-start.5 = (f32[128,512]{1,0:T(8,128)S(1)}, f32[128,512]{1,0:T(8,128)S(1)}, u32[]{:S(2)}, u32[]{:S(2)}) collective-permute-start(f32[128,512]{1,0:T(8,128)S(1)} %get-tuple-element.85), channel_id=1, source_target_pairs={{1,2},{3,4},{5,6},{7,0},{2,1},{4,3},{6,5},{0,7},{9,10},{11,12},{13... | collective-permute-start | bytes 786440 | tf_op jit(solution)/shard_map/ppermute | solution.py:574
  30.7 18.6 %collective-permute-start.4 = (f32[128,512]{1,0:T(8,128)S(1)}, f32[128,512]{1,0:T(8,128)S(1)}, u32[]{:S(2)}, u32[]{:S(2)}) collective-permute-start(f32[128,512]{1,0:T(8,128)S(1)} %get-tuple-element.85), channel_id=1, source_target_pairs={{0,1},{1,0},{2,3},{3,2},{4,5},{5,4},{6,7},{7,6},{8,9},{9,8},{10,11... | collective-permute-start | bytes 786440 | tf_op jit(solution)/shard_map/ppermute | solution.py:555
  30.7 11.7 %collective-permute-start.9 = (f32[136,256]{1,0:T(8,128)S(1)}, f32[136,256]{1,0:T(8,128)S(1)}, u32[]{:S(2)}, u32[]{:S(2)}) collective-permute-start(f32[136,256]{1,0:T(8,128)S(1)} %shard_map.100.refs_5_), channel_id=1, source_target_pairs={{0,6},{1,7},{2,4},{3,5},{4,2},{5,3},{6,0},{7,1},{8,14},{9,15},{10,... | collective-permute-start | bytes 417800 | tf_op jit(solution)/shard_map/ppermute | solution.py:588
  33.8 14.9 %collective-permute-start.8 = (f32[136,256]{1,0:T(8,128)S(1)}, f32[136,256]{1,0:T(8,128)S(1)}, u32[]{:S(2)}, u32[]{:S(2)}) collective-permute-start(f32[136,256]{1,0:T(8,128)S(1)} %shard_map.100.refs_5_), channel_id=1, source_target_pairs={{0,4},{1,5},{2,6},{3,7},{4,0},{5,1},{6,2},{7,3},{8,12},{9,13},{10,... | collective-permute-start | bytes 417800 | tf_op jit(solution)/shard_map/ppermute | solution.py:588
  33.8 15.6 %collective-permute-start.7 = (f32[136,256]{1,0:T(8,128)S(1)}, f32[136,256]{1,0:T(8,128)S(1)}, u32[]{:S(2)}, u32[]{:S(2)}) collective-permute-start(f32[136,256]{1,0:T(8,128)S(1)} %shard_map.100.refs_5_), channel_id=1, source_target_pairs={{0,2},{1,3},{2,0},{3,1},{4,6},{5,7},{6,4},{7,5},{8,10},{9,11},{10,... | collective-permute-start | bytes 417800 | tf_op jit(solution)/shard_map/ppermute | solution.py:588
  42.4 13.9 %collective-permute-start.2 = (f32[408,128]{1,0:T(8,128)S(1)}, f32[408,128]{1,0:T(8,128)S(1)}, u32[]{:S(2)}, u32[]{:S(2)}) collective-permute-start(f32[408,128]{1,0:T(8,128)S(1)} %get-tuple-element.75), channel_id=1, source_target_pairs={{0,1},{1,0},{2,3},{3,2},{4,5},{5,4},{6,7},{7,6},{8,9},{9,8},{10,11... | collective-permute-start | bytes 626696 | tf_op jit(solution)/shard_map/ppermute | solution.py:555
  48.6 7.7 %collective-permute-start.3 = (f32[408,128]{1,0:T(8,128)S(1)}, f32[408,128]{1,0:T(8,128)S(1)}, u32[]{:S(2)}, u32[]{:S(2)}) collective-permute-start(f32[408,128]{1,0:T(8,128)S(1)} %get-tuple-element.76), channel_id=1, source_target_pairs={{1,2},{3,4},{5,6},{7,8},{9,10},{11,12},{13,14},{15,16},{17,18},{19... | collective-permute-start | bytes 626696 | tf_op jit(solution)/shard_map/ppermute | solution.py:561
  50.0 17.3 %collective-permute-start.10 = (f32[392,256]{1,0:T(8,128)S(1)}, f32[392,256]{1,0:T(8,128)S(1)}, u32[]{:S(2)}, u32[]{:S(2)}) collective-permute-start(f32[392,256]{1,0:T(8,128)S(1)} %get-tuple-element.87), channel_id=1, source_target_pairs={{0,1},{1,0},{2,3},{3,2},{4,5},{5,4},{6,7},{7,6},{8,9},{9,8},{10,11... | collective-permute-start | bytes 1204232 | tf_op jit(solution)/shard_map/ppermute | solution.py:555
  54.0 7.0 %collective-permute-start.11 = (f32[128,256]{1,0:T(8,128)S(1)}, f32[128,256]{1,0:T(8,128)S(1)}, u32[]{:S(2)}, u32[]{:S(2)}) collective-permute-start(f32[128,256]{1,0:T(8,128)S(1)} %get-tuple-element.88), channel_id=1, source_target_pairs={{0,8},{8,16},{16,24},{15,7},{23,15},{31,23}} | collective-permute-start | bytes 393224 | tf_op jit(solution)/shard_map/ppermute | solution.py:628
  55.5 5.5 %collective-permute-start.12 = (f32[128,256]{1,0:T(8,128)S(1)}, f32[128,256]{1,0:T(8,128)S(1)}, u32[]{:S(2)}, u32[]{:S(2)}) collective-permute-start(f32[128,256]{1,0:T(8,128)S(1)} %get-tuple-element.89), channel_id=1, source_target_pairs={{1,8},{9,16},{17,24},{14,7},{22,15},{30,23}} | collective-permute-start | bytes 393224 | tf_op jit(solution)/shard_map/ppermute | solution.py:628
  79.8 20.0 %collective-permute-start.13 = (f32[384,256]{1,0:T(8,128)S(1)}, f32[384,256]{1,0:T(8,128)S(1)}, u32[]{:S(2)}, u32[]{:S(2)}) collective-permute-start(f32[384,256]{1,0:T(8,128)S(1)} %shard_map.105.refs_5_), channel_id=1, source_target_pairs={{0,1},{1,0},{2,3},{3,2},{4,5},{5,4},{6,7},{7,6},{8,9},{9,8},{10,11... | collective-permute-start | bytes 1179656 | tf_op jit(solution)/shard_map/ppermute | solution.py:555
  82.2 17.5 %collective-permute-start.14 = (f32[384,256]{1,0:T(8,128)S(1)}, f32[384,256]{1,0:T(8,128)S(1)}, u32[]{:S(2)}, u32[]{:S(2)}) collective-permute-start(f32[384,256]{1,0:T(8,128)S(1)} %shard_map.106.refs_6_), channel_id=1, source_target_pairs={{1,2},{3,4},{5,6},{7,8},{9,10},{11,12},{13,14},{15,16},{17,18},{19... | collective-permute-start | bytes 1179656 | tf_op jit(solution)/shard_map/ppermute | solution.py:561
  100.2 12.4 %collective-permute-start.17 = (f32[136,256]{1,0:T(8,128)S(1)}, f32[136,256]{1,0:T(8,128)S(1)}, u32[]{:S(2)}, u32[]{:S(2)}) collective-permute-start(f32[136,256]{1,0:T(8,128)S(1)} %get-tuple-element.98.refs_5_), channel_id=1, source_target_pairs={{0,6},{1,7},{2,4},{3,5},{4,2},{5,3},{6,0},{7,1},{8,14},{9,15},{10,... | collective-permute-start | bytes 417800 | tf_op jit(solution)/shard_map/ppermute | solution.py:588
  103.4 10.9 %collective-permute-start.16 = (f32[136,256]{1,0:T(8,128)S(1)}, f32[136,256]{1,0:T(8,128)S(1)}, u32[]{:S(2)}, u32[]{:S(2)}) collective-permute-start(f32[136,256]{1,0:T(8,128)S(1)} %get-tuple-element.98.refs_5_), channel_id=1, source_target_pairs={{0,4},{1,5},{2,6},{3,7},{4,0},{5,1},{6,2},{7,3},{8,12},{9,13},{10,... | collective-permute-start | bytes 417800 | tf_op jit(solution)/shard_map/ppermute | solution.py:588
  103.4 10.9 %collective-permute-start.15 = (f32[136,256]{1,0:T(8,128)S(1)}, f32[136,256]{1,0:T(8,128)S(1)}, u32[]{:S(2)}, u32[]{:S(2)}) collective-permute-start(f32[136,256]{1,0:T(8,128)S(1)} %get-tuple-element.98.refs_5_), channel_id=1, source_target_pairs={{0,2},{1,3},{2,0},{3,1},{4,6},{5,7},{6,4},{7,5},{8,10},{9,11},{10,... | collective-permute-start | bytes 417800 | tf_op jit(solution)/shard_map/ppermute | solution.py:588
  115.0 12.2 %collective-permute-start.18 = (f32[392,256]{1,0:T(8,128)S(1)}, f32[392,256]{1,0:T(8,128)S(1)}, u32[]{:S(2)}, u32[]{:S(2)}) collective-permute-start(f32[392,256]{1,0:T(8,128)S(1)} %get-tuple-element.104), channel_id=1, source_target_pairs={{0,1},{1,0},{2,3},{3,2},{4,5},{5,4},{6,7},{7,6},{8,9},{9,8},{10,11... | collective-permute-start | bytes 1204232 | tf_op jit(solution)/shard_map/ppermute | solution.py:555
  116.5 6.2 %collective-permute-start.21 = (f32[128,256]{1,0:T(8,128)S(1)}, f32[128,256]{1,0:T(8,128)S(1)}, u32[]{:S(2)}, u32[]{:S(2)}) collective-permute-start(f32[128,256]{1,0:T(8,128)S(1)} %get-tuple-element.105), channel_id=1, source_target_pairs={{0,8},{8,16},{16,24},{15,7},{23,15},{31,23}} | collective-permute-start | bytes 393224 | tf_op jit(solution)/shard_map/ppermute | solution.py:628
  128.0 19.7 %collective-permute-start.23 = (f32[384,256]{1,0:T(8,128)S(1)}, f32[384,256]{1,0:T(8,128)S(1)}, u32[]{:S(2)}, u32[]{:S(2)}) collective-permute-start(f32[384,256]{1,0:T(8,128)S(1)} %get-tuple-element.110.refs_5_), channel_id=1, source_target_pairs={{0,1},{1,0},{2,3},{3,2},{4,5},{5,4},{6,7},{7,6},{8,9},{9,8},{10,11... | collective-permute-start | bytes 1179656 | tf_op jit(solution)/shard_map/ppermute | solution.py:555
  129.5 18.2 %collective-permute-start.24 = (f32[384,256]{1,0:T(8,128)S(1)}, f32[384,256]{1,0:T(8,128)S(1)}, u32[]{:S(2)}, u32[]{:S(2)}) collective-permute-start(f32[384,256]{1,0:T(8,128)S(1)} %get-tuple-element.111.refs_6_), channel_id=1, source_target_pairs={{1,2},{3,4},{5,6},{7,8},{9,10},{11,12},{13,14},{15,16},{17,18},{19... | collective-permute-start | bytes 1179656 | tf_op jit(solution)/shard_map/ppermute | solution.py:561
  148.2 12.4 %collective-permute-start.27 = (f32[136,256]{1,0:T(8,128)S(1)}, f32[136,256]{1,0:T(8,128)S(1)}, u32[]{:S(2)}, u32[]{:S(2)}) collective-permute-start(f32[136,256]{1,0:T(8,128)S(1)} %get-tuple-element.113.refs_5_), channel_id=1, source_target_pairs={{0,6},{1,7},{2,4},{3,5},{4,2},{5,3},{6,0},{7,1},{8,14},{9,15},{10,... | collective-permute-start | bytes 417800 | tf_op jit(solution)/shard_map/ppermute | solution.py:588
  150.4 11.9 %collective-permute-start.26 = (f32[136,256]{1,0:T(8,128)S(1)}, f32[136,256]{1,0:T(8,128)S(1)}, u32[]{:S(2)}, u32[]{:S(2)}) collective-permute-start(f32[136,256]{1,0:T(8,128)S(1)} %get-tuple-element.113.refs_5_), channel_id=1, source_target_pairs={{0,4},{1,5},{2,6},{3,7},{4,0},{5,1},{6,2},{7,3},{8,12},{9,13},{10,... | collective-permute-start | bytes 417800 | tf_op jit(solution)/shard_map/ppermute | solution.py:588
  150.4 11.9 %collective-permute-start.25 = (f32[136,256]{1,0:T(8,128)S(1)}, f32[136,256]{1,0:T(8,128)S(1)}, u32[]{:S(2)}, u32[]{:S(2)}) collective-permute-start(f32[136,256]{1,0:T(8,128)S(1)} %get-tuple-element.113.refs_5_), channel_id=1, source_target_pairs={{0,2},{1,3},{2,0},{3,1},{4,6},{5,7},{6,4},{7,5},{8,10},{9,11},{10,... | collective-permute-start | bytes 417800 | tf_op jit(solution)/shard_map/ppermute | solution.py:588
  162.9 12.2 %collective-permute-start.28 = (f32[392,256]{1,0:T(8,128)S(1)}, f32[392,256]{1,0:T(8,128)S(1)}, u32[]{:S(2)}, u32[]{:S(2)}) collective-permute-start(f32[392,256]{1,0:T(8,128)S(1)} %get-tuple-element.119), channel_id=1, source_target_pairs={{0,1},{1,0},{2,3},{3,2},{4,5},{5,4},{6,7},{7,6},{8,9},{9,8},{10,11... | collective-permute-start | bytes 1204232 | tf_op jit(solution)/shard_map/ppermute | solution.py:555
  163.1 6.3 %collective-permute-start.31 = (f32[128,256]{1,0:T(8,128)S(1)}, f32[128,256]{1,0:T(8,128)S(1)}, u32[]{:S(2)}, u32[]{:S(2)}) collective-permute-start(f32[128,256]{1,0:T(8,128)S(1)} %get-tuple-element.121), channel_id=1, source_target_pairs={{0,8},{8,16},{16,24},{15,7},{23,15},{31,23}} | collective-permute-start | bytes 393224 | tf_op jit(solution)/shard_map/ppermute | solution.py:628
  175.8 19.8 %collective-permute-start.33 = (f32[384,256]{1,0:T(8,128)S(1)}, f32[384,256]{1,0:T(8,128)S(1)}, u32[]{:S(2)}, u32[]{:S(2)}) collective-permute-start(f32[384,256]{1,0:T(8,128)S(1)} %get-tuple-element.129.refs_5_), channel_id=1, source_target_pairs={{0,1},{1,0},{2,3},{3,2},{4,5},{5,4},{6,7},{7,6},{8,9},{9,8},{10,11... | collective-permute-start | bytes 1179656 | tf_op jit(solution)/shard_map/ppermute | solution.py:555
  177.3 18.3 %collective-permute-start.34 = (f32[384,256]{1,0:T(8,128)S(1)}, f32[384,256]{1,0:T(8,128)S(1)}, u32[]{:S(2)}, u32[]{:S(2)}) collective-permute-start(f32[384,256]{1,0:T(8,128)S(1)} %get-tuple-element.130.refs_6_), channel_id=1, source_target_pairs={{1,2},{3,4},{5,6},{7,8},{9,10},{11,12},{13,14},{15,16},{17,18},{19... | collective-permute-start | bytes 1179656 | tf_op jit(solution)/shard_map/ppermute | solution.py:561
  198.1 4.5 %collective-permute-start.38 = (f32[8,256]{1,0:T(8,128)S(1)}, f32[8,256]{1,0:T(8,128)S(1)}, u32[]{:S(2)}, u32[]{:S(2)}) collective-permute-start(f32[8,256]{1,0:T(8,128)S(1)} %slice_add_fusion.5), channel_id=1, source_target_pairs={{0,17},{1,16},{2,19},{3,18},{4,21},{5,20},{6,23},{7,22},{8,25},{9,... | collective-permute-start | bytes 24584 | tf_op jit(solution)/shard_map/ppermute | solution.py:611
  198.2 4.5 %collective-permute-start.37 = (f32[8,256]{1,0:T(8,128)S(1)}, f32[8,256]{1,0:T(8,128)S(1)}, u32[]{:S(2)}, u32[]{:S(2)}) collective-permute-start(f32[8,256]{1,0:T(8,128)S(1)} %slice_add_fusion.5), channel_id=1, source_target_pairs={{0,1},{1,0},{2,3},{3,2},{4,5},{5,4},{6,7},{7,6},{8,9},{9,8},{10,11... | collective-permute-start | bytes 24584 | tf_op jit(solution)/shard_map/ppermute | solution.py:611
  207.2 4.6 %collective-permute-start.40 = (f32[8,256]{1,0:T(8,128)S(1)}, f32[8,256]{1,0:T(8,128)S(1)}, u32[]{:S(2)}, u32[]{:S(2)}) collective-permute-start(f32[8,256]{1,0:T(8,128)S(1)} %add.60), channel_id=1, source_target_pairs={{0,4},{1,5},{2,6},{3,7},{4,0},{5,1},{6,2},{7,3},{8,12},{9,13},{10,... | collective-permute-start | bytes 24584 | tf_op jit(solution)/shard_map/ppermute | solution.py:618
  (14 other events, 99.2 us)

commit v6 on v5

--- a/solution.py
+++ b/solution.py
@@ -296,7 +296,7 @@
     )
 
 
-def schur_modes(schur, modes, after=()):
+def schur_modes(schur, modes, unroll):
     order, n = modes[0].shape
 
     def body(s_ref, h_ref, l_ref, q_ref):
@@ -306,9 +306,9 @@
             q_ref[r] = mm3(split2(s_ref[r]), rhs)
             return carry
 
-        over_blocks(order, block, unroll=True)
-
-    return call(body, [schur, *modes], [shape(order, n)], 6 * order * order * n, mb=10, after=after)[0]
+        over_blocks(order, block, unroll=unroll)
+
+    return call(body, [schur, *modes], [shape(order, n)], 6 * order * order * n, mb=10)[0]
 
 
 def schur_apply(schur, x):
@@ -379,7 +379,7 @@
             xh_ref[r], xl_ref[r] = split2(mm3(p, c) + w_ref[r, 0:1] * r_ref[r])
             return carry
 
-        over_blocks(order, step)
+        over_blocks(order, step, unroll=True)
 
     return call(
         body, [keep, recv, *edges, *phi, *phi_n, w, resid],
@@ -515,7 +515,7 @@
                 xh_ref[r], xl_ref[r] = split2(w_ref[r, 0:1] * new)
             return carry
 
-        over_blocks(order, step)
+        over_blocks(order, step, unroll=True)
 
     ins = [onehot_t, p, got] + ([] if w is None else [w])
     outs = [shape(order, k)] + ([] if w is None else [shape(order, k, dtype=BF16)] * 2)
@@ -646,7 +646,7 @@
     )
     phi, phi_t, phi_ts = (p_hi, p_lo), (pt_hi, pt_lo), (ts_hi, ts_lo)
     rows_own, rows_z, other = coarse_rows(me, coarse_inverse, (own,))
-    q_own = schur_modes(schur, phi)
+    q_own = schur_modes(schur, phi, True)
     (modal,) = finish(phi_ts, own, recv, after=(q_own,))
     blocks = parity_blocks(modal)
     other, _ = lax.optimization_barrier((other, modal))
@@ -676,7 +676,7 @@
         recv = from_x, swap_d(to_d)
         if first:
             p, own = first_image(y, vec, phi_t, resid)
-            q = (q_own, schur_modes(schur, phi_n))
+            q = (q_own, schur_modes(schur, phi_n, False))
             q_shared = gather_shared(me, left_rows, right_rows, list(q))
             modal, far, near = finish(phi_ts, own, recv, (to_x, to_d), (), tuple(q_shared))
         else:

time: 215 us -> 213 us (level)
  Pallas kernels: 88.9 us -> 85.7 us
    pallas_call x31, Pallas kernels: 88.9 us -> 85.7 us  [call(): pl.pallas_call(run, in_specs=[pl.BlockSpec(memory_space=pltpu.SMEM)] * le...]
  transfers between devices with their start and end apart: 41 -> 41, of which waited for: 18 -> 18; matrix products, arithmetic and copies ran while one was open for 0% -> 0% of each run, Pallas kernels for 31% -> 30%
where the time goes in v6:
time: 213 us
  Pallas kernels  85.7 us (40%)
  waiting for transfers between devices  61.9 us (29%)
  starting transfers between devices  60 us (28%)
  between operations  2.51 us (1%)
  other arithmetic  2.39 us (1%)
    pallas_call x31, Pallas kernels, call(): pl.pallas_call(run, in_specs=[pl.BlockSpec(memory_space=pltpu.SMEM)] * le...  85.7 us
    ppermute x9, waiting for transfers between devices, swap_x(): return lax.ppermute(value, 'sub', [(i, i ^ 1) for i in range(n)])  33.5 us
    ppermute x9, waiting for transfers between devices, parity_blocks(): lax.ppermute(modal, 'sub', [(i, i ^ 2 * d) for i in range(n)])  17 us
    ppermute x9, starting transfers between devices, swap_x(): return lax.ppermute(value, 'sub', [(i, i ^ 1) for i in range(n)])  15 us
    ppermute x9, starting transfers between devices, parity_blocks(): lax.ppermute(modal, 'sub', [(i, i ^ 2 * d) for i in range(n)])  13.3 us
    ppermute x4, starting transfers between devices, over_axis(): value = value + lax.ppermute(value, axis, [(i, i ^ step) for i in range(n)])  8.94 us
    ppermute x4, waiting for transfers between devices, over_axis(): value = value + lax.ppermute(value, axis, [(i, i ^ step) for i in range(n)])  6.72 us
    ppermute x6, starting transfers between devices, edge_blocks(): out.append(lax.ppermute(value, BOTH, up + down))  6.69 us
  transfers between devices with their start and end apart: 41, of which 18 were waited for; matrix products, arithmetic and copies ran while one was open for 0% of the time, Pallas kernels for 30%

profile of v6, /device:TPU:0, one launch (start us, length us, event | category | flops | bytes accessed | tf_op | source)
XLA Modules:
  0.0 212.6 jit_solution(2758415934902299227)
XLA Ops:
  0.7 5.3 %shard_map.96 = (f32[384,256]{1,0:T(8,128)S(1)}, f32[384,256]{1,0:T(8,128)S(1)}) custom-call(s32[1]{0:T(128)} %bitcast.refs_0_, s32[1,384]{1,0:T(1,128)} %refs_1_.18, s32[1,384]{1,0:T(1,128)} %refs_2_.18, f32[1792,256]{1,0:T(8,128)} %refs_2_.11), custom_call_target="tpu_custom_call" | custom-call | bytes 786432 | tf_op jit(solution)/shard_map/pallas_call | solution.py:55
  6.0 3.0 %collective-permute-start = (f32[384,256]{1,0:T(8,128)S(1)}, f32[384,256]{1,0:T(8,128)S(1)}, u32[]{:S(2)}, u32[]{:S(2)}) collective-permute-start(f32[384,256]{1,0:T(8,128)S(1)} %get-tuple-element.73), channel_id=1, source_target_pairs={{0,1},{1,0},{2,3},{3,2},{4,5},{5,4},{6,7},{7,6},{8,9},{9,8},{10,11... | collective-permute-start | bytes 1179656 | tf_op jit(solution)/shard_map/ppermute | solution.py:555
  11.0 6.4 %shard_map.95 = (bf16[1792,768]{1,0:T(8,128)(2,1)S(1)}, bf16[1792,128]{1,0:T(8,128)(2,1)S(1)}, bf16[1792,128]{1,0:T(8,128)(2,1)S(1)}, bf16[128,1792]{1,0:T(8,128...) custom-call(s32[1]{0:T(128)} %bitcast.refs_0_, ...), custom_call_target="tpu_custom_call" | custom-call | flops 1056964608 | bytes 6458368 | tf_op jit(solution)/shard_map/pallas_call | solution.py:55
  17.5 5.3 %collective-permute-start.6 = (f32[128,512]{1,0:T(8,128)S(1)}, f32[128,512]{1,0:T(8,128)S(1)}, u32[]{:S(2)}, u32[]{:S(2)}) collective-permute-start(f32[128,512]{1,0:T(8,128)S(1)} %get-tuple-element.81.refs_1_), channel_id=1, source_target_pairs={{0,6},{1,3},{2,0},{3,5},{4,2},{5,7},{6,4},{7,1},{8,14},{9,11},{10,... | collective-permute-start | bytes 786440 | tf_op jit(solution)/shard_map/ppermute | solution.py:567
  22.8 5.2 %shard_map.99.refs_5_.refs_3_.refs_0_ = f32[1792,128]{1,0:T(8,128)S(1)} custom-call(f32[1792,1792]{1,0:T(8,128)S(1)} %copy-done, bf16[1792,128]{1,0:T(8,128)(2,1)S(1)} %get-tuple-element.69.refs_1_.refs_5_.refs_0_, bf16[1792,128]{1,0:T(8,128)(2,1)S(1)} %get-tuple-element.70.refs_2_.refs_6_.refs_1_), custom_call_target="tpu_custom_call" | custom-call | flops 2466250752 | bytes 14680064 | tf_op jit(solution)/shard_map/pallas_call | solution.py:55
  30.7 3.1 %collective-permute-start.9 = (f32[136,256]{1,0:T(8,128)S(1)}, f32[136,256]{1,0:T(8,128)S(1)}, u32[]{:S(2)}, u32[]{:S(2)}) collective-permute-start(f32[136,256]{1,0:T(8,128)S(1)} %shard_map.100.refs_5_), channel_id=1, source_target_pairs={{0,6},{1,7},{2,4},{3,5},{4,2},{5,3},{6,0},{7,1},{8,14},{9,15},{10,... | collective-permute-start | bytes 417800 | tf_op jit(solution)/shard_map/ppermute | solution.py:588
  35.1 7.3 %collective-permute-done.9.refs_8_ = f32[136,256]{1,0:T(8,128)S(1)} collective-permute-done((f32[136,256]{1,0:T(8,128)S(1)}, f32[136,256]{1,0:T(8,128)S(1)}, u32[]{:S(2)}, u32[]{:S(2)}) %collective-permute-start.9) | collective-permute-done | bytes 139296 | tf_op jit(solution)/shard_map/ppermute | solution.py:588
  44.0 4.7 %collective-permute-done.8.refs_7_ = f32[136,256]{1,0:T(8,128)S(1)} collective-permute-done((f32[136,256]{1,0:T(8,128)S(1)}, f32[136,256]{1,0:T(8,128)S(1)}, u32[]{:S(2)}, u32[]{:S(2)}) %collective-permute-start.8) | collective-permute-done | bytes 139296 | tf_op jit(solution)/shard_map/ppermute | solution.py:588
  50.0 4.0 %collective-permute-start.10 = (f32[392,256]{1,0:T(8,128)S(1)}, f32[392,256]{1,0:T(8,128)S(1)}, u32[]{:S(2)}, u32[]{:S(2)}) collective-permute-start(f32[392,256]{1,0:T(8,128)S(1)} %get-tuple-element.87), channel_id=1, source_target_pairs={{0,1},{1,0},{2,3},{3,2},{4,5},{5,4},{6,7},{7,6},{8,9},{9,8},{10,11... | collective-permute-start | bytes 1204232 | tf_op jit(solution)/shard_map/ppermute | solution.py:555
  56.3 4.6 %shard_map.97 = (f32[1792,256]{1,0:T(8,128)S(1)}, f32[1792,128]{1,0:T(8,128)S(1)}, bf16[1792,256]{1,0:T(8,128)(2,1)S(1)}, bf16[1792,256]{1,0:T(8,128)(2,1)S(1)}) custom-call(bf16[1792,768]{1,0:T(8,128)(2,1)S(1)} %get-tuple-element.71.refs_0_, f32[1792,128]{1,0:T(8,128)S(1)} %get-tuple-element.72.refs_1_.refs_3_, f32[1792,256]{1,0:T(8,128)S(1)} %copy-done.1, ...), custom_call_target="tpu_custom_call" | custom-call | flops 2818572288 | bytes 11296768 | tf_op jit(solution)/shard_map/pallas_call | solution.py:55
  61.0 6.3 %collective-permute-done.10.refs_2_ = f32[392,256]{1,0:T(8,128)S(1)} collective-permute-done((f32[392,256]{1,0:T(8,128)S(1)}, f32[392,256]{1,0:T(8,128)S(1)}, u32[]{:S(2)}, u32[]{:S(2)}) %collective-permute-start.10) | collective-permute-done | bytes 401440 | tf_op jit(solution)/shard_map/ppermute | solution.py:555
  68.7 5.1 %shard_map.103.refs_0_.refs_3_ = f32[1792,256]{1,0:T(8,128)S(1)} custom-call(f32[1792,1792]{1,0:T(8,128)S(1)} %copy-done, bf16[1792,256]{1,0:T(8,128)(2,1)S(1)} %get-tuple-element.91.refs_1_, bf16[1792,256]{1,0:T(8,128)(2,1)S(1)} %get-tuple-element.92.refs_2_), custom_call_target="tpu_custom_call" | custom-call | flops 4932501504 | bytes 16515072 | tf_op jit(solution)/shard_map/pallas_call | solution.py:55
  81.9 6.4 %shard_map.107.refs_4_.refs_1_ = f32[1792,256]{1,0:T(8,128)S(1)} custom-call(f32[1792,1792]{1,0:T(8,128)S(1)} %copy-done, bf16[1792,256]{1,0:T(8,128)(2,1)S(1)} %get-tuple-element.77.refs_7_.refs_1_.refs_2_, bf16[1792,256]{1,0:T(8,128)(2,1)S(1)} %get-tuple-element.78.refs_8_.refs_2_.refs_3_), custom_call_target="tpu_custom_call" | custom-call | flops 4932501504 | bytes 16515072 | tf_op jit(solution)/shard_map/pallas_call | solution.py:55
  88.2 4.3 %shard_map.108 = (f32[768,128]{1,0:T(8,128)S(1)}, f32[768,256]{1,0:T(8,128)S(1)}) custom-call(s32[1]{0:T(128)} %bitcast.refs_0_, s32[1,384]{1,0:T(1,128)S(1)} %copy-done.3, s32[1,384]{1,0:T(1,128)S(1)} %copy-done.4, f32[1792,128]{1,0:T(8,128)S(1)} %shard_map.99.refs_5_.refs_3_.refs_0_, f32[1792,256]{1,0:T(8,128)S(1)} %shard_map.107.refs_4_.refs_1_), custom_call_target="tpu_custom_call" | custom-call | flops 2000000000 | bytes 3932160 | tf_op jit(solution)/shard_map/pallas_call | solution.py:55
  94.8 3.9 %collective-permute-done.13.refs_3_ = f32[384,256]{1,0:T(8,128)S(1)} collective-permute-done((f32[384,256]{1,0:T(8,128)S(1)}, f32[384,256]{1,0:T(8,128)S(1)}, u32[]{:S(2)}, u32[]{:S(2)}) %collective-permute-start.13) | collective-permute-done | bytes 393248 | tf_op jit(solution)/shard_map/ppermute | solution.py:555
  99.2 3.2 %collective-permute-start.17 = (f32[136,256]{1,0:T(8,128)S(1)}, f32[136,256]{1,0:T(8,128)S(1)}, u32[]{:S(2)}, u32[]{:S(2)}) collective-permute-start(f32[136,256]{1,0:T(8,128)S(1)} %get-tuple-element.98.refs_5_), channel_id=1, source_target_pairs={{0,6},{1,7},{2,4},{3,5},{4,2},{5,3},{6,0},{7,1},{8,14},{9,15},{10,... | collective-permute-start | bytes 417800 | tf_op jit(solution)/shard_map/ppermute | solution.py:588
  105.3 5.1 %shard_map.111.refs_9_.refs_3_.refs_2_ = f32[1792,256]{1,0:T(8,128)S(1)} custom-call(f32[1792,1792]{1,0:T(8,128)S(1)} %copy-done, bf16[1792,256]{1,0:T(8,128)(2,1)S(1)} %get-tuple-element.101.refs_1_, bf16[1792,256]{1,0:T(8,128)(2,1)S(1)} %get-tuple-element.102.refs_2_), custom_call_target="tpu_custom_call" | custom-call | flops 4932501504 | bytes 16515072 | tf_op jit(solution)/shard_map/pallas_call | solution.py:55
  110.4 3.4 %collective-permute-done.16.refs_7_ = f32[136,256]{1,0:T(8,128)S(1)} collective-permute-done((f32[136,256]{1,0:T(8,128)S(1)}, f32[136,256]{1,0:T(8,128)S(1)}, u32[]{:S(2)}, u32[]{:S(2)}) %collective-permute-start.16) | collective-permute-done | bytes 139296 | tf_op jit(solution)/shard_map/ppermute | solution.py:588
  118.0 3.8 %shard_map.113.refs_5_ = f32[768,256]{1,0:T(8,128)S(1)} custom-call(s32[1]{0:T(128)} %bitcast.refs_0_, s32[1,384]{1,0:T(1,128)S(1)} %copy-done.3, s32[1,384]{1,0:T(1,128)S(1)} %copy-done.4, f32[1792,256]{1,0:T(8,128)S(1)} %shard_map.111.refs_9_.refs_3_.refs_2_), custom_call_target="tpu_custom_call" | custom-call | flops 2000000000 | bytes 2621440 | tf_op jit(solution)/shard_map/pallas_call | solution.py:55
  121.9 4.8 %collective-permute-done.18.refs_7_ = f32[392,256]{1,0:T(8,128)S(1)} collective-permute-done((f32[392,256]{1,0:T(8,128)S(1)}, f32[392,256]{1,0:T(8,128)S(1)}, u32[]{:S(2)}, u32[]{:S(2)}) %collective-permute-start.18) | collective-permute-done | bytes 401440 | tf_op jit(solution)/shard_map/ppermute | solution.py:555
  129.5 4.3 %collective-permute-start.19 = (f32[8,256]{1,0:T(8,128)S(1)}, f32[8,256]{1,0:T(8,128)S(1)}, u32[]{:S(2)}, u32[]{:S(2)}) collective-permute-start(f32[8,256]{1,0:T(8,128)S(1)} %slice_add_fusion.1), channel_id=1, source_target_pairs={{0,8},{8,0},{16,24},{24,16},{1,9},{9,1},{17,25},{25,17},{2,10},{10... | collective-permute-start | bytes 24584 | tf_op jit(solution)/shard_map/ppermute | solution.py:598
  135.3 3.0 %collective-permute-done.20 = f32[8,256]{1,0:T(8,128)S(1)} collective-permute-done((f32[8,256]{1,0:T(8,128)S(1)}, f32[8,256]{1,0:T(8,128)S(1)}, u32[]{:S(2)}, u32[]{:S(2)}) %collective-permute-start.20) | collective-permute-done | bytes 8224 | tf_op jit(solution)/shard_map/ppermute | solution.py:598
  138.3 4.5 %shard_map.115 = (f32[1792,256]{1,0:T(8,128)S(1)}, f32[1792,256]{1,0:T(8,128)S(1)}, f32[136,256]{1,0:T(8,128)S(1)}) custom-call(f32[1792,128]{1,0:T(8,128)S(1)} %shard_map.99.refs_5_.refs_3_.refs_0_, f32[1792,256]{1,0:T(8,128)S(1)} %shard_map.107.refs_4_.refs_1_, f32[1792,256]{1,0:T(8,128)S(1)} %shard_map.111.refs_9_.refs_3_.refs_2_, ...), custom_call_target="tpu_custom_call" | custom-call | flops 1409286144 | bytes 16138240 | tf_op jit(solution)/shard_map/pallas_call | solution.py:55
  142.9 4.5 %collective-permute-done.23.refs_3_ = f32[384,256]{1,0:T(8,128)S(1)} collective-permute-done((f32[384,256]{1,0:T(8,128)S(1)}, f32[384,256]{1,0:T(8,128)S(1)}, u32[]{:S(2)}, u32[]{:S(2)}) %collective-permute-start.23) | collective-permute-done | bytes 393248 | tf_op jit(solution)/shard_map/ppermute | solution.py:555
  149.7 2.7 %collective-permute-start.25 = (f32[136,256]{1,0:T(8,128)S(1)}, f32[136,256]{1,0:T(8,128)S(1)}, u32[]{:S(2)}, u32[]{:S(2)}) collective-permute-start(f32[136,256]{1,0:T(8,128)S(1)} %get-tuple-element.113.refs_5_), channel_id=1, source_target_pairs={{0,2},{1,3},{2,0},{3,1},{4,6},{5,7},{6,4},{7,5},{8,10},{9,11},{10,... | collective-permute-start | bytes 417800 | tf_op jit(solution)/shard_map/ppermute | solution.py:588
  154.0 5.1 %shard_map.118.refs_9_.refs_3_.refs_2_ = f32[1792,256]{1,0:T(8,128)S(1)} custom-call(f32[1792,1792]{1,0:T(8,128)S(1)} %copy-done, bf16[1792,256]{1,0:T(8,128)(2,1)S(1)} %get-tuple-element.116.refs_1_, bf16[1792,256]{1,0:T(8,128)(2,1)S(1)} %get-tuple-element.117.refs_2_), custom_call_target="tpu_custom_call" | custom-call | flops 4932501504 | bytes 16515072 | tf_op jit(solution)/shard_map/pallas_call | solution.py:55
  164.1 3.8 %shard_map.120.refs_5_ = f32[768,256]{1,0:T(8,128)S(1)} custom-call(s32[1]{0:T(128)} %bitcast.refs_0_, s32[1,384]{1,0:T(1,128)S(1)} %copy-done.3, s32[1,384]{1,0:T(1,128)S(1)} %copy-done.4, f32[1792,256]{1,0:T(8,128)S(1)} %shard_map.118.refs_9_.refs_3_.refs_2_), custom_call_target="tpu_custom_call" | custom-call | flops 2000000000 | bytes 2621440 | tf_op jit(solution)/shard_map/pallas_call | solution.py:55
  167.9 5.4 %collective-permute-done.28.refs_7_ = f32[392,256]{1,0:T(8,128)S(1)} collective-permute-done((f32[392,256]{1,0:T(8,128)S(1)}, f32[392,256]{1,0:T(8,128)S(1)}, u32[]{:S(2)}, u32[]{:S(2)}) %collective-permute-start.28) | collective-permute-done | bytes 401440 | tf_op jit(solution)/shard_map/ppermute | solution.py:555
  183.0 2.8 %shard_map.122 = (f32[1792,256]{1,0:T(8,128)S(1)}, f32[1792,256]{1,0:T(8,128)S(1)}, f32[136,256]{1,0:T(8,128)S(1)}) custom-call(f32[1792,128]{1,0:T(8,128)S(1)} %shard_map.99.refs_5_.refs_3_.refs_0_, f32[1792,256]{1,0:T(8,128)S(1)} %shard_map.107.refs_4_.refs_1_, f32[1792,256]{1,0:T(8,128)S(1)} %shard_map.118.refs_9_.refs_3_.refs_2_, ...), custom_call_target="tpu_custom_call" | custom-call | flops 1409286144 | bytes 16138240 | tf_op jit(solution)/shard_map/pallas_call | solution.py:55
  185.7 8.5 %collective-permute-done.33.refs_3_ = f32[384,256]{1,0:T(8,128)S(1)} collective-permute-done((f32[384,256]{1,0:T(8,128)S(1)}, f32[384,256]{1,0:T(8,128)S(1)}, u32[]{:S(2)}, u32[]{:S(2)}) %collective-permute-start.33) | collective-permute-done | bytes 393248 | tf_op jit(solution)/shard_map/ppermute | solution.py:555
  197.5 2.7 %collective-permute-start.36 = (f32[8,256]{1,0:T(8,128)S(1)}, f32[8,256]{1,0:T(8,128)S(1)}, u32[]{:S(2)}, u32[]{:S(2)}) collective-permute-start(f32[8,256]{1,0:T(8,128)S(1)} %slice_add_fusion.5), channel_id=1, source_target_pairs={{0,16},{1,17},{2,18},{3,19},{4,20},{5,21},{6,22},{7,23},{8,24},{9,... | collective-permute-start | bytes 24584 | tf_op jit(solution)/shard_map/ppermute | solution.py:611
  201.8 3.8 %shard_map.123 = (f32[1792,256]{1,0:T(8,128)S(1)}, f32[1792,256]{1,0:T(8,128)S(1)}) custom-call(bf16[1792,128]{1,0:T(8,128)(2,1)S(1)} %get-tuple-element.69.refs_1_.refs_5_.refs_0_, bf16[1792,128]{1,0:T(8,128)(2,1)S(1)} %get-tuple-element.70.refs_2_.refs_6_.refs_1_, bf16[1792,256]{1,0:T(8,128)(2,1)S(1)} %get-tuple-element.77.refs_7_.refs_1_.refs_2_, ...), custom_call_target="tpu_custom_call" | custom-call | flops 2113929216 | bytes 14041088 | tf_op jit(solution)/shard_map/pallas_call | solution.py:55
  (108 shorter events, 63.6 us)
Async XLA Ops:
  6.0 22.1 %collective-permute-start = (f32[384,256]{1,0:T(8,128)S(1)}, f32[384,256]{1,0:T(8,128)S(1)}, u32[]{:S(2)}, u32[]{:S(2)}) collective-permute-start(f32[384,256]{1,0:T(8,128)S(1)} %get-tuple-element.73), channel_id=1, source_target_pairs={{0,1},{1,0},{2,3},{3,2},{4,5},{5,4},{6,7},{7,6},{8,9},{9,8},{10,11... | collective-permute-start | bytes 1179656 | tf_op jit(solution)/shard_map/ppermute | solution.py:555
  9.0 19.1 %collective-permute-start.1 = (f32[384,256]{1,0:T(8,128)S(1)}, f32[384,256]{1,0:T(8,128)S(1)}, u32[]{:S(2)}, u32[]{:S(2)}) collective-permute-start(f32[384,256]{1,0:T(8,128)S(1)} %get-tuple-element.74), channel_id=1, source_target_pairs={{1,2},{3,4},{5,6},{7,8},{9,10},{11,12},{13,14},{15,16},{17,18},{19... | collective-permute-start | bytes 1179656 | tf_op jit(solution)/shard_map/ppermute | solution.py:561
  17.5 16.3 %collective-permute-start.6 = (f32[128,512]{1,0:T(8,128)S(1)}, f32[128,512]{1,0:T(8,128)S(1)}, u32[]{:S(2)}, u32[]{:S(2)}) collective-permute-start(f32[128,512]{1,0:T(8,128)S(1)} %get-tuple-element.81.refs_1_), channel_id=1, source_target_pairs={{0,6},{1,3},{2,0},{3,5},{4,2},{5,7},{6,4},{7,1},{8,14},{9,11},{10,... | collective-permute-start | bytes 786440 | tf_op jit(solution)/shard_map/ppermute | solution.py:567
  28.4 20.9 %collective-permute-start.5 = (f32[128,512]{1,0:T(8,128)S(1)}, f32[128,512]{1,0:T(8,128)S(1)}, u32[]{:S(2)}, u32[]{:S(2)}) collective-permute-start(f32[128,512]{1,0:T(8,128)S(1)} %get-tuple-element.85), channel_id=1, source_target_pairs={{1,2},{3,4},{5,6},{7,0},{2,1},{4,3},{6,5},{0,7},{9,10},{11,12},{13... | collective-permute-start | bytes 786440 | tf_op jit(solution)/shard_map/ppermute | solution.py:574
  30.7 18.6 %collective-permute-start.4 = (f32[128,512]{1,0:T(8,128)S(1)}, f32[128,512]{1,0:T(8,128)S(1)}, u32[]{:S(2)}, u32[]{:S(2)}) collective-permute-start(f32[128,512]{1,0:T(8,128)S(1)} %get-tuple-element.85), channel_id=1, source_target_pairs={{0,1},{1,0},{2,3},{3,2},{4,5},{5,4},{6,7},{7,6},{8,9},{9,8},{10,11... | collective-permute-start | bytes 786440 | tf_op jit(solution)/shard_map/ppermute | solution.py:555
  30.7 11.7 %collective-permute-start.9 = (f32[136,256]{1,0:T(8,128)S(1)}, f32[136,256]{1,0:T(8,128)S(1)}, u32[]{:S(2)}, u32[]{:S(2)}) collective-permute-start(f32[136,256]{1,0:T(8,128)S(1)} %shard_map.100.refs_5_), channel_id=1, source_target_pairs={{0,6},{1,7},{2,4},{3,5},{4,2},{5,3},{6,0},{7,1},{8,14},{9,15},{10,... | collective-permute-start | bytes 417800 | tf_op jit(solution)/shard_map/ppermute | solution.py:588
  33.8 14.9 %collective-permute-start.8 = (f32[136,256]{1,0:T(8,128)S(1)}, f32[136,256]{1,0:T(8,128)S(1)}, u32[]{:S(2)}, u32[]{:S(2)}) collective-permute-start(f32[136,256]{1,0:T(8,128)S(1)} %shard_map.100.refs_5_), channel_id=1, source_target_pairs={{0,4},{1,5},{2,6},{3,7},{4,0},{5,1},{6,2},{7,3},{8,12},{9,13},{10,... | collective-permute-start | bytes 417800 | tf_op jit(solution)/shard_map/ppermute | solution.py:588
  33.8 15.6 %collective-permute-start.7 = (f32[136,256]{1,0:T(8,128)S(1)}, f32[136,256]{1,0:T(8,128)S(1)}, u32[]{:S(2)}, u32[]{:S(2)}) collective-permute-start(f32[136,256]{1,0:T(8,128)S(1)} %shard_map.100.refs_5_), channel_id=1, source_target_pairs={{0,2},{1,3},{2,0},{3,1},{4,6},{5,7},{6,4},{7,5},{8,10},{9,11},{10,... | collective-permute-start | bytes 417800 | tf_op jit(solution)/shard_map/ppermute | solution.py:588
  42.4 13.9 %collective-permute-start.2 = (f32[408,128]{1,0:T(8,128)S(1)}, f32[408,128]{1,0:T(8,128)S(1)}, u32[]{:S(2)}, u32[]{:S(2)}) collective-permute-start(f32[408,128]{1,0:T(8,128)S(1)} %get-tuple-element.75), channel_id=1, source_target_pairs={{0,1},{1,0},{2,3},{3,2},{4,5},{5,4},{6,7},{7,6},{8,9},{9,8},{10,11... | collective-permute-start | bytes 626696 | tf_op jit(solution)/shard_map/ppermute | solution.py:555
  48.6 7.7 %collective-permute-start.3 = (f32[408,128]{1,0:T(8,128)S(1)}, f32[408,128]{1,0:T(8,128)S(1)}, u32[]{:S(2)}, u32[]{:S(2)}) collective-permute-start(f32[408,128]{1,0:T(8,128)S(1)} %get-tuple-element.76), channel_id=1, source_target_pairs={{1,2},{3,4},{5,6},{7,8},{9,10},{11,12},{13,14},{15,16},{17,18},{19... | collective-permute-start | bytes 626696 | tf_op jit(solution)/shard_map/ppermute | solution.py:561
  50.0 17.3 %collective-permute-start.10 = (f32[392,256]{1,0:T(8,128)S(1)}, f32[392,256]{1,0:T(8,128)S(1)}, u32[]{:S(2)}, u32[]{:S(2)}) collective-permute-start(f32[392,256]{1,0:T(8,128)S(1)} %get-tuple-element.87), channel_id=1, source_target_pairs={{0,1},{1,0},{2,3},{3,2},{4,5},{5,4},{6,7},{7,6},{8,9},{9,8},{10,11... | collective-permute-start | bytes 1204232 | tf_op jit(solution)/shard_map/ppermute | solution.py:555
  54.0 7.0 %collective-permute-start.11 = (f32[128,256]{1,0:T(8,128)S(1)}, f32[128,256]{1,0:T(8,128)S(1)}, u32[]{:S(2)}, u32[]{:S(2)}) collective-permute-start(f32[128,256]{1,0:T(8,128)S(1)} %get-tuple-element.88), channel_id=1, source_target_pairs={{0,8},{8,16},{16,24},{15,7},{23,15},{31,23}} | collective-permute-start | bytes 393224 | tf_op jit(solution)/shard_map/ppermute | solution.py:628
  55.5 5.5 %collective-permute-start.12 = (f32[128,256]{1,0:T(8,128)S(1)}, f32[128,256]{1,0:T(8,128)S(1)}, u32[]{:S(2)}, u32[]{:S(2)}) collective-permute-start(f32[128,256]{1,0:T(8,128)S(1)} %get-tuple-element.89), channel_id=1, source_target_pairs={{1,8},{9,16},{17,24},{14,7},{22,15},{30,23}} | collective-permute-start | bytes 393224 | tf_op jit(solution)/shard_map/ppermute | solution.py:628
  78.8 20.0 %collective-permute-start.13 = (f32[384,256]{1,0:T(8,128)S(1)}, f32[384,256]{1,0:T(8,128)S(1)}, u32[]{:S(2)}, u32[]{:S(2)}) collective-permute-start(f32[384,256]{1,0:T(8,128)S(1)} %shard_map.105.refs_5_), channel_id=1, source_target_pairs={{0,1},{1,0},{2,3},{3,2},{4,5},{5,4},{6,7},{7,6},{8,9},{9,8},{10,11... | collective-permute-start | bytes 1179656 | tf_op jit(solution)/shard_map/ppermute | solution.py:555
  81.2 17.5 %collective-permute-start.14 = (f32[384,256]{1,0:T(8,128)S(1)}, f32[384,256]{1,0:T(8,128)S(1)}, u32[]{:S(2)}, u32[]{:S(2)}) collective-permute-start(f32[384,256]{1,0:T(8,128)S(1)} %shard_map.106.refs_6_), channel_id=1, source_target_pairs={{1,2},{3,4},{5,6},{7,8},{9,10},{11,12},{13,14},{15,16},{17,18},{19... | collective-permute-start | bytes 1179656 | tf_op jit(solution)/shard_map/ppermute | solution.py:561
  99.2 11.2 %collective-permute-start.17 = (f32[136,256]{1,0:T(8,128)S(1)}, f32[136,256]{1,0:T(8,128)S(1)}, u32[]{:S(2)}, u32[]{:S(2)}) collective-permute-start(f32[136,256]{1,0:T(8,128)S(1)} %get-tuple-element.98.refs_5_), channel_id=1, source_target_pairs={{0,6},{1,7},{2,4},{3,5},{4,2},{5,3},{6,0},{7,1},{8,14},{9,15},{10,... | collective-permute-start | bytes 417800 | tf_op jit(solution)/shard_map/ppermute | solution.py:588
  102.4 11.4 %collective-permute-start.16 = (f32[136,256]{1,0:T(8,128)S(1)}, f32[136,256]{1,0:T(8,128)S(1)}, u32[]{:S(2)}, u32[]{:S(2)}) collective-permute-start(f32[136,256]{1,0:T(8,128)S(1)} %get-tuple-element.98.refs_5_), channel_id=1, source_target_pairs={{0,4},{1,5},{2,6},{3,7},{4,0},{5,1},{6,2},{7,3},{8,12},{9,13},{10,... | collective-permute-start | bytes 417800 | tf_op jit(solution)/shard_map/ppermute | solution.py:588
  102.4 11.4 %collective-permute-start.15 = (f32[136,256]{1,0:T(8,128)S(1)}, f32[136,256]{1,0:T(8,128)S(1)}, u32[]{:S(2)}, u32[]{:S(2)}) collective-permute-start(f32[136,256]{1,0:T(8,128)S(1)} %get-tuple-element.98.refs_5_), channel_id=1, source_target_pairs={{0,2},{1,3},{2,0},{3,1},{4,6},{5,7},{6,4},{7,5},{8,10},{9,11},{10,... | collective-permute-start | bytes 417800 | tf_op jit(solution)/shard_map/ppermute | solution.py:588
  114.4 12.2 %collective-permute-start.18 = (f32[392,256]{1,0:T(8,128)S(1)}, f32[392,256]{1,0:T(8,128)S(1)}, u32[]{:S(2)}, u32[]{:S(2)}) collective-permute-start(f32[392,256]{1,0:T(8,128)S(1)} %get-tuple-element.104), channel_id=1, source_target_pairs={{0,1},{1,0},{2,3},{3,2},{4,5},{5,4},{6,7},{7,6},{8,9},{9,8},{10,11... | collective-permute-start | bytes 1204232 | tf_op jit(solution)/shard_map/ppermute | solution.py:555
  115.6 6.3 %collective-permute-start.21 = (f32[128,256]{1,0:T(8,128)S(1)}, f32[128,256]{1,0:T(8,128)S(1)}, u32[]{:S(2)}, u32[]{:S(2)}) collective-permute-start(f32[128,256]{1,0:T(8,128)S(1)} %get-tuple-element.105), channel_id=1, source_target_pairs={{0,8},{8,16},{16,24},{15,7},{23,15},{31,23}} | collective-permute-start | bytes 393224 | tf_op jit(solution)/shard_map/ppermute | solution.py:628
  127.4 20.1 %collective-permute-start.23 = (f32[384,256]{1,0:T(8,128)S(1)}, f32[384,256]{1,0:T(8,128)S(1)}, u32[]{:S(2)}, u32[]{:S(2)}) collective-permute-start(f32[384,256]{1,0:T(8,128)S(1)} %get-tuple-element.110.refs_5_), channel_id=1, source_target_pairs={{0,1},{1,0},{2,3},{3,2},{4,5},{5,4},{6,7},{7,6},{8,9},{9,8},{10,11... | collective-permute-start | bytes 1179656 | tf_op jit(solution)/shard_map/ppermute | solution.py:555
  128.6 18.9 %collective-permute-start.24 = (f32[384,256]{1,0:T(8,128)S(1)}, f32[384,256]{1,0:T(8,128)S(1)}, u32[]{:S(2)}, u32[]{:S(2)}) collective-permute-start(f32[384,256]{1,0:T(8,128)S(1)} %get-tuple-element.111.refs_6_), channel_id=1, source_target_pairs={{1,2},{3,4},{5,6},{7,8},{9,10},{11,12},{13,14},{15,16},{17,18},{19... | collective-permute-start | bytes 1179656 | tf_op jit(solution)/shard_map/ppermute | solution.py:561
  129.5 5.1 %collective-permute-start.19 = (f32[8,256]{1,0:T(8,128)S(1)}, f32[8,256]{1,0:T(8,128)S(1)}, u32[]{:S(2)}, u32[]{:S(2)}) collective-permute-start(f32[8,256]{1,0:T(8,128)S(1)} %slice_add_fusion.1), channel_id=1, source_target_pairs={{0,8},{8,0},{16,24},{24,16},{1,9},{9,1},{17,25},{25,17},{2,10},{10... | collective-permute-start | bytes 24584 | tf_op jit(solution)/shard_map/ppermute | solution.py:598
  147.9 11.2 %collective-permute-start.27 = (f32[136,256]{1,0:T(8,128)S(1)}, f32[136,256]{1,0:T(8,128)S(1)}, u32[]{:S(2)}, u32[]{:S(2)}) collective-permute-start(f32[136,256]{1,0:T(8,128)S(1)} %get-tuple-element.113.refs_5_), channel_id=1, source_target_pairs={{0,6},{1,7},{2,4},{3,5},{4,2},{5,3},{6,0},{7,1},{8,14},{9,15},{10,... | collective-permute-start | bytes 417800 | tf_op jit(solution)/shard_map/ppermute | solution.py:588
  149.7 11.2 %collective-permute-start.26 = (f32[136,256]{1,0:T(8,128)S(1)}, f32[136,256]{1,0:T(8,128)S(1)}, u32[]{:S(2)}, u32[]{:S(2)}) collective-permute-start(f32[136,256]{1,0:T(8,128)S(1)} %get-tuple-element.113.refs_5_), channel_id=1, source_target_pairs={{0,4},{1,5},{2,6},{3,7},{4,0},{5,1},{6,2},{7,3},{8,12},{9,13},{10,... | collective-permute-start | bytes 417800 | tf_op jit(solution)/shard_map/ppermute | solution.py:588
  149.7 11.2 %collective-permute-start.25 = (f32[136,256]{1,0:T(8,128)S(1)}, f32[136,256]{1,0:T(8,128)S(1)}, u32[]{:S(2)}, u32[]{:S(2)}) collective-permute-start(f32[136,256]{1,0:T(8,128)S(1)} %get-tuple-element.113.refs_5_), channel_id=1, source_target_pairs={{0,2},{1,3},{2,0},{3,1},{4,6},{5,7},{6,4},{7,5},{8,10},{9,11},{10,... | collective-permute-start | bytes 417800 | tf_op jit(solution)/shard_map/ppermute | solution.py:588
  161.5 11.9 %collective-permute-start.28 = (f32[392,256]{1,0:T(8,128)S(1)}, f32[392,256]{1,0:T(8,128)S(1)}, u32[]{:S(2)}, u32[]{:S(2)}) collective-permute-start(f32[392,256]{1,0:T(8,128)S(1)} %get-tuple-element.119), channel_id=1, source_target_pairs={{0,1},{1,0},{2,3},{3,2},{4,5},{5,4},{6,7},{7,6},{8,9},{9,8},{10,11... | collective-permute-start | bytes 1204232 | tf_op jit(solution)/shard_map/ppermute | solution.py:555
  162.1 5.8 %collective-permute-start.31 = (f32[128,256]{1,0:T(8,128)S(1)}, f32[128,256]{1,0:T(8,128)S(1)}, u32[]{:S(2)}, u32[]{:S(2)}) collective-permute-start(f32[128,256]{1,0:T(8,128)S(1)} %get-tuple-element.121), channel_id=1, source_target_pairs={{0,8},{8,16},{16,24},{15,7},{23,15},{31,23}} | collective-permute-start | bytes 393224 | tf_op jit(solution)/shard_map/ppermute | solution.py:628
  174.1 20.2 %collective-permute-start.33 = (f32[384,256]{1,0:T(8,128)S(1)}, f32[384,256]{1,0:T(8,128)S(1)}, u32[]{:S(2)}, u32[]{:S(2)}) collective-permute-start(f32[384,256]{1,0:T(8,128)S(1)} %get-tuple-element.129.refs_5_), channel_id=1, source_target_pairs={{0,1},{1,0},{2,3},{3,2},{4,5},{5,4},{6,7},{7,6},{8,9},{9,8},{10,11... | collective-permute-start | bytes 1179656 | tf_op jit(solution)/shard_map/ppermute | solution.py:555
  175.1 19.2 %collective-permute-start.34 = (f32[384,256]{1,0:T(8,128)S(1)}, f32[384,256]{1,0:T(8,128)S(1)}, u32[]{:S(2)}, u32[]{:S(2)}) collective-permute-start(f32[384,256]{1,0:T(8,128)S(1)} %get-tuple-element.130.refs_6_), channel_id=1, source_target_pairs={{1,2},{3,4},{5,6},{7,8},{9,10},{11,12},{13,14},{15,16},{17,18},{19... | collective-permute-start | bytes 1179656 | tf_op jit(solution)/shard_map/ppermute | solution.py:561
  196.6 4.5 %collective-permute-start.38 = (f32[8,256]{1,0:T(8,128)S(1)}, f32[8,256]{1,0:T(8,128)S(1)}, u32[]{:S(2)}, u32[]{:S(2)}) collective-permute-start(f32[8,256]{1,0:T(8,128)S(1)} %slice_add_fusion.5), channel_id=1, source_target_pairs={{0,17},{1,16},{2,19},{3,18},{4,21},{5,20},{6,23},{7,22},{8,25},{9,... | collective-permute-start | bytes 24584 | tf_op jit(solution)/shard_map/ppermute | solution.py:611
  205.6 4.6 %collective-permute-start.40 = (f32[8,256]{1,0:T(8,128)S(1)}, f32[8,256]{1,0:T(8,128)S(1)}, u32[]{:S(2)}, u32[]{:S(2)}) collective-permute-start(f32[8,256]{1,0:T(8,128)S(1)} %add.60), channel_id=1, source_target_pairs={{0,4},{1,5},{2,6},{3,7},{4,0},{5,1},{6,2},{7,3},{8,12},{9,13},{10,... | collective-permute-start | bytes 24584 | tf_op jit(solution)/shard_map/ppermute | solution.py:618
  (14 other events, 100.6 us)
